TPU v7x, 256 devices: a whole 4x4x8 slice. The times are simulated.
256 devices in a mesh: rows: 32 (over z, y), cols: 8 (over x, core).
Axes of the slice: x: 4, y: 4, z: 8, core: 2. Of those that a mesh axis runs over, the one named last changes fastest.
Arguments:
- matrix: float32 [32768, 10, 1024], P('rows', None, 'cols'), may hold values from -6 to 6
Outputs:
- reduced: float32 [32768, 10, 1024], P('rows', None, 'cols')
- top_rows: float32 [256, 10, 1024], P(None, None, 'cols')
All inputs are finite; a program needn't handle non-finite values.
Results may differ from a plain program's by a relative error of at most 0.0001.
Values sent between devices are 32-bit elements; how exact they have to be, the bound alone decides.
No kernel may reach another device: no remote copies, remote signals or barrier semaphores. Data moves between devices by JAX's collectives and lax.ppermute only.
A program may use at most 64 MiB of HBM per device.

v0:
```python
import jax
import jax.numpy as jnp
from jax import lax
from jax.experimental import pallas as pl
from jax.experimental.pallas import tpu as pltpu
from jax.sharding import Mesh, PartitionSpec as P

PRECISE = lax.Precision.HIGHEST
NZ, NY, NX, NC = 8, 4, 4, 2
LANES, SUB = 128, 8
RIDE = 1280
NT = (((1,), (1,)), ((), ()))
VMEM = pl.BlockSpec(memory_space=pltpu.VMEM)
HBM = pl.BlockSpec(memory_space=pltpu.HBM)


def in_hbm(values):
    return pltpu.with_memory_space_constraint(values, pltpu.HBM)


def params(mib):
    return pltpu.CompilerParams(vmem_limit_bytes=mib << 20)


def dot(left, right, dims=(((1,), (0,)), ((), ()))):
    return lax.dot_general(left, right, dims, precision=PRECISE, preferred_element_type=jnp.float32)


def split(values):
    high = values.astype(jnp.bfloat16)
    return high, (values - high.astype(jnp.float32)).astype(jnp.bfloat16)


def wide_left(values):
    high, low = split(values)
    return jnp.concatenate([high, high, low], axis=1)


def wide_right(values):
    high, low = split(values)
    return jnp.concatenate([high, low, high], axis=0)


def narrow_dot(left, right):
    return lax.dot_general(left, right, (((1,), (0,)), ((), ())), preferred_element_type=jnp.float32)


def pick(index, choices):
    value = choices[-1]
    for at in range(len(choices) - 2, -1, -1):
        value = jnp.where(index == at, choices[at], value)
    return value


def swap(values):
    return lax.ppermute(values, "c", [(0, 1), (1, 0)])


def relay(own):
    x = lax.axis_index("x")
    half = own.shape[0] // 2
    low, high = own[:half], own[half:]
    up_low = lax.ppermute(low, "x", [(0, 1)])
    down_high = lax.ppermute(high, "x", [(0, 3)])
    up_high = lax.ppermute(high, "x", [(0, 1)])
    down_low = lax.ppermute(low, "x", [(0, 3)])
    on_low = lax.ppermute(up_low, "x", [(1, 2)])
    on_high = lax.ppermute(down_high, "x", [(3, 2)])
    mine_low = pick(x, [low, up_low, on_low, down_low])
    mine_high = pick(x, [high, up_high, on_high, down_high])
    return mine_low, mine_high, swap(mine_low), swap(mine_high)


def index_of(axis):
    return lax.axis_index(axis).astype(jnp.int32)[None]


SCALAR = pl.BlockSpec(memory_space=pltpu.SMEM)


def place(core, pieces, p_ref):
    half, k = pieces[0].shape
    first = core == 0
    for at in range(2):
        rows = slice(at * half, (at + 1) * half)
        mine, other = pieces[at][...], pieces[2 + at][...]
        p_ref[rows, :k] = jnp.where(first, mine, other)
        p_ref[rows, k:] = jnp.where(first, other, mine)


def around(at_ref, by, size, rows, base=0):
    return pl.ds(pl.multiple_of(base + ((at_ref[0] + by) % size) * rows, SUB), rows)


def fetch(source, target, sem):
    copies = [pltpu.make_async_copy(source.at[r], target.at[r], sem.at[r]) for r in range(source.shape[0])]
    for copy in copies:
        copy.start()
    return copies


def products_kernel(
    x_ref, y_ref, core_ref, ml_ref, mh_ref, ol_ref, oh_ref, c_hbm, o0_ref, o1_ref, o2_ref, o3_ref, p_hbm, c_ref, p_ref, t_ref, sem, p_sem
):
    rounds, n, k = c_ref.shape
    w = 2 * k
    arriving = fetch(c_hbm, c_ref, sem)
    place(core_ref[0], (ml_ref, mh_ref, ol_ref, oh_ref), p_ref)
    leaving = pltpu.make_async_copy(p_ref, p_hbm, p_sem)
    leaving.start()
    t_ref[...] = p_ref[...].T
    outs = (o0_ref, o1_ref, o2_ref, o3_ref)
    part = w // NY
    left = wide_left(jnp.concatenate([t_ref[around(y_ref, by, NY, part), :] for by in range(NY)], axis=0))
    base = (x_ref[0] * NC + core_ref[0]) * (NY * SUB)
    rows = [t_ref[around(y_ref, by, NY, SUB, base), :] for by in range(NY)]
    gram = dot(jnp.concatenate(rows, axis=0), p_ref[...])
    for by, o_ref in enumerate(outs):
        piece = gram[by * SUB : (by + 1) * SUB]
        o_ref[:, RIDE:] = jnp.zeros((part, LANES), jnp.float32)
        o_ref[:SUB, RIDE:] = piece[:, :LANES]
        o_ref[SUB : 2 * SUB, RIDE:] = piece[:, LANES:]
    group = rounds // 2
    for r in range(0, rounds, group):
        for copy in arriving[r : r + group]:
            copy.wait()
        some = jnp.concatenate([c_ref[at] for at in range(r, r + group)], axis=1)
        cross = narrow_dot(left, wide_right(some))
        for by, o_ref in enumerate(outs):
            o_ref[:, r * k : (r + group) * k] = cross[by * part : (by + 1) * part]
    leaving.wait()


def products(pieces, columns):
    rounds, n, k = columns.shape
    w = 2 * k
    return pl.pallas_call(
        products_kernel,
        in_specs=[SCALAR] * 3 + [VMEM] * 4 + [HBM],
        out_specs=[VMEM] * NY + [HBM],
        out_shape=[jax.ShapeDtypeStruct((w // NY, RIDE + LANES), jnp.float32)] * NY
        + [jax.ShapeDtypeStruct((n, w), jnp.float32)],
        scratch_shapes=[
            pltpu.VMEM(columns.shape, jnp.float32),
            pltpu.VMEM((n, w), jnp.float32),
            pltpu.VMEM((w, n), jnp.float32),
            pltpu.SemaphoreType.DMA((rounds,)),
            pltpu.SemaphoreType.DMA(()),
        ],
        compiler_params=params(20),
        name="products",
    )(index_of("x"), index_of("y"), index_of("c"), *pieces, columns)


def sum_y_kernel(a0_ref, a1_ref, a2_ref, a3_ref, o_ref):
    total = (a0_ref[...] + a1_ref[...]) + (a2_ref[...] + a3_ref[...])
    for z in range(NZ):
        o_ref[z, :, :RIDE] = total[z * SUB : (z + 1) * SUB, :RIDE]
        o_ref[z, :, RIDE : RIDE + LANES] = total[:SUB, RIDE:]
        o_ref[z, :, RIDE + LANES :] = total[SUB : 2 * SUB, RIDE:]


def sum_y(pieces):
    return pl.pallas_call(
        sum_y_kernel,
        in_specs=[VMEM] * NY,
        out_specs=VMEM,
        out_shape=jax.ShapeDtypeStruct((NZ, SUB, RIDE + 2 * LANES), jnp.float32),
        compiler_params=params(4),
        name="sum_y",
    )(*pieces)


def sum_z_kernel(a_ref, o_ref, g_ref):
    total = a_ref[0]
    for z in range(1, NZ):
        total = total + a_ref[z]
    for z in range(NZ):
        o_ref[z] = total[:, :RIDE]
    g_ref[...] = total[:, RIDE:]


def sum_z(pieces):
    return pl.pallas_call(
        sum_z_kernel,
        in_specs=[VMEM],
        out_specs=[VMEM] * 2,
        out_shape=[
            jax.ShapeDtypeStruct((NZ, SUB, RIDE), jnp.float32),
            jax.ShapeDtypeStruct((SUB, 2 * LANES), jnp.float32),
        ],
        compiler_params=params(4),
        name="sum_z",
    )(pieces)


def deal(pieces, axis):
    size = len(pieces)
    return [pieces[0]] + [
        lax.ppermute(pieces[by], axis, [(at, (at + by) % size) for at in range(size)]) for by in range(1, size)
    ]


def every(values, axis, size):
    return [values] + [
        lax.ppermute(values, axis, [(at, (at - by) % size) for at in range(size)]) for by in range(1, size)
    ]


def collect(values, axis, size):
    return jnp.concatenate(every(values, axis, size), axis=0)


def inverse_root(d):
    y = lax.rsqrt(d)
    return y * (1.5 - 0.5 * d * y * y)


def invert_factor(block, w_ref, row0, col0):
    n = LANES
    tiles = n // SUB
    a = [block[SUB * t:SUB * (t + 1)] for t in range(tiles)]
    lane = lax.broadcasted_iota(jnp.int32, (SUB, LANES), 1)
    sub = lax.broadcasted_iota(jnp.int32, (SUB, LANES), 0)
    b = [jnp.where(lane == sub + SUB * t, 1.0, 0.0).astype(jnp.float32) for t in range(tiles)]

    def across(v, j):
        return jnp.broadcast_to(v[:, j:j + 1], (SUB, LANES))

    def down(v, s):
        return jnp.broadcast_to(v[s:s + 1, :], (SUB, LANES))

    for q in range(n // 4):
        t, s, j = q // 2, (q % 2) * 4, 4 * q
        ra = [down(a[t], s + k) for k in range(4)]
        rb = [down(b[t], s + k) for k in range(4)]
        d = {}
        for x in range(4):
            for y in range(x + 1):
                d[x, y] = across(ra[y], j + x)
                d[y, x] = d[x, y]
        det = 1.0 / (d[0, 0] * d[1, 1] - d[1, 0] * d[1, 0])
        p00, p01, p11 = d[1, 1] * det, -d[1, 0] * det, d[0, 0] * det
        z = [[d[r, 0] * p00 + d[r, 1] * p01, d[r, 0] * p01 + d[r, 1] * p11] for r in (2, 3)]
        s00 = d[2, 2] - (z[0][0] * d[2, 0] + z[0][1] * d[2, 1])
        s01 = d[3, 2] - (z[1][0] * d[2, 0] + z[1][1] * d[2, 1])
        s11 = d[3, 3] - (z[1][0] * d[3, 0] + z[1][1] * d[3, 1])
        sdet = 1.0 / (s00 * s11 - s01 * s01)
        i00, i01, i11 = s11 * sdet, -s01 * sdet, s00 * sdet

        def solve(r):
            u0 = p00 * r[0] + p01 * r[1]
            u1 = p01 * r[0] + p11 * r[1]
            v2 = r[2] - (z[0][0] * r[0] + z[0][1] * r[1])
            v3 = r[3] - (z[1][0] * r[0] + z[1][1] * r[1])
            y2 = i00 * v2 + i01 * v3
            y3 = i01 * v2 + i11 * v3
            return [u0 - (z[0][0] * y2 + z[1][0] * y3), u1 - (z[0][1] * y2 + z[1][1] * y3), y2, y3]

        ya, yb = solve(ra), solve(rb)
        for u in range(t, tiles):
            if u == t and s == 4:
                continue
            c = [across(a[u], j + k) for k in range(4)]
            na, nb = a[u], b[u]
            fa = (c[0] * ya[0] + c[1] * ya[1]) + (c[2] * ya[2] + c[3] * ya[3])
            fb = (c[0] * yb[0] + c[1] * yb[1]) + (c[2] * yb[2] + c[3] * yb[3])
            if u == t:
                a[u] = jnp.where(sub >= 4, na - fa, na)
                b[u] = jnp.where(sub >= 4, nb - fb, nb)
            else:
                a[u], b[u] = na - fa, nb - fb
        k0 = inverse_root(d[0, 0])
        l10 = d[1, 0] * k0
        k1 = inverse_root(d[1, 1] - l10 * l10)
        w0 = k0 * rb[0]
        w1 = k1 * (rb[1] - l10 * w0)
        k2 = inverse_root(s00)
        l32 = s01 * k2
        k3 = inverse_root(s11 - l32 * l32)
        v2 = rb[2] - (z[0][0] * rb[0] + z[0][1] * rb[1])
        v3 = rb[3] - (z[1][0] * rb[0] + z[1][1] * rb[1])
        w2 = k2 * v2
        w3 = k3 * (v3 - l32 * w2)
        for k, w in enumerate((w0, w1, w2, w3)):
            w_ref[row0 + j + k:row0 + j + k + 1, col0:col0 + LANES] = w[0:1]


def factor_first_kernel(x_ref, y_ref, core_ref, mine_ref, other_ref, w_ref, l_ref, s_ref, g_ref):
    h = LANES
    for half, half_ref in enumerate((mine_ref, other_ref)):
        core = (core_ref[0] + half) % NC
        for dy in range(NY):
            for dx in range(NX):
                x, y = (x_ref[0] + dx) % NX, (y_ref[0] + dy) % NY
                at = pl.multiple_of(((x * NC + core) * NY + y) * SUB, SUB)
                row = (dy * NX + dx) * SUB
                g_ref[pl.ds(at, SUB), :] = half_ref[row : row + SUB, :]
    invert_factor(g_ref[:h, :h], w_ref, 0, 0)
    l21 = dot(g_ref[h:, :h], w_ref[...], NT)
    l_ref[...] = l21
    s_ref[...] = g_ref[h:, h:] - dot(l21, l21, NT)


def factor_last_kernel(w11_ref, l_ref, s_ref, p_hbm, w_ref, q_ref, p_ref, sem):
    arriving = pltpu.make_async_copy(p_hbm, p_ref, sem)
    arriving.start()
    h = LANES
    w11 = w11_ref[...]
    w_ref[:h, :h] = w11
    w_ref[:h, h:] = jnp.zeros((h, h), jnp.float32)
    invert_factor(s_ref[...], w_ref, h, h)
    w_ref[h:, :h] = -dot(w_ref[h:, h:], dot(l_ref[...], w11))
    arriving.wait()
    high, low = split(w_ref[...])
    right = jnp.concatenate([high, low, high], axis=1)
    basis = lax.dot_general(wide_left(p_ref[...]), right, NT, preferred_element_type=jnp.float32)
    q_ref[...] = wide_left(basis)


def factor_first(mine, other):
    h, w = mine.shape
    return pl.pallas_call(
        factor_first_kernel,
        in_specs=[SCALAR] * 3 + [VMEM] * 2,
        out_specs=[VMEM] * 3,
        out_shape=[jax.ShapeDtypeStruct((h, h), jnp.float32)] * 3,
        scratch_shapes=[pltpu.VMEM((w, w), jnp.float32)],
        compiler_params=params(8),
        name="factor_first",
    )(index_of("x"), index_of("y"), index_of("c"), mine, other)


def factor_last(w11, l21, schur, panels):
    n, w = panels.shape
    return pl.pallas_call(
        factor_last_kernel,
        in_specs=[VMEM] * 3 + [HBM],
        out_specs=[VMEM] * 2,
        out_shape=[jax.ShapeDtypeStruct((w, w), jnp.float32), jax.ShapeDtypeStruct((n, 3 * w), jnp.bfloat16)],
        scratch_shapes=[pltpu.VMEM((n, w), jnp.float32), pltpu.SemaphoreType.DMA(())],
        compiler_params=params(12),
        name="factor_last",
    )(w11, l21, schur, panels)


BAND = 256


def update_kernel(
    y_ref, w_ref, q_ref, x0_ref, x1_ref, x2_ref, x3_ref, c_hbm, red_hbm, top_hbm, x_ref, red_ref, top_ref, c_sem, red_sem, top_sem
):
    rounds, n, k = red_ref.shape
    bands = [pl.ds(at, BAND) for at in range(0, n, BAND)]
    arriving = [
        pltpu.make_async_copy(c_hbm.at[:, band], red_ref.at[:, band], c_sem.at[at]) for at, band in enumerate(bands)
    ]
    for copy in arriving:
        copy.start()
    for by, part_ref in enumerate((x0_ref, x1_ref, x2_ref, x3_ref)):
        x_ref[around(y_ref, by, NY, part_ref.shape[0]), :] = part_ref[...]
    top = narrow_dot(wide_left(w_ref[...]), wide_right(x_ref[...]))
    for r in range(rounds):
        top_ref[r] = top[:, r * k : (r + 1) * k]
    leaving = [pltpu.make_async_copy(top_ref, top_hbm, top_sem)]
    leaving[0].start()
    right = wide_right(top)
    for at, band in enumerate(bands):
        fit = narrow_dot(q_ref[at * BAND : (at + 1) * BAND], right)
        arriving[at].wait()
        for r in range(rounds):
            red_ref[r, at * BAND : (at + 1) * BAND] -= fit[:, r * k : (r + 1) * k]
        copy = pltpu.make_async_copy(red_ref.at[:, band], red_hbm.at[:, band], red_sem.at[at])
        copy.start()
        leaving.append(copy)
    for copy in leaving:
        copy.wait()


def update(inverse, basis, cross, columns):
    rounds, n, k = columns.shape
    w = inverse.shape[0]
    reduced, top = (rounds, n, k), (rounds, w, k)
    return pl.pallas_call(
        update_kernel,
        in_specs=[SCALAR] + [VMEM] * (2 + NY) + [HBM],
        out_specs=[HBM] * 2,
        out_shape=[jax.ShapeDtypeStruct(reduced, jnp.float32), jax.ShapeDtypeStruct(top, jnp.float32)],
        scratch_shapes=[
            pltpu.VMEM((w, rounds * k), jnp.float32),
            pltpu.VMEM(reduced, jnp.float32),
            pltpu.VMEM(top, jnp.float32),
            pltpu.SemaphoreType.DMA((n // BAND,)),
            pltpu.SemaphoreType.DMA((n // BAND,)),
            pltpu.SemaphoreType.DMA(()),
        ],
        compiler_params=params(24),
        name="update",
    )(index_of("y"), inverse, basis, *cross, columns)


def exchange_z(pieces):
    return lax.all_to_all(pieces, "z", 0, 0)


def shards(matrix):
    columns = jnp.transpose(matrix, (1, 0, 2))
    own, columns = columns[0], in_hbm(columns)
    *pieces, panels = products(relay(own), columns)
    copies, gram = sum_z(exchange_z(sum_y(deal(pieces, "y"))))
    part = exchange_z(copies).reshape(NZ * SUB, RIDE)
    gram = collect(collect(gram, "x", NX), "y", NY)
    part, gram = lax.optimization_barrier((part, gram))
    inverse, basis = factor_last(*factor_first(gram, swap(gram)), in_hbm(panels))
    reduced, top = update(inverse, basis, every(part, "y", NY), columns)
    return jnp.transpose(reduced, (1, 0, 2)), jnp.transpose(top, (1, 0, 2))


def solution(mesh):
    fine = Mesh(mesh.devices.reshape(NZ, NY, NX, NC), ("z", "y", "x", "c"))
    return jax.shard_map(
        shards,
        mesh=fine,
        in_specs=(P(("z", "y"), None, ("x", "c")),),
        out_specs=(P(("z", "y"), None, ("x", "c")), P(None, None, ("x", "c"))),
        check_vma=False,
    )
```

profile of v0, /device:TPU:8, one launch (start us, length us, event | category | flops | bytes accessed | tf_op | source)
XLA Modules:
  0.0 119.7 jit_solution(4097382570539950939)
XLA Ops:
  0.6 1.1 slice_bitcast_fusion
  1.7 4.7 %collective-permute-start.4 = (f32[512,128]{1,0:T(8,128)S(1)}, f32[512,128]{1,0:T(8,128)S(1)}, u32[]{:S(2)}, u32[]{:S(2)}) collective-permute-start(f32[512,128]{1,0:T(8,128)S(1)} %get-tuple-element.36), channel_id=1, source_target_pairs={{0,6},{1,7},{8,14},{9,15},{16,22},{17,23},{24,30},{25,31},{32,38},... | collective-permute-start | bytes 786440 | tf_op jit(solution)/shard_map/ppermute | solution.py:64
  6.4 1.3 %collective-permute-start = (f32[512,128]{1,0:T(8,128)S(1)}, f32[512,128]{1,0:T(8,128)S(1)}, u32[]{:S(2)}, u32[]{:S(2)}) collective-permute-start(f32[512,128]{1,0:T(8,128)S(1)} %get-tuple-element.37), channel_id=1, source_target_pairs={{0,2},{1,3},{8,10},{9,11},{16,18},{17,19},{24,26},{25,27},{32,34},... | collective-permute-start | bytes 786440 | tf_op jit(solution)/shard_map/ppermute | solution.py:63
  7.7 1.3 %collective-permute-start.3 = (f32[512,128]{1,0:T(8,128)S(1)}, f32[512,128]{1,0:T(8,128)S(1)}, u32[]{:S(2)}, u32[]{:S(2)}) collective-permute-start(f32[512,128]{1,0:T(8,128)S(1)} %get-tuple-element.36), channel_id=1, source_target_pairs={{0,2},{1,3},{8,10},{9,11},{16,18},{17,19},{24,26},{25,27},{32,34},... | collective-permute-start | bytes 786440 | tf_op jit(solution)/shard_map/ppermute | solution.py:65
  9.0 1.3 %collective-permute-start.2 = (f32[512,128]{1,0:T(8,128)S(1)}, f32[512,128]{1,0:T(8,128)S(1)}, u32[]{:S(2)}, u32[]{:S(2)}) collective-permute-start(f32[512,128]{1,0:T(8,128)S(1)} %get-tuple-element.37), channel_id=1, source_target_pairs={{0,6},{1,7},{8,14},{9,15},{16,22},{17,23},{24,30},{25,31},{32,38},... | collective-permute-start | bytes 786440 | tf_op jit(solution)/shard_map/ppermute | solution.py:66
  10.3 2.7 %collective-permute-done.4 = f32[512,128]{1,0:T(8,128)S(1)} collective-permute-done((f32[512,128]{1,0:T(8,128)S(1)}, f32[512,128]{1,0:T(8,128)S(1)}, u32[]{:S(2)}, u32[]{:S(2)}) %collective-permute-start.4) | collective-permute-done | bytes 262176 | tf_op jit(solution)/shard_map/ppermute | solution.py:64
  13.1 0.7 collective-permute-start.5
  13.7 0.6 collective-permute-done
  14.4 0.7 collective-permute-start.1
  15.1 3.8 %collective-permute-done.3 = f32[512,128]{1,0:T(8,128)S(1)} collective-permute-done((f32[512,128]{1,0:T(8,128)S(1)}, f32[512,128]{1,0:T(8,128)S(1)}, u32[]{:S(2)}, u32[]{:S(2)}) %collective-permute-start.3) | collective-permute-done | bytes 262176 | tf_op jit(solution)/shard_map/ppermute | solution.py:65
  18.8 0.0 collective-permute-done.2
  18.9 0.0 collective-permute-done.5
  18.9 0.0 collective-permute-done.1
  18.9 1.1 select_select_fusion
  20.0 0.1 collective-permute-start.7
  20.1 0.5 collective-permute-start.6
  20.6 1.0 collective-permute-done.7.oh_ref
  21.6 0.4 collective-permute-done.6.ol_ref
  22.0 5.0 %products.1 = (f32[64,1408]{1,0:T(8,128)S(1)}, f32[64,1408]{1,0:T(8,128)S(1)}, f32[64,1408]{1,0:T(8,128)S(1)}, f32[64,1408]{1,0:T(8,128)S(1)}, f32[1024,256]{1,0:T(8,128)S(1)}) custom-call(s32[1]{0:T(128)} %bitcast.1.x_ref, s32[1]{0:T(128)} %bitcast.y_ref, s32[1]{0:T(128)} %bitcast.2.core_ref, f32[512,128]{1,0:T(8,128)S(1)} %get-tuple-element.35.ml_ref, ...), custom_call_target="tpu_custom_call" | custom-call | tf_op jit(solution)/shard_map/products/pallas_call | solution.py:137
  27.0 0.0 copy-start
  27.0 1.7 %collective-permute-start.8 = (f32[64,1408]{1,0:T(8,128)S(1)}, f32[64,1408]{1,0:T(8,128)S(1)}, u32[]{:S(2)}, u32[]{:S(2)}) collective-permute-start(f32[64,1408]{1,0:T(8,128)S(1)} %get-tuple-element.19), channel_id=1, source_target_pairs={{0,8},{8,16},{16,24},{24,0},{1,9},{9,17},{17,25},{25,1},{2,10},{10... | collective-permute-start | bytes 1081352 | tf_op jit(solution)/shard_map/ppermute | solution.py:200
  28.6 0.9 collective-permute-start.9
  29.6 2.4 %collective-permute-start.10 = (f32[64,1408]{1,0:T(8,128)S(1)}, f32[64,1408]{1,0:T(8,128)S(1)}, u32[]{:S(2)}, u32[]{:S(2)}) collective-permute-start(f32[64,1408]{1,0:T(8,128)S(1)} %get-tuple-element.21), channel_id=1, source_target_pairs={{0,24},{8,0},{16,8},{24,16},{1,25},{9,1},{17,9},{25,17},{2,26},{10... | collective-permute-start | bytes 1081352 | tf_op jit(solution)/shard_map/ppermute | solution.py:200
  32.0 6.3 %collective-permute-done.8.a1_ref = f32[64,1408]{1,0:T(8,128)S(1)} collective-permute-done((f32[64,1408]{1,0:T(8,128)S(1)}, f32[64,1408]{1,0:T(8,128)S(1)}, u32[]{:S(2)}, u32[]{:S(2)}) %collective-permute-start.8) | collective-permute-done | bytes 360480 | tf_op jit(solution)/shard_map/ppermute | solution.py:200
  38.3 3.1 %collective-permute-done.9.a2_ref = f32[64,1408]{1,0:T(8,128)S(1)} collective-permute-done((f32[64,1408]{1,0:T(8,128)S(1)}, f32[64,1408]{1,0:T(8,128)S(1)}, u32[]{:S(2)}, u32[]{:S(2)}) %collective-permute-start.9) | collective-permute-done | bytes 360480 | tf_op jit(solution)/shard_map/ppermute | solution.py:200
  41.4 5.9 %collective-permute-done.10.a3_ref = f32[64,1408]{1,0:T(8,128)S(1)} collective-permute-done((f32[64,1408]{1,0:T(8,128)S(1)}, f32[64,1408]{1,0:T(8,128)S(1)}, u32[]{:S(2)}, u32[]{:S(2)}) %collective-permute-start.10) | collective-permute-done | bytes 360480 | tf_op jit(solution)/shard_map/ppermute | solution.py:200
  47.4 0.1 sum_y.1
  47.4 22.4 %all_to_all.10.a_ref = f32[8,8,1536]{2,1,0:T(8,128)S(1)} all-to-all(f32[8,8,1536]{2,1,0:T(8,128)S(1)} %sum_y.1), channel_id=1, replica_groups=mesh['z'=8,'y'=4,'x'=4,'c'=2] {'z'}, dimensions={0} | all-to-all | bytes 786432 | tf_op jit(solution)/shard_map/all_to_all | solution.py:403
  69.8 0.8 sum_z.1
  70.6 0.0 copy-done
  70.6 3.2 %collective-permute-start.13 = (f32[8,256]{1,0:T(8,128)S(1)}, f32[8,256]{1,0:T(8,128)S(1)}, u32[]{:S(2)}, u32[]{:S(2)}) collective-permute-start(f32[8,256]{1,0:T(8,128)S(1)} %get-tuple-element.23), channel_id=1, source_target_pairs={{0,2},{2,4},{4,6},{6,0},{1,3},{3,5},{5,7},{7,1},{8,10},{10,12},{12... | collective-permute-start | bytes 24584 | tf_op jit(solution)/shard_map/ppermute | solution.py:206
  73.7 2.5 %collective-permute-start.12 = (f32[8,256]{1,0:T(8,128)S(1)}, f32[8,256]{1,0:T(8,128)S(1)}, u32[]{:S(2)}, u32[]{:S(2)}) collective-permute-start(f32[8,256]{1,0:T(8,128)S(1)} %get-tuple-element.23), channel_id=1, source_target_pairs={{0,4},{2,6},{4,0},{6,2},{1,5},{3,7},{5,1},{7,3},{8,12},{10,14},{12... | collective-permute-start | bytes 24584 | tf_op jit(solution)/shard_map/ppermute | solution.py:206
  76.3 2.6 %collective-permute-start.11 = (f32[8,256]{1,0:T(8,128)S(1)}, f32[8,256]{1,0:T(8,128)S(1)}, u32[]{:S(2)}, u32[]{:S(2)}) collective-permute-start(f32[8,256]{1,0:T(8,128)S(1)} %get-tuple-element.23), channel_id=1, source_target_pairs={{0,6},{2,0},{4,2},{6,4},{1,7},{3,1},{5,3},{7,5},{8,14},{10,8},{12,... | collective-permute-start | bytes 24584 | tf_op jit(solution)/shard_map/ppermute | solution.py:206
  78.9 3.4 %all-to-all-start.1 = ((f32[8,8,1280]{2,1,0:T(8,128)}), f32[8,8,1280]{2,1,0:T(8,128)S(1)}, u32[]{:S(2)}, u32[]{:S(2)}) async-start(f32[8,8,1280]{2,1,0:T(8,128)} %get-tuple-element.22), calls=%async_computation.1 | async-start | bytes 655360 | tf_op jit(solution)/shard_map/all_to_all | solution.py:403
  82.3 0.0 collective-permute-done.11
  82.4 0.0 collective-permute-done.12
  82.4 0.0 collective-permute-done.13
  82.4 0.9 collective-permute-start.14
  83.3 1.2 %collective-permute-start.16 = (f32[32,256]{1,0:T(8,128)S(1)}, f32[32,256]{1,0:T(8,128)S(1)}, u32[]{:S(2)}, u32[]{:S(2)}) collective-permute-start(f32[32,256]{1,0:T(8,128)S(1)} %get-tuple-element.38), channel_id=1, source_target_pairs={{0,8},{8,16},{16,24},{24,0},{1,9},{9,17},{17,25},{25,1},{2,10},{10... | collective-permute-start | bytes 98312 | tf_op jit(solution)/shard_map/ppermute | solution.py:206
  84.5 3.7 %collective-permute-start.15 = (f32[32,256]{1,0:T(8,128)S(1)}, f32[32,256]{1,0:T(8,128)S(1)}, u32[]{:S(2)}, u32[]{:S(2)}) collective-permute-start(f32[32,256]{1,0:T(8,128)S(1)} %get-tuple-element.38), channel_id=1, source_target_pairs={{0,16},{8,24},{16,0},{24,8},{1,17},{9,25},{17,1},{25,9},{2,18},{10... | collective-permute-start | bytes 98312 | tf_op jit(solution)/shard_map/ppermute | solution.py:206
  88.2 0.0 collective-permute-done.14
  88.2 1.9 %collective-permute-done.15 = f32[32,256]{1,0:T(8,128)S(1)} collective-permute-done((f32[32,256]{1,0:T(8,128)S(1)}, f32[32,256]{1,0:T(8,128)S(1)}, u32[]{:S(2)}, u32[]{:S(2)}) %collective-permute-start.15) | collective-permute-done | bytes 32800 | tf_op jit(solution)/shard_map/ppermute | solution.py:206
  90.1 0.0 collective-permute-done.16
  90.1 3.3 %all-to-all-done.1 = f32[8,8,1280]{2,1,0:T(8,128)S(1)} async-done(((f32[8,8,1280]{2,1,0:T(8,128)}), f32[8,8,1280]{2,1,0:T(8,128)S(1)}, u32[]{:S(2)}, u32[]{:S(2)}) %all-to-all-start.1) | async-done | bytes 327712 | tf_op jit(solution)/shard_map/all_to_all | solution.py:403
  93.4 1.0 collective-permute-start.20
  94.5 1.8 %collective-permute-start.19 = (f32[64,1280]{1,0:T(8,128)S(1)}, f32[64,1280]{1,0:T(8,128)S(1)}, u32[]{:S(2)}, u32[]{:S(2)}) collective-permute-start(f32[64,1280]{1,0:T(8,128)S(1)} %bitcast.16), channel_id=1, source_target_pairs={{0,16},{8,24},{16,0},{24,8},{1,17},{9,25},{17,1},{25,9},{2,18},{10... | collective-permute-start | bytes 983048 | tf_op jit(solution)/shard_map/ppermute | solution.py:206
  96.3 2.3 %collective-permute-start.18 = (f32[64,1280]{1,0:T(8,128)S(1)}, f32[64,1280]{1,0:T(8,128)S(1)}, u32[]{:S(2)}, u32[]{:S(2)}) collective-permute-start(f32[64,1280]{1,0:T(8,128)S(1)} %bitcast.17), channel_id=1, source_target_pairs={{0,24},{8,0},{16,8},{24,16},{1,25},{9,1},{17,9},{25,17},{2,26},{10... | collective-permute-start | bytes 983048 | tf_op jit(solution)/shard_map/ppermute | solution.py:206
  98.7 0.0 collective-permute-start.17
  98.7 1.3 %collective-permute-done.17.other_ref = f32[128,256]{1,0:T(8,128)S(1)} collective-permute-done((f32[128,256]{1,0:T(8,128)S(1)}, f32[128,256]{1,0:T(8,128)S(1)}, u32[]{:S(2)}, u32[]{:S(2)}) %collective-permute-start.17) | collective-permute-done | bytes 131104 | tf_op jit(solution)/shard_map/ppermute | solution.py:56
  100.0 6.6 %factor_first.1 = (f32[128,128]{1,0:T(8,128)S(1)}, f32[128,128]{1,0:T(8,128)S(1)}, f32[128,128]{1,0:T(8,128)S(1)}) custom-call(s32[1]{0:T(128)} %bitcast.1.x_ref, s32[1]{0:T(128)} %bitcast.y_ref, s32[1]{0:T(128)} %bitcast.2.core_ref, f32[128,256]{1,0:T(8,128)S(1)} %constant_dynamic-update-slice_fusion.4.mine_ref, ...), custom_call_target="tpu_custom_call" | custom-call | tf_op jit(solution)/shard_map/factor_first/pallas_call | solution.py:323
  106.6 7.3 %factor_last.1 = (f32[256,256]{1,0:T(8,128)S(1)}, bf16[1024,768]{1,0:T(8,128)(2,1)S(1)}) custom-call(f32[128,128]{1,0:T(8,128)S(1)} %get-tuple-element.25.w11_ref, f32[128,128]{1,0:T(8,128)S(1)} %get-tuple-element.26.l_ref, f32[128,128]{1,0:T(8,128)S(1)} %get-tuple-element.27.s_ref, f32[1024,256]{1,0:T(8,128)} %copy-done), custom_call_target="tpu_custom_call" | custom-call | tf_op jit(solution)/shard_map/factor_last/pallas_call | solution.py:336
  113.9 0.0 collective-permute-done.20.x3_ref
  114.0 0.0 collective-permute-done.19.x2_ref
  114.0 0.0 collective-permute-done.18.x1_ref
  114.0 5.5 %update.1 = (f32[10,1024,128]{2,1,0:T(8,128)}, f32[10,256,128]{2,1,0:T(8,128)}) custom-call(s32[1]{0:T(128)} %bitcast.y_ref, f32[256,256]{1,0:T(8,128)S(1)} %get-tuple-element.29.w_ref, bf16[1024,768]{1,0:T(8,128)(2,1)S(1)} %get-tuple-element.30.q_ref, f32[64,1280]{1,0:T(8,128)S(1)} %bitcast.18, f32[64,1280]{1,0:T(8,128)S(1)} %collective-permute-done.18.x1_ref, ...), custom_call_target="tpu_custom_call" | custom-call | tf_op jit(solution)/shard_map/update/pallas_call | solution.py:384
  (7 shorter events, 0.0 us)
Async XLA Ops:
  1.7 11.4 %collective-permute-start.4 = (f32[512,128]{1,0:T(8,128)S(1)}, f32[512,128]{1,0:T(8,128)S(1)}, u32[]{:S(2)}, u32[]{:S(2)}) collective-permute-start(f32[512,128]{1,0:T(8,128)S(1)} %get-tuple-element.36), channel_id=1, source_target_pairs={{0,6},{1,7},{8,14},{9,15},{16,22},{17,23},{24,30},{25,31},{32,38},... | collective-permute-start | bytes 786440 | tf_op jit(solution)/shard_map/ppermute | solution.py:64
  6.4 8.0 %collective-permute-start = (f32[512,128]{1,0:T(8,128)S(1)}, f32[512,128]{1,0:T(8,128)S(1)}, u32[]{:S(2)}, u32[]{:S(2)}) collective-permute-start(f32[512,128]{1,0:T(8,128)S(1)} %get-tuple-element.37), channel_id=1, source_target_pairs={{0,2},{1,3},{8,10},{9,11},{16,18},{17,19},{24,26},{25,27},{32,34},... | collective-permute-start | bytes 786440 | tf_op jit(solution)/shard_map/ppermute | solution.py:63
  7.7 11.1 %collective-permute-start.3 = (f32[512,128]{1,0:T(8,128)S(1)}, f32[512,128]{1,0:T(8,128)S(1)}, u32[]{:S(2)}, u32[]{:S(2)}) collective-permute-start(f32[512,128]{1,0:T(8,128)S(1)} %get-tuple-element.36), channel_id=1, source_target_pairs={{0,2},{1,3},{8,10},{9,11},{16,18},{17,19},{24,26},{25,27},{32,34},... | collective-permute-start | bytes 786440 | tf_op jit(solution)/shard_map/ppermute | solution.py:65
  9.0 9.8 %collective-permute-start.2 = (f32[512,128]{1,0:T(8,128)S(1)}, f32[512,128]{1,0:T(8,128)S(1)}, u32[]{:S(2)}, u32[]{:S(2)}) collective-permute-start(f32[512,128]{1,0:T(8,128)S(1)} %get-tuple-element.37), channel_id=1, source_target_pairs={{0,6},{1,7},{8,14},{9,15},{16,22},{17,23},{24,30},{25,31},{32,38},... | collective-permute-start | bytes 786440 | tf_op jit(solution)/shard_map/ppermute | solution.py:66
  13.1 5.8 %collective-permute-start.5 = (f32[512,128]{1,0:T(8,128)S(1)}, f32[512,128]{1,0:T(8,128)S(1)}, u32[]{:S(2)}, u32[]{:S(2)}) collective-permute-start(f32[512,128]{1,0:T(8,128)S(1)} %collective-permute-done.4), channel_id=1, source_target_pairs={{6,4},{7,5},{14,12},{15,13},{22,20},{23,21},{30,28},{31,29},{38,36... | collective-permute-start | bytes 786440 | tf_op jit(solution)/shard_map/ppermute | solution.py:68
  14.4 4.5 %collective-permute-start.1 = (f32[512,128]{1,0:T(8,128)S(1)}, f32[512,128]{1,0:T(8,128)S(1)}, u32[]{:S(2)}, u32[]{:S(2)}) collective-permute-start(f32[512,128]{1,0:T(8,128)S(1)} %collective-permute-done), channel_id=1, source_target_pairs={{2,4},{3,5},{10,12},{11,13},{18,20},{19,21},{26,28},{27,29},{34,36... | collective-permute-start | bytes 786440 | tf_op jit(solution)/shard_map/ppermute | solution.py:67
  20.0 1.6 %collective-permute-start.7 = (f32[512,128]{1,0:T(8,128)S(1)}, f32[512,128]{1,0:T(8,128)S(1)}, u32[]{:S(2)}, u32[]{:S(2)}) collective-permute-start(f32[512,128]{1,0:T(8,128)S(1)} %get-tuple-element.34.mh_ref), channel_id=1, source_target_pairs={{0,1},{1,0},{2,3},{3,2},{4,5},{5,4},{6,7},{7,6},{8,9},{9,8},{10,11... | collective-permute-start | bytes 786440 | tf_op jit(solution)/shard_map/ppermute | solution.py:56
  20.1 1.9 %collective-permute-start.6 = (f32[512,128]{1,0:T(8,128)S(1)}, f32[512,128]{1,0:T(8,128)S(1)}, u32[]{:S(2)}, u32[]{:S(2)}) collective-permute-start(f32[512,128]{1,0:T(8,128)S(1)} %get-tuple-element.35.ml_ref), channel_id=1, source_target_pairs={{0,1},{1,0},{2,3},{3,2},{4,5},{5,4},{6,7},{7,6},{8,9},{9,8},{10,11... | collective-permute-start | bytes 786440 | tf_op jit(solution)/shard_map/ppermute | solution.py:56
  27.0 43.6 %copy-start = (f32[1024,256]{1,0:T(8,128)}, f32[1024,256]{1,0:T(8,128)S(1)}, u32[]{:S(2)}) copy-start(f32[1024,256]{1,0:T(8,128)S(1)} %get-tuple-element.28.p_hbm) | copy-start | bytes 3145732
  27.0 11.3 %collective-permute-start.8 = (f32[64,1408]{1,0:T(8,128)S(1)}, f32[64,1408]{1,0:T(8,128)S(1)}, u32[]{:S(2)}, u32[]{:S(2)}) collective-permute-start(f32[64,1408]{1,0:T(8,128)S(1)} %get-tuple-element.19), channel_id=1, source_target_pairs={{0,8},{8,16},{16,24},{24,0},{1,9},{9,17},{17,25},{25,1},{2,10},{10... | collective-permute-start | bytes 1081352 | tf_op jit(solution)/shard_map/ppermute | solution.py:200
  28.6 12.8 %collective-permute-start.9 = (f32[64,1408]{1,0:T(8,128)S(1)}, f32[64,1408]{1,0:T(8,128)S(1)}, u32[]{:S(2)}, u32[]{:S(2)}) collective-permute-start(f32[64,1408]{1,0:T(8,128)S(1)} %get-tuple-element.20), channel_id=1, source_target_pairs={{0,16},{8,24},{16,0},{24,8},{1,17},{9,25},{17,1},{25,9},{2,18},{10... | collective-permute-start | bytes 1081352 | tf_op jit(solution)/shard_map/ppermute | solution.py:200
  29.6 17.8 %collective-permute-start.10 = (f32[64,1408]{1,0:T(8,128)S(1)}, f32[64,1408]{1,0:T(8,128)S(1)}, u32[]{:S(2)}, u32[]{:S(2)}) collective-permute-start(f32[64,1408]{1,0:T(8,128)S(1)} %get-tuple-element.21), channel_id=1, source_target_pairs={{0,24},{8,0},{16,8},{24,16},{1,25},{9,1},{17,9},{25,17},{2,26},{10... | collective-permute-start | bytes 1081352 | tf_op jit(solution)/shard_map/ppermute | solution.py:200
  70.6 11.8 %collective-permute-start.13 = (f32[8,256]{1,0:T(8,128)S(1)}, f32[8,256]{1,0:T(8,128)S(1)}, u32[]{:S(2)}, u32[]{:S(2)}) collective-permute-start(f32[8,256]{1,0:T(8,128)S(1)} %get-tuple-element.23), channel_id=1, source_target_pairs={{0,2},{2,4},{4,6},{6,0},{1,3},{3,5},{5,7},{7,1},{8,10},{10,12},{12... | collective-permute-start | bytes 24584 | tf_op jit(solution)/shard_map/ppermute | solution.py:206
  73.7 8.6 %collective-permute-start.12 = (f32[8,256]{1,0:T(8,128)S(1)}, f32[8,256]{1,0:T(8,128)S(1)}, u32[]{:S(2)}, u32[]{:S(2)}) collective-permute-start(f32[8,256]{1,0:T(8,128)S(1)} %get-tuple-element.23), channel_id=1, source_target_pairs={{0,4},{2,6},{4,0},{6,2},{1,5},{3,7},{5,1},{7,3},{8,12},{10,14},{12... | collective-permute-start | bytes 24584 | tf_op jit(solution)/shard_map/ppermute | solution.py:206
  76.3 6.1 %collective-permute-start.11 = (f32[8,256]{1,0:T(8,128)S(1)}, f32[8,256]{1,0:T(8,128)S(1)}, u32[]{:S(2)}, u32[]{:S(2)}) collective-permute-start(f32[8,256]{1,0:T(8,128)S(1)} %get-tuple-element.23), channel_id=1, source_target_pairs={{0,6},{2,0},{4,2},{6,4},{1,7},{3,1},{5,3},{7,5},{8,14},{10,8},{12,... | collective-permute-start | bytes 24584 | tf_op jit(solution)/shard_map/ppermute | solution.py:206
  78.9 14.5 %all-to-all-start.1 = ((f32[8,8,1280]{2,1,0:T(8,128)}), f32[8,8,1280]{2,1,0:T(8,128)S(1)}, u32[]{:S(2)}, u32[]{:S(2)}) async-start(f32[8,8,1280]{2,1,0:T(8,128)} %get-tuple-element.22), calls=%async_computation.1 | async-start | bytes 655360 | tf_op jit(solution)/shard_map/all_to_all | solution.py:403
  82.4 5.8 %collective-permute-start.14 = (f32[32,256]{1,0:T(8,128)S(1)}, f32[32,256]{1,0:T(8,128)S(1)}, u32[]{:S(2)}, u32[]{:S(2)}) collective-permute-start(f32[32,256]{1,0:T(8,128)S(1)} %get-tuple-element.38), channel_id=1, source_target_pairs={{0,24},{8,0},{16,8},{24,16},{1,25},{9,1},{17,9},{25,17},{2,26},{10... | collective-permute-start | bytes 98312 | tf_op jit(solution)/shard_map/ppermute | solution.py:206
  83.3 6.8 %collective-permute-start.16 = (f32[32,256]{1,0:T(8,128)S(1)}, f32[32,256]{1,0:T(8,128)S(1)}, u32[]{:S(2)}, u32[]{:S(2)}) collective-permute-start(f32[32,256]{1,0:T(8,128)S(1)} %get-tuple-element.38), channel_id=1, source_target_pairs={{0,8},{8,16},{16,24},{24,0},{1,9},{9,17},{17,25},{25,1},{2,10},{10... | collective-permute-start | bytes 98312 | tf_op jit(solution)/shard_map/ppermute | solution.py:206
  84.5 5.6 %collective-permute-start.15 = (f32[32,256]{1,0:T(8,128)S(1)}, f32[32,256]{1,0:T(8,128)S(1)}, u32[]{:S(2)}, u32[]{:S(2)}) collective-permute-start(f32[32,256]{1,0:T(8,128)S(1)} %get-tuple-element.38), channel_id=1, source_target_pairs={{0,16},{8,24},{16,0},{24,8},{1,17},{9,25},{17,1},{25,9},{2,18},{10... | collective-permute-start | bytes 98312 | tf_op jit(solution)/shard_map/ppermute | solution.py:206
  93.4 20.5 %collective-permute-start.20 = (f32[64,1280]{1,0:T(8,128)S(1)}, f32[64,1280]{1,0:T(8,128)S(1)}, u32[]{:S(2)}, u32[]{:S(2)}) collective-permute-start(f32[64,1280]{1,0:T(8,128)S(1)} %bitcast.15), channel_id=1, source_target_pairs={{0,8},{8,16},{16,24},{24,0},{1,9},{9,17},{17,25},{25,1},{2,10},{10... | collective-permute-start | bytes 983048 | tf_op jit(solution)/shard_map/ppermute | solution.py:206
  94.5 19.5 %collective-permute-start.19 = (f32[64,1280]{1,0:T(8,128)S(1)}, f32[64,1280]{1,0:T(8,128)S(1)}, u32[]{:S(2)}, u32[]{:S(2)}) collective-permute-start(f32[64,1280]{1,0:T(8,128)S(1)} %bitcast.16), channel_id=1, source_target_pairs={{0,16},{8,24},{16,0},{24,8},{1,17},{9,25},{17,1},{25,9},{2,18},{10... | collective-permute-start | bytes 983048 | tf_op jit(solution)/shard_map/ppermute | solution.py:206
  96.3 17.7 %collective-permute-start.18 = (f32[64,1280]{1,0:T(8,128)S(1)}, f32[64,1280]{1,0:T(8,128)S(1)}, u32[]{:S(2)}, u32[]{:S(2)}) collective-permute-start(f32[64,1280]{1,0:T(8,128)S(1)} %bitcast.17), channel_id=1, source_target_pairs={{0,24},{8,0},{16,8},{24,16},{1,25},{9,1},{17,9},{25,17},{2,26},{10... | collective-permute-start | bytes 983048 | tf_op jit(solution)/shard_map/ppermute | solution.py:206
  98.7 1.3 %collective-permute-start.17 = (f32[128,256]{1,0:T(8,128)S(1)}, f32[128,256]{1,0:T(8,128)S(1)}, u32[]{:S(2)}, u32[]{:S(2)}) collective-permute-start(f32[128,256]{1,0:T(8,128)S(1)} %constant_dynamic-update-slice_fusion.4.mine_ref), channel_id=1, source_target_pairs={{0,1},{1,0},{2,3},{3,2},{4,5},{5,4},{6,7},{7,6},{8,9},{9,8},{10,11... | collective-permute-start | bytes 393224 | tf_op jit(solution)/shard_map/ppermute | solution.py:56
where the time goes:
time: 121 us; the launch traced here: 120 us
  starting transfers between devices  38.3 us (32%)
  waiting for transfers between devices  30.5 us (25%)
  Pallas kernels  25.2 us (21%)
  blocking collectives  22.4 us (19%)
    all_to_all x1, blocking collectives, exchange_z(): return lax.all_to_all(pieces, 'z', 0, 0)  22.4 us
    ppermute x9, starting transfers between devices, every(): lax.ppermute(values, axis, [(at, (at - by) % size) for at in range(size)])  19.3 us
    ppermute x3, waiting for transfers between devices, deal(): lax.ppermute(pieces[by], axis, [(at, (at + by) % size) for at in range(si...  15.4 us
    pallas_call x1, Pallas kernels, factor_last(): pl.pallas_call(factor_last_kernel, in_specs=[VMEM] * 3 + [HBM], out_specs...  7.35 us
    pallas_call x1, Pallas kernels, factor_first(): pl.pallas_call(factor_first_kernel, in_specs=[SCALAR] * 3 + [VMEM] * 2, o...  6.58 us
    pallas_call x1, Pallas kernels, update(): pl.pallas_call(update_kernel, in_specs=[SCALAR] + [VMEM] * (2 + NY) + [HB...  5.52 us
    ppermute x3, starting transfers between devices, deal(): lax.ppermute(pieces[by], axis, [(at, (at + by) % size) for at in range(si...  5 us
    pallas_call x1, Pallas kernels, products(): pl.pallas_call(products_kernel, in_specs=[SCALAR] * 3 + [VMEM] * 4 + [HBM...  4.97 us
  transfers between devices with their start and end apart: 22, of which 11 were waited for; matrix products, arithmetic and copies ran while one was open for 0% of the time, Pallas kernels for 12%

commit v1 on v0

--- a/solution.py
+++ b/solution.py
@@ -56,16 +56,24 @@
     return lax.ppermute(values, "c", [(0, 1), (1, 0)])
 
 
+def turned(axis, size, pairs):
+    sign = [1, size - 1]
+    return dict(
+        axis_name=(axis, "c"),
+        perm=[(a * sign[c] % size * NC + c, b * sign[c] % size * NC + c) for a, b in pairs for c in range(NC)],
+    )
+
+
 def relay(own):
-    x = lax.axis_index("x")
+    x = lax.axis_index("x") * jnp.where(lax.axis_index("c") == 0, 1, NX - 1) % NX
     half = own.shape[0] // 2
     low, high = own[:half], own[half:]
-    up_low = lax.ppermute(low, "x", [(0, 1)])
-    down_high = lax.ppermute(high, "x", [(0, 3)])
-    up_high = lax.ppermute(high, "x", [(0, 1)])
-    down_low = lax.ppermute(low, "x", [(0, 3)])
-    on_low = lax.ppermute(up_low, "x", [(1, 2)])
-    on_high = lax.ppermute(down_high, "x", [(3, 2)])
+    up_low = lax.ppermute(low, **turned("x", NX, [(0, 1)]))
+    down_high = lax.ppermute(high, **turned("x", NX, [(0, 3)]))
+    up_high = lax.ppermute(high, **turned("x", NX, [(0, 1)]))
+    down_low = lax.ppermute(low, **turned("x", NX, [(0, 3)]))
+    on_low = lax.ppermute(up_low, **turned("x", NX, [(1, 2)]))
+    on_high = lax.ppermute(down_high, **turned("x", NX, [(3, 2)]))
     mine_low = pick(x, [low, up_low, on_low, down_low])
     mine_high = pick(x, [high, up_high, on_high, down_high])
     return mine_low, mine_high, swap(mine_low), swap(mine_high)
@@ -88,8 +96,8 @@
         p_ref[rows, k:] = jnp.where(first, other, mine)
 
 
-def around(at_ref, by, size, rows, base=0):
-    return pl.ds(pl.multiple_of(base + ((at_ref[0] + by) % size) * rows, SUB), rows)
+def around(y_ref, core_ref, by, rows, base=0):
+    return pl.ds(pl.multiple_of(base + ((y_ref[0] + by * (1 + (NY - 2) * core_ref[0])) % NY) * rows, SUB), rows)
 
 
 def fetch(source, target, sem):
@@ -111,9 +119,9 @@
     t_ref[...] = p_ref[...].T
     outs = (o0_ref, o1_ref, o2_ref, o3_ref)
     part = w // NY
-    left = wide_left(jnp.concatenate([t_ref[around(y_ref, by, NY, part), :] for by in range(NY)], axis=0))
+    left = wide_left(jnp.concatenate([t_ref[around(y_ref, core_ref, by, part), :] for by in range(NY)], axis=0))
     base = (x_ref[0] * NC + core_ref[0]) * (NY * SUB)
-    rows = [t_ref[around(y_ref, by, NY, SUB, base), :] for by in range(NY)]
+    rows = [t_ref[around(y_ref, core_ref, by, SUB, base), :] for by in range(NY)]
     gram = dot(jnp.concatenate(rows, axis=0), p_ref[...])
     for by, o_ref in enumerate(outs):
         piece = gram[by * SUB : (by + 1) * SUB]
@@ -194,21 +202,20 @@
     )(pieces)
 
 
-def deal(pieces, axis):
-    size = len(pieces)
-    return [pieces[0]] + [
-        lax.ppermute(pieces[by], axis, [(at, (at + by) % size) for at in range(size)]) for by in range(1, size)
-    ]
-
-
-def every(values, axis, size):
-    return [values] + [
-        lax.ppermute(values, axis, [(at, (at - by) % size) for at in range(size)]) for by in range(1, size)
-    ]
-
-
-def collect(values, axis, size):
-    return jnp.concatenate(every(values, axis, size), axis=0)
+def deal(pieces):
+    hops = [[(y, (y + by) % NY) for y in range(NY)] for by in range(1, NY)]
+    return [pieces[0]] + [lax.ppermute(piece, **turned("y", NY, pairs)) for piece, pairs in zip(pieces[1:], hops)]
+
+
+def every(values):
+    hops = [[(y, (y - by) % NY) for y in range(NY)] for by in range(1, NY)]
+    return [values] + [lax.ppermute(values, **turned("y", NY, pairs)) for pairs in hops]
+
+
+def collect(values):
+    for axis in ("x", "y", "c"):
+        values = lax.all_gather(values, axis, tiled=True)
+    return values
 
 
 def inverse_root(d):
@@ -286,16 +293,13 @@
             w_ref[row0 + j + k:row0 + j + k + 1, col0:col0 + LANES] = w[0:1]
 
 
-def factor_first_kernel(x_ref, y_ref, core_ref, mine_ref, other_ref, w_ref, l_ref, s_ref, g_ref):
+def factor_first_kernel(p_ref, w_ref, l_ref, s_ref, g_ref):
     h = LANES
-    for half, half_ref in enumerate((mine_ref, other_ref)):
-        core = (core_ref[0] + half) % NC
-        for dy in range(NY):
-            for dx in range(NX):
-                x, y = (x_ref[0] + dx) % NX, (y_ref[0] + dy) % NY
-                at = pl.multiple_of(((x * NC + core) * NY + y) * SUB, SUB)
-                row = (dy * NX + dx) * SUB
-                g_ref[pl.ds(at, SUB), :] = half_ref[row : row + SUB, :]
+    for c in range(NC):
+        for y in range(NY):
+            for x in range(NX):
+                row, at = ((c * NY + y) * NX + x) * SUB, ((x * NC + c) * NY + y) * SUB
+                g_ref[at : at + SUB, :] = p_ref[row : row + SUB, :]
     invert_factor(g_ref[:h, :h], w_ref, 0, 0)
     l21 = dot(g_ref[h:, :h], w_ref[...], NT)
     l_ref[...] = l21
@@ -318,17 +322,18 @@
     q_ref[...] = wide_left(basis)
 
 
-def factor_first(mine, other):
-    h, w = mine.shape
+def factor_first(pieces):
+    w = pieces.shape[0]
+    h = w // 2
     return pl.pallas_call(
         factor_first_kernel,
-        in_specs=[SCALAR] * 3 + [VMEM] * 2,
+        in_specs=[VMEM],
         out_specs=[VMEM] * 3,
         out_shape=[jax.ShapeDtypeStruct((h, h), jnp.float32)] * 3,
         scratch_shapes=[pltpu.VMEM((w, w), jnp.float32)],
         compiler_params=params(8),
         name="factor_first",
-    )(index_of("x"), index_of("y"), index_of("c"), mine, other)
+    )(pieces)
 
 
 def factor_last(w11, l21, schur, panels):
@@ -348,7 +353,7 @@
 
 
 def update_kernel(
-    y_ref, w_ref, q_ref, x0_ref, x1_ref, x2_ref, x3_ref, c_hbm, red_hbm, top_hbm, x_ref, red_ref, top_ref, c_sem, red_sem, top_sem
+    y_ref, core_ref, w_ref, q_ref, x0_ref, x1_ref, x2_ref, x3_ref, c_hbm, red_hbm, top_hbm, x_ref, red_ref, top_ref, c_sem, red_sem, top_sem
 ):
     rounds, n, k = red_ref.shape
     bands = [pl.ds(at, BAND) for at in range(0, n, BAND)]
@@ -358,7 +363,7 @@
     for copy in arriving:
         copy.start()
     for by, part_ref in enumerate((x0_ref, x1_ref, x2_ref, x3_ref)):
-        x_ref[around(y_ref, by, NY, part_ref.shape[0]), :] = part_ref[...]
+        x_ref[around(y_ref, core_ref, by, part_ref.shape[0]), :] = part_ref[...]
     top = narrow_dot(wide_left(w_ref[...]), wide_right(x_ref[...]))
     for r in range(rounds):
         top_ref[r] = top[:, r * k : (r + 1) * k]
@@ -383,7 +388,7 @@
     reduced, top = (rounds, n, k), (rounds, w, k)
     return pl.pallas_call(
         update_kernel,
-        in_specs=[SCALAR] + [VMEM] * (2 + NY) + [HBM],
+        in_specs=[SCALAR] * 2 + [VMEM] * (2 + NY) + [HBM],
         out_specs=[HBM] * 2,
         out_shape=[jax.ShapeDtypeStruct(reduced, jnp.float32), jax.ShapeDtypeStruct(top, jnp.float32)],
         scratch_shapes=[
@@ -396,7 +401,7 @@
         ],
         compiler_params=params(24),
         name="update",
-    )(index_of("y"), inverse, basis, *cross, columns)
+    )(index_of("y"), index_of("c"), inverse, basis, *cross, columns)
 
 
 def exchange_z(pieces):
@@ -407,12 +412,11 @@
     columns = jnp.transpose(matrix, (1, 0, 2))
     own, columns = columns[0], in_hbm(columns)
     *pieces, panels = products(relay(own), columns)
-    copies, gram = sum_z(exchange_z(sum_y(deal(pieces, "y"))))
+    copies, gram = sum_z(exchange_z(sum_y(deal(pieces))))
     part = exchange_z(copies).reshape(NZ * SUB, RIDE)
-    gram = collect(collect(gram, "x", NX), "y", NY)
-    part, gram = lax.optimization_barrier((part, gram))
-    inverse, basis = factor_last(*factor_first(gram, swap(gram)), in_hbm(panels))
-    reduced, top = update(inverse, basis, every(part, "y", NY), columns)
+    part, gram = lax.optimization_barrier((part, collect(gram)))
+    inverse, basis = factor_last(*factor_first(gram), in_hbm(panels))
+    reduced, top = update(inverse, basis, every(part), columns)
     return jnp.transpose(reduced, (1, 0, 2)), jnp.transpose(top, (1, 0, 2))
 
 

time: 121 us -> 130 us (1.074)
  blocking collectives: 22.4 us -> 54.5 us
  starting transfers between devices: 38.3 us -> 23.7 us
  waiting for transfers between devices: 30.5 us -> 21.2 us
    all_gather x0 -> x3, blocking collectives: none -> 30.7 us  [collect(): values = lax.all_gather(values, axis, tiled=True)]
    ppermute x18 -> x12, starting transfers between devices: 34.3 us -> 19.6 us  [the longest x3 5 us: deal(): lax.ppermute(piece, **turned('y', NY, pairs))]
    ppermute x18 -> x12, waiting for transfers between devices: 24.4 us -> 19.8 us  [the longest x3 13.3 us: deal(): lax.ppermute(piece, **turned('y', NY, pairs))]
    all_to_all x1, waiting for transfers between devices: 3.3 us -> 0.01 us  [exchange_z(): return lax.all_to_all(pieces, 'z', 0, 0)]
    all_to_all x1, blocking collectives: 22.4 us -> 23.8 us  [exchange_z(): return lax.all_to_all(pieces, 'z', 0, 0)]
    ppermute x3 -> x2, waiting for transfers between devices: 2.74 us -> 1.4 us  [swap(): return lax.ppermute(values, 'c', [(0, 1), (1, 0)])]
  transfers between devices with their start and end apart: 22 -> 15, of which waited for: 11 -> 7; matrix products, arithmetic and copies ran while one was open for 0% -> 0% of each run, Pallas kernels for 12% -> 11%
where the time goes in v1:
time: 130 us; the launch traced here: 128 us
  blocking collectives  54.5 us (42%)
  Pallas kernels  25.2 us (19%)
  starting transfers between devices  23.7 us (18%)
  waiting for transfers between devices  21.2 us (16%)
    all_gather x3, blocking collectives, collect(): values = lax.all_gather(values, axis, tiled=True)  30.7 us
    all_to_all x1, blocking collectives, exchange_z(): return lax.all_to_all(pieces, 'z', 0, 0)  23.8 us
    ppermute x3, waiting for transfers between devices, deal(): lax.ppermute(piece, **turned('y', NY, pairs))  13.3 us
    pallas_call x1, Pallas kernels, factor_last(): pl.pallas_call(factor_last_kernel, in_specs=[VMEM] * 3 + [HBM], out_specs...  7.35 us
    pallas_call x1, Pallas kernels, factor_first(): pl.pallas_call(factor_first_kernel, in_specs=[VMEM], out_specs=[VMEM] * 3...  6.51 us
    pallas_call x1, Pallas kernels, update(): pl.pallas_call(update_kernel, in_specs=[SCALAR] * 2 + [VMEM] * (2 + NY) +...  5.52 us
    ppermute x3, starting transfers between devices, deal(): lax.ppermute(piece, **turned('y', NY, pairs))  5 us
    pallas_call x1, Pallas kernels, products(): pl.pallas_call(products_kernel, in_specs=[SCALAR] * 3 + [VMEM] * 4 + [HBM...  4.97 us
  transfers between devices with their start and end apart: 15, of which 7 were waited for; matrix products, arithmetic and copies ran while one was open for 0% of the time, Pallas kernels for 11%

profile of v1, /device:TPU:8, one launch (start us, length us, event | category | flops | bytes accessed | tf_op | source)
XLA Modules:
  0.0 127.7 jit_solution(5398458050237871948)
XLA Ops:
  0.6 1.1 slice_bitcast_fusion
  1.7 4.7 %collective-permute-start.4 = (f32[512,128]{1,0:T(8,128)S(1)}, f32[512,128]{1,0:T(8,128)S(1)}, u32[]{:S(2)}, u32[]{:S(2)}) collective-permute-start(f32[512,128]{1,0:T(8,128)S(1)} %get-tuple-element.36), channel_id=1, source_target_pairs={{0,6},{1,3},{8,14},{9,11},{16,22},{17,19},{24,30},{25,27},{32,38},... | collective-permute-start | bytes 786440 | tf_op jit(solution)/shard_map/ppermute | solution.py:72
  6.4 1.3 %collective-permute-start = (f32[512,128]{1,0:T(8,128)S(1)}, f32[512,128]{1,0:T(8,128)S(1)}, u32[]{:S(2)}, u32[]{:S(2)}) collective-permute-start(f32[512,128]{1,0:T(8,128)S(1)} %get-tuple-element.37), channel_id=1, source_target_pairs={{0,2},{1,7},{8,10},{9,15},{16,18},{17,23},{24,26},{25,31},{32,34},... | collective-permute-start | bytes 786440 | tf_op jit(solution)/shard_map/ppermute | solution.py:71
  7.7 1.3 %collective-permute-start.3 = (f32[512,128]{1,0:T(8,128)S(1)}, f32[512,128]{1,0:T(8,128)S(1)}, u32[]{:S(2)}, u32[]{:S(2)}) collective-permute-start(f32[512,128]{1,0:T(8,128)S(1)} %get-tuple-element.36), channel_id=1, source_target_pairs={{0,2},{1,7},{8,10},{9,15},{16,18},{17,23},{24,26},{25,31},{32,34},... | collective-permute-start | bytes 786440 | tf_op jit(solution)/shard_map/ppermute | solution.py:73
  9.0 1.3 %collective-permute-start.2 = (f32[512,128]{1,0:T(8,128)S(1)}, f32[512,128]{1,0:T(8,128)S(1)}, u32[]{:S(2)}, u32[]{:S(2)}) collective-permute-start(f32[512,128]{1,0:T(8,128)S(1)} %get-tuple-element.37), channel_id=1, source_target_pairs={{0,6},{1,3},{8,14},{9,11},{16,22},{17,19},{24,30},{25,27},{32,38},... | collective-permute-start | bytes 786440 | tf_op jit(solution)/shard_map/ppermute | solution.py:74
  10.3 2.6 %collective-permute-done.4 = f32[512,128]{1,0:T(8,128)S(1)} collective-permute-done((f32[512,128]{1,0:T(8,128)S(1)}, f32[512,128]{1,0:T(8,128)S(1)}, u32[]{:S(2)}, u32[]{:S(2)}) %collective-permute-start.4) | collective-permute-done | bytes 262176 | tf_op jit(solution)/shard_map/ppermute | solution.py:72
  13.0 0.7 collective-permute-start.5
  13.6 0.0 collective-permute-done
  13.7 0.7 collective-permute-start.1
  14.4 2.8 %collective-permute-done.3 = f32[512,128]{1,0:T(8,128)S(1)} collective-permute-done((f32[512,128]{1,0:T(8,128)S(1)}, f32[512,128]{1,0:T(8,128)S(1)}, u32[]{:S(2)}, u32[]{:S(2)}) %collective-permute-start.3) | collective-permute-done | bytes 262176 | tf_op jit(solution)/shard_map/ppermute | solution.py:73
  17.2 1.0 collective-permute-done.2
  18.2 0.0 collective-permute-done.5
  18.2 0.0 collective-permute-done.1
  18.2 1.1 select_select_fusion
  19.4 0.1 collective-permute-start.7
  19.5 0.5 collective-permute-start.6
  20.0 1.0 collective-permute-done.7.oh_ref
  21.0 0.4 collective-permute-done.6.ol_ref
  21.4 5.0 %products.1 = (f32[64,1408]{1,0:T(8,128)S(1)}, f32[64,1408]{1,0:T(8,128)S(1)}, f32[64,1408]{1,0:T(8,128)S(1)}, f32[64,1408]{1,0:T(8,128)S(1)}, f32[1024,256]{1,0:T(8,128)S(1)}) custom-call(s32[1]{0:T(128)} %bitcast.2.x_ref, s32[1]{0:T(128)} %bitcast.y_ref, s32[1]{0:T(128)} %bitcast.1.core_ref, f32[512,128]{1,0:T(8,128)S(1)} %get-tuple-element.35.ml_ref, ...), custom_call_target="tpu_custom_call" | custom-call | tf_op jit(solution)/shard_map/products/pallas_call | solution.py:145
  26.3 0.0 copy-start
  26.3 1.7 %collective-permute-start.8 = (f32[64,1408]{1,0:T(8,128)S(1)}, f32[64,1408]{1,0:T(8,128)S(1)}, u32[]{:S(2)}, u32[]{:S(2)}) collective-permute-start(f32[64,1408]{1,0:T(8,128)S(1)} %get-tuple-element.19), channel_id=1, source_target_pairs={{0,8},{1,25},{8,16},{25,17},{16,24},{17,9},{24,0},{9,1},{2,10},{3,... | collective-permute-start | bytes 1081352 | tf_op jit(solution)/shard_map/ppermute | solution.py:207
  28.0 1.0 collective-permute-start.9
  29.0 2.4 %collective-permute-start.10 = (f32[64,1408]{1,0:T(8,128)S(1)}, f32[64,1408]{1,0:T(8,128)S(1)}, u32[]{:S(2)}, u32[]{:S(2)}) collective-permute-start(f32[64,1408]{1,0:T(8,128)S(1)} %get-tuple-element.21), channel_id=1, source_target_pairs={{0,24},{1,9},{8,0},{25,1},{16,8},{17,25},{24,16},{9,17},{2,26},{3,... | collective-permute-start | bytes 1081352 | tf_op jit(solution)/shard_map/ppermute | solution.py:207
  31.4 10.8 %collective-permute-done.8.a1_ref = f32[64,1408]{1,0:T(8,128)S(1)} collective-permute-done((f32[64,1408]{1,0:T(8,128)S(1)}, f32[64,1408]{1,0:T(8,128)S(1)}, u32[]{:S(2)}, u32[]{:S(2)}) %collective-permute-start.8) | collective-permute-done | bytes 360480 | tf_op jit(solution)/shard_map/ppermute | solution.py:207
  42.2 0.0 collective-permute-done.9.a2_ref
  42.2 2.4 %collective-permute-done.10.a3_ref = f32[64,1408]{1,0:T(8,128)S(1)} collective-permute-done((f32[64,1408]{1,0:T(8,128)S(1)}, f32[64,1408]{1,0:T(8,128)S(1)}, u32[]{:S(2)}, u32[]{:S(2)}) %collective-permute-start.10) | collective-permute-done | bytes 360480 | tf_op jit(solution)/shard_map/ppermute | solution.py:207
  44.6 0.1 sum_y.1
  44.7 23.8 %all_to_all.10.a_ref = f32[8,8,1536]{2,1,0:T(8,128)S(1)} all-to-all(f32[8,8,1536]{2,1,0:T(8,128)S(1)} %sum_y.1), channel_id=1, replica_groups=mesh['z'=8,'y'=4,'x'=4,'c'=2] {'z'}, dimensions={0} | all-to-all | bytes 786432 | tf_op jit(solution)/shard_map/all_to_all | solution.py:408
  68.4 0.8 sum_z.1
  69.2 0.0 copy-done
  69.2 3.4 %all-to-all-start.1 = ((f32[8,8,1280]{2,1,0:T(8,128)}), f32[8,8,1280]{2,1,0:T(8,128)S(1)}, u32[]{:S(2)}, u32[]{:S(2)}) async-start(f32[8,8,1280]{2,1,0:T(8,128)} %get-tuple-element.22), calls=%async_computation.1 | async-start | bytes 655360 | tf_op jit(solution)/shard_map/all_to_all | solution.py:408
  72.6 16.2 %all_gather.9 = f32[32,256]{1,0:T(8,128)S(1)} all-gather(f32[8,256]{1,0:T(8,128)S(1)} %get-tuple-element.23), channel_id=1, replica_groups=mesh['z'=8,'y'=4,'x'=4,'c'=2] {'x'}, dimensions={0}, use_global_device_ids=true | all-gather | bytes 40960 | tf_op jit(solution)/shard_map/all_gather | solution.py:217
  88.9 12.5 %all_gather.10 = f32[128,256]{1,0:T(8,128)S(1)} all-gather(f32[32,256]{1,0:T(8,128)S(1)} %all_gather.9), channel_id=1, replica_groups=mesh['z'=8,'y'=4,'x'=4,'c'=2] {'y'}, dimensions={0}, use_global_device_ids=true | all-gather | bytes 163840 | tf_op jit(solution)/shard_map/all_gather | solution.py:217
  101.4 2.0 %all_gather.11.p_ref = f32[256,256]{1,0:T(8,128)S(1)} all-gather(f32[128,256]{1,0:T(8,128)S(1)} %all_gather.10), channel_id=1, replica_groups=mesh['z'=8,'y'=4,'x'=4,'c'=2] {'c'}, dimensions={0}, use_global_device_ids=true | all-gather | bytes 393216 | tf_op jit(solution)/shard_map/all_gather | solution.py:217
  103.4 0.0 all-to-all-done.1
  103.4 0.5 collective-permute-start.13
  103.9 2.7 %collective-permute-start.12 = (f32[64,1280]{1,0:T(8,128)S(1)}, f32[64,1280]{1,0:T(8,128)S(1)}, u32[]{:S(2)}, u32[]{:S(2)}) collective-permute-start(f32[64,1280]{1,0:T(8,128)S(1)} %bitcast.16), channel_id=1, source_target_pairs={{0,16},{1,17},{8,24},{25,9},{16,0},{17,1},{24,8},{9,25},{2,18},{3,... | collective-permute-start | bytes 983048 | tf_op jit(solution)/shard_map/ppermute | solution.py:212
  106.6 1.5 %collective-permute-start.11 = (f32[64,1280]{1,0:T(8,128)S(1)}, f32[64,1280]{1,0:T(8,128)S(1)}, u32[]{:S(2)}, u32[]{:S(2)}) collective-permute-start(f32[64,1280]{1,0:T(8,128)S(1)} %bitcast.17), channel_id=1, source_target_pairs={{0,24},{1,9},{8,0},{25,1},{16,8},{17,25},{24,16},{9,17},{2,26},{3,... | collective-permute-start | bytes 983048 | tf_op jit(solution)/shard_map/ppermute | solution.py:212
  108.1 6.5 %factor_first.1 = (f32[128,128]{1,0:T(8,128)S(1)}, f32[128,128]{1,0:T(8,128)S(1)}, f32[128,128]{1,0:T(8,128)S(1)}) custom-call(f32[256,256]{1,0:T(8,128)S(1)} %all_gather.11.p_ref), custom_call_target="tpu_custom_call" | custom-call | tf_op jit(solution)/shard_map/factor_first/pallas_call | solution.py:328
  114.6 7.3 %factor_last.1 = (f32[256,256]{1,0:T(8,128)S(1)}, bf16[1024,768]{1,0:T(8,128)(2,1)S(1)}) custom-call(f32[128,128]{1,0:T(8,128)S(1)} %get-tuple-element.25.w11_ref, f32[128,128]{1,0:T(8,128)S(1)} %get-tuple-element.26.l_ref, f32[128,128]{1,0:T(8,128)S(1)} %get-tuple-element.27.s_ref, f32[1024,256]{1,0:T(8,128)} %copy-done), custom_call_target="tpu_custom_call" | custom-call | tf_op jit(solution)/shard_map/factor_last/pallas_call | solution.py:341
  121.9 0.0 collective-permute-done.13.x3_ref
  122.0 0.0 collective-permute-done.12.x2_ref
  122.0 0.0 collective-permute-done.11.x1_ref
  122.0 5.5 %update.1 = (f32[10,1024,128]{2,1,0:T(8,128)}, f32[10,256,128]{2,1,0:T(8,128)}) custom-call(s32[1]{0:T(128)} %bitcast.y_ref, s32[1]{0:T(128)} %bitcast.1.core_ref, f32[256,256]{1,0:T(8,128)S(1)} %get-tuple-element.29.w_ref, bf16[1024,768]{1,0:T(8,128)(2,1)S(1)} %get-tuple-element.30.q_ref, f32[64,1280]{1,0:T(8,128)S(1)} %bitcast.18, ...), custom_call_target="tpu_custom_call" | custom-call | tf_op jit(solution)/shard_map/update/pallas_call | solution.py:389
Async XLA Ops:
  1.7 11.3 %collective-permute-start.4 = (f32[512,128]{1,0:T(8,128)S(1)}, f32[512,128]{1,0:T(8,128)S(1)}, u32[]{:S(2)}, u32[]{:S(2)}) collective-permute-start(f32[512,128]{1,0:T(8,128)S(1)} %get-tuple-element.36), channel_id=1, source_target_pairs={{0,6},{1,3},{8,14},{9,11},{16,22},{17,19},{24,30},{25,27},{32,38},... | collective-permute-start | bytes 786440 | tf_op jit(solution)/shard_map/ppermute | solution.py:72
  6.4 7.3 %collective-permute-start = (f32[512,128]{1,0:T(8,128)S(1)}, f32[512,128]{1,0:T(8,128)S(1)}, u32[]{:S(2)}, u32[]{:S(2)}) collective-permute-start(f32[512,128]{1,0:T(8,128)S(1)} %get-tuple-element.37), channel_id=1, source_target_pairs={{0,2},{1,7},{8,10},{9,15},{16,18},{17,23},{24,26},{25,31},{32,34},... | collective-permute-start | bytes 786440 | tf_op jit(solution)/shard_map/ppermute | solution.py:71
  7.7 9.5 %collective-permute-start.3 = (f32[512,128]{1,0:T(8,128)S(1)}, f32[512,128]{1,0:T(8,128)S(1)}, u32[]{:S(2)}, u32[]{:S(2)}) collective-permute-start(f32[512,128]{1,0:T(8,128)S(1)} %get-tuple-element.36), channel_id=1, source_target_pairs={{0,2},{1,7},{8,10},{9,15},{16,18},{17,23},{24,26},{25,31},{32,34},... | collective-permute-start | bytes 786440 | tf_op jit(solution)/shard_map/ppermute | solution.py:73
  9.0 9.2 %collective-permute-start.2 = (f32[512,128]{1,0:T(8,128)S(1)}, f32[512,128]{1,0:T(8,128)S(1)}, u32[]{:S(2)}, u32[]{:S(2)}) collective-permute-start(f32[512,128]{1,0:T(8,128)S(1)} %get-tuple-element.37), channel_id=1, source_target_pairs={{0,6},{1,3},{8,14},{9,11},{16,22},{17,19},{24,30},{25,27},{32,38},... | collective-permute-start | bytes 786440 | tf_op jit(solution)/shard_map/ppermute | solution.py:74
  13.0 5.2 %collective-permute-start.5 = (f32[512,128]{1,0:T(8,128)S(1)}, f32[512,128]{1,0:T(8,128)S(1)}, u32[]{:S(2)}, u32[]{:S(2)}) collective-permute-start(f32[512,128]{1,0:T(8,128)S(1)} %collective-permute-done.4), channel_id=1, source_target_pairs={{6,4},{3,5},{14,12},{11,13},{22,20},{19,21},{30,28},{27,29},{38,36... | collective-permute-start | bytes 786440 | tf_op jit(solution)/shard_map/ppermute | solution.py:76
  13.7 4.6 %collective-permute-start.1 = (f32[512,128]{1,0:T(8,128)S(1)}, f32[512,128]{1,0:T(8,128)S(1)}, u32[]{:S(2)}, u32[]{:S(2)}) collective-permute-start(f32[512,128]{1,0:T(8,128)S(1)} %collective-permute-done), channel_id=1, source_target_pairs={{2,4},{7,5},{10,12},{15,13},{18,20},{23,21},{26,28},{31,29},{34,36... | collective-permute-start | bytes 786440 | tf_op jit(solution)/shard_map/ppermute | solution.py:75
  19.4 1.6 %collective-permute-start.7 = (f32[512,128]{1,0:T(8,128)S(1)}, f32[512,128]{1,0:T(8,128)S(1)}, u32[]{:S(2)}, u32[]{:S(2)}) collective-permute-start(f32[512,128]{1,0:T(8,128)S(1)} %get-tuple-element.34.mh_ref), channel_id=1, source_target_pairs={{0,1},{1,0},{2,3},{3,2},{4,5},{5,4},{6,7},{7,6},{8,9},{9,8},{10,11... | collective-permute-start | bytes 786440 | tf_op jit(solution)/shard_map/ppermute | solution.py:56
  19.5 1.9 %collective-permute-start.6 = (f32[512,128]{1,0:T(8,128)S(1)}, f32[512,128]{1,0:T(8,128)S(1)}, u32[]{:S(2)}, u32[]{:S(2)}) collective-permute-start(f32[512,128]{1,0:T(8,128)S(1)} %get-tuple-element.35.ml_ref), channel_id=1, source_target_pairs={{0,1},{1,0},{2,3},{3,2},{4,5},{5,4},{6,7},{7,6},{8,9},{9,8},{10,11... | collective-permute-start | bytes 786440 | tf_op jit(solution)/shard_map/ppermute | solution.py:56
  26.3 42.9 %copy-start = (f32[1024,256]{1,0:T(8,128)}, f32[1024,256]{1,0:T(8,128)S(1)}, u32[]{:S(2)}) copy-start(f32[1024,256]{1,0:T(8,128)S(1)} %get-tuple-element.28.p_hbm) | copy-start | bytes 3145732
  26.3 15.8 %collective-permute-start.8 = (f32[64,1408]{1,0:T(8,128)S(1)}, f32[64,1408]{1,0:T(8,128)S(1)}, u32[]{:S(2)}, u32[]{:S(2)}) collective-permute-start(f32[64,1408]{1,0:T(8,128)S(1)} %get-tuple-element.19), channel_id=1, source_target_pairs={{0,8},{1,25},{8,16},{25,17},{16,24},{17,9},{24,0},{9,1},{2,10},{3,... | collective-permute-start | bytes 1081352 | tf_op jit(solution)/shard_map/ppermute | solution.py:207
  28.0 14.2 %collective-permute-start.9 = (f32[64,1408]{1,0:T(8,128)S(1)}, f32[64,1408]{1,0:T(8,128)S(1)}, u32[]{:S(2)}, u32[]{:S(2)}) collective-permute-start(f32[64,1408]{1,0:T(8,128)S(1)} %get-tuple-element.20), channel_id=1, source_target_pairs={{0,16},{1,17},{8,24},{25,9},{16,0},{17,1},{24,8},{9,25},{2,18},{3,... | collective-permute-start | bytes 1081352 | tf_op jit(solution)/shard_map/ppermute | solution.py:207
  29.0 15.6 %collective-permute-start.10 = (f32[64,1408]{1,0:T(8,128)S(1)}, f32[64,1408]{1,0:T(8,128)S(1)}, u32[]{:S(2)}, u32[]{:S(2)}) collective-permute-start(f32[64,1408]{1,0:T(8,128)S(1)} %get-tuple-element.21), channel_id=1, source_target_pairs={{0,24},{1,9},{8,0},{25,1},{16,8},{17,25},{24,16},{9,17},{2,26},{3,... | collective-permute-start | bytes 1081352 | tf_op jit(solution)/shard_map/ppermute | solution.py:207
  69.2 34.2 %all-to-all-start.1 = ((f32[8,8,1280]{2,1,0:T(8,128)}), f32[8,8,1280]{2,1,0:T(8,128)S(1)}, u32[]{:S(2)}, u32[]{:S(2)}) async-start(f32[8,8,1280]{2,1,0:T(8,128)} %get-tuple-element.22), calls=%async_computation.1 | async-start | bytes 655360 | tf_op jit(solution)/shard_map/all_to_all | solution.py:408
  103.4 18.6 %collective-permute-start.13 = (f32[64,1280]{1,0:T(8,128)S(1)}, f32[64,1280]{1,0:T(8,128)S(1)}, u32[]{:S(2)}, u32[]{:S(2)}) collective-permute-start(f32[64,1280]{1,0:T(8,128)S(1)} %bitcast.15), channel_id=1, source_target_pairs={{0,8},{1,25},{8,16},{25,17},{16,24},{17,9},{24,0},{9,1},{2,10},{3,... | collective-permute-start | bytes 983048 | tf_op jit(solution)/shard_map/ppermute | solution.py:212
  103.9 18.1 %collective-permute-start.12 = (f32[64,1280]{1,0:T(8,128)S(1)}, f32[64,1280]{1,0:T(8,128)S(1)}, u32[]{:S(2)}, u32[]{:S(2)}) collective-permute-start(f32[64,1280]{1,0:T(8,128)S(1)} %bitcast.16), channel_id=1, source_target_pairs={{0,16},{1,17},{8,24},{25,9},{16,0},{17,1},{24,8},{9,25},{2,18},{3,... | collective-permute-start | bytes 983048 | tf_op jit(solution)/shard_map/ppermute | solution.py:212
  106.6 15.4 %collective-permute-start.11 = (f32[64,1280]{1,0:T(8,128)S(1)}, f32[64,1280]{1,0:T(8,128)S(1)}, u32[]{:S(2)}, u32[]{:S(2)}) collective-permute-start(f32[64,1280]{1,0:T(8,128)S(1)} %bitcast.17), channel_id=1, source_target_pairs={{0,24},{1,9},{8,0},{25,1},{16,8},{17,25},{24,16},{9,17},{2,26},{3,... | collective-permute-start | bytes 983048 | tf_op jit(solution)/shard_map/ppermute | solution.py:212

commit v2 on v0

--- a/solution.py
+++ b/solution.py
@@ -216,74 +216,86 @@
     return y * (1.5 - 0.5 * d * y * y)
 
 
+def sum4(left, right):
+    return (left[0] * right[0] + left[1] * right[1]) + (left[2] * right[2] + left[3] * right[3])
+
+
+class Pivot:
+    def __init__(self, d):
+        det = 1.0 / (d[0][0] * d[1][1] - d[1][0] * d[1][0])
+        self.p = p00, p01, p11 = d[1][1] * det, -d[1][0] * det, d[0][0] * det
+        self.z = z = [[d[r][0] * p00 + d[r][1] * p01, d[r][0] * p01 + d[r][1] * p11] for r in (2, 3)]
+        s00 = d[2][2] - (z[0][0] * d[2][0] + z[0][1] * d[2][1])
+        s01 = d[3][2] - (z[1][0] * d[2][0] + z[1][1] * d[2][1])
+        s11 = d[3][3] - (z[1][0] * d[3][0] + z[1][1] * d[3][1])
+        sdet = 1.0 / (s00 * s11 - s01 * s01)
+        self.i = s11 * sdet, -s01 * sdet, s00 * sdet
+        self.d, self.s = d, (s00, s01, s11)
+
+    def lower(self, r):
+        z = self.z
+        return [r[2 + at] - (z[at][0] * r[0] + z[at][1] * r[1]) for at in range(2)]
+
+    def solve(self, r):
+        (p00, p01, p11), (i00, i01, i11), z = self.p, self.i, self.z
+        v2, v3 = self.lower(r)
+        y2, y3 = i00 * v2 + i01 * v3, i01 * v2 + i11 * v3
+        u0, u1 = p00 * r[0] + p01 * r[1], p01 * r[0] + p11 * r[1]
+        return [u0 - (z[0][0] * y2 + z[1][0] * y3), u1 - (z[0][1] * y2 + z[1][1] * y3), y2, y3]
+
+    def rows(self, r):
+        d, (s00, s01, s11) = self.d, self.s
+        k0 = inverse_root(d[0][0])
+        l10 = d[1][0] * k0
+        w0 = k0 * r[0]
+        w1 = inverse_root(d[1][1] - l10 * l10) * (r[1] - l10 * w0)
+        k2 = inverse_root(s00)
+        l32 = s01 * k2
+        v2, v3 = self.lower(r)
+        w2 = k2 * v2
+        return [w0, w1, w2, inverse_root(s11 - l32 * l32) * (v3 - l32 * w2)]
+
+
 def invert_factor(block, w_ref, row0, col0):
     n = LANES
     tiles = n // SUB
-    a = [block[SUB * t:SUB * (t + 1)] for t in range(tiles)]
+    a = [block[SUB * t : SUB * (t + 1)] for t in range(tiles)]
     lane = lax.broadcasted_iota(jnp.int32, (SUB, LANES), 1)
     sub = lax.broadcasted_iota(jnp.int32, (SUB, LANES), 0)
     b = [jnp.where(lane == sub + SUB * t, 1.0, 0.0).astype(jnp.float32) for t in range(tiles)]
 
     def across(v, j):
-        return jnp.broadcast_to(v[:, j:j + 1], (SUB, LANES))
+        return jnp.broadcast_to(v[:, j : j + 1], (SUB, LANES))
 
     def down(v, s):
-        return jnp.broadcast_to(v[s:s + 1, :], (SUB, LANES))
-
-    for q in range(n // 4):
-        t, s, j = q // 2, (q % 2) * 4, 4 * q
-        ra = [down(a[t], s + k) for k in range(4)]
-        rb = [down(b[t], s + k) for k in range(4)]
-        d = {}
+        return jnp.broadcast_to(v[s : s + 1, :], (SUB, LANES))
+
+    for t in range(tiles):
+        j = SUB * t
+        columns = [across(a[t], j + k) for k in range(SUB)]
+        d = [[down(columns[y], x) for y in range(SUB)] for x in range(SUB)]
+        ra = [down(a[t], k) for k in range(SUB)]
+        rb = [down(b[t], k) for k in range(SUB)]
+        head = Pivot([row[:4] for row in d[:4]])
+        g = [head.solve([d[y][k] for k in range(4)]) for y in range(4, SUB)]
+        rest = [[None] * 4 for _ in range(4)]
         for x in range(4):
             for y in range(x + 1):
-                d[x, y] = across(ra[y], j + x)
-                d[y, x] = d[x, y]
-        det = 1.0 / (d[0, 0] * d[1, 1] - d[1, 0] * d[1, 0])
-        p00, p01, p11 = d[1, 1] * det, -d[1, 0] * det, d[0, 0] * det
-        z = [[d[r, 0] * p00 + d[r, 1] * p01, d[r, 0] * p01 + d[r, 1] * p11] for r in (2, 3)]
-        s00 = d[2, 2] - (z[0][0] * d[2, 0] + z[0][1] * d[2, 1])
-        s01 = d[3, 2] - (z[1][0] * d[2, 0] + z[1][1] * d[2, 1])
-        s11 = d[3, 3] - (z[1][0] * d[3, 0] + z[1][1] * d[3, 1])
-        sdet = 1.0 / (s00 * s11 - s01 * s01)
-        i00, i01, i11 = s11 * sdet, -s01 * sdet, s00 * sdet
-
-        def solve(r):
-            u0 = p00 * r[0] + p01 * r[1]
-            u1 = p01 * r[0] + p11 * r[1]
-            v2 = r[2] - (z[0][0] * r[0] + z[0][1] * r[1])
-            v3 = r[3] - (z[1][0] * r[0] + z[1][1] * r[1])
-            y2 = i00 * v2 + i01 * v3
-            y3 = i01 * v2 + i11 * v3
-            return [u0 - (z[0][0] * y2 + z[1][0] * y3), u1 - (z[0][1] * y2 + z[1][1] * y3), y2, y3]
-
-        ya, yb = solve(ra), solve(rb)
-        for u in range(t, tiles):
-            if u == t and s == 4:
-                continue
-            c = [across(a[u], j + k) for k in range(4)]
-            na, nb = a[u], b[u]
-            fa = (c[0] * ya[0] + c[1] * ya[1]) + (c[2] * ya[2] + c[3] * ya[3])
-            fb = (c[0] * yb[0] + c[1] * yb[1]) + (c[2] * yb[2] + c[3] * yb[3])
-            if u == t:
-                a[u] = jnp.where(sub >= 4, na - fa, na)
-                b[u] = jnp.where(sub >= 4, nb - fb, nb)
-            else:
-                a[u], b[u] = na - fa, nb - fb
-        k0 = inverse_root(d[0, 0])
-        l10 = d[1, 0] * k0
-        k1 = inverse_root(d[1, 1] - l10 * l10)
-        w0 = k0 * rb[0]
-        w1 = k1 * (rb[1] - l10 * w0)
-        k2 = inverse_root(s00)
-        l32 = s01 * k2
-        k3 = inverse_root(s11 - l32 * l32)
-        v2 = rb[2] - (z[0][0] * rb[0] + z[0][1] * rb[1])
-        v3 = rb[3] - (z[1][0] * rb[0] + z[1][1] * rb[1])
-        w2 = k2 * v2
-        w3 = k3 * (v3 - l32 * w2)
-        for k, w in enumerate((w0, w1, w2, w3)):
-            w_ref[row0 + j + k:row0 + j + k + 1, col0:col0 + LANES] = w[0:1]
+                rest[x][y] = rest[y][x] = d[4 + x][4 + y] - sum4(d[4 + x][:4], g[y])
+        tail = Pivot(rest)
+        za, zb, low_b = [], [], None
+        for r, z in ((ra, za), (rb, zb)):
+            low = [r[4 + x] - sum4(g[x], r[:4]) for x in range(4)]
+            y1, y2 = head.solve(r[:4]), tail.solve(low)
+            z += [y1[k] - sum4([g[x][k] for x in range(4)], y2) for k in range(4)] + y2
+            low_b = low
+        for u in range(t + 1, tiles):
+            c = [across(a[u], j + k) for k in range(SUB)]
+            a[u], b[u] = (
+                v - (sum4(c[:4], z[:4]) + sum4(c[4:], z[4:])) for v, z in ((a[u], za), (b[u], zb))
+            )
+        for k, w in enumerate(head.rows(rb[:4]) + tail.rows(low_b)):
+            w_ref[row0 + j + k : row0 + j + k + 1, col0 : col0 + LANES] = w[0:1]
 
 
 def factor_first_kernel(x_ref, y_ref, core_ref, mine_ref, other_ref, w_ref, l_ref, s_ref, g_ref):

time: 121 us -> 119 us (0.983)
  Pallas kernels: 25.2 us -> 23.4 us
  transfers between devices with their start and end apart: 22 -> 22, of which waited for: 11 -> 11; matrix products, arithmetic and copies ran while one was open for 0% -> 0% of each run, Pallas kernels for 12% -> 10%
where the time goes in v2:
time: 119 us; the launch traced here: 118 us
  starting transfers between devices  38.3 us (32%)
  waiting for transfers between devices  30.5 us (26%)
  Pallas kernels  23.4 us (20%)
  blocking collectives  22.4 us (19%)
    all_to_all x1, blocking collectives, exchange_z(): return lax.all_to_all(pieces, 'z', 0, 0)  22.4 us
    ppermute x9, starting transfers between devices, every(): lax.ppermute(values, axis, [(at, (at - by) % size) for at in range(size)])  19.3 us
    ppermute x3, waiting for transfers between devices, deal(): lax.ppermute(pieces[by], axis, [(at, (at + by) % size) for at in range(si...  15.4 us
    pallas_call x1, Pallas kernels, factor_last(): pl.pallas_call(factor_last_kernel, in_specs=[VMEM] * 3 + [HBM], out_specs...  6.52 us
    pallas_call x1, Pallas kernels, factor_first(): pl.pallas_call(factor_first_kernel, in_specs=[SCALAR] * 3 + [VMEM] * 2, o...  5.56 us
    pallas_call x1, Pallas kernels, update(): pl.pallas_call(update_kernel, in_specs=[SCALAR] + [VMEM] * (2 + NY) + [HB...  5.52 us
    ppermute x3, starting transfers between devices, deal(): lax.ppermute(pieces[by], axis, [(at, (at + by) % size) for at in range(si...  5 us
    pallas_call x1, Pallas kernels, products(): pl.pallas_call(products_kernel, in_specs=[SCALAR] * 3 + [VMEM] * 4 + [HBM...  4.97 us
  transfers between devices with their start and end apart: 22, of which 11 were waited for; matrix products, arithmetic and copies ran while one was open for 0% of the time, Pallas kernels for 10%

profile of v2, /device:TPU:8, one launch (start us, length us, event | category | flops | bytes accessed | tf_op | source)
XLA Modules:
  0.0 117.8 jit_solution(11090321050249142486)
XLA Ops:
  0.6 1.1 slice_bitcast_fusion
  1.7 4.7 %collective-permute-start.4 = (f32[512,128]{1,0:T(8,128)S(1)}, f32[512,128]{1,0:T(8,128)S(1)}, u32[]{:S(2)}, u32[]{:S(2)}) collective-permute-start(f32[512,128]{1,0:T(8,128)S(1)} %get-tuple-element.36), channel_id=1, source_target_pairs={{0,6},{1,7},{8,14},{9,15},{16,22},{17,23},{24,30},{25,31},{32,38},... | collective-permute-start | bytes 786440 | tf_op jit(solution)/shard_map/ppermute | solution.py:64
  6.4 1.3 %collective-permute-start = (f32[512,128]{1,0:T(8,128)S(1)}, f32[512,128]{1,0:T(8,128)S(1)}, u32[]{:S(2)}, u32[]{:S(2)}) collective-permute-start(f32[512,128]{1,0:T(8,128)S(1)} %get-tuple-element.37), channel_id=1, source_target_pairs={{0,2},{1,3},{8,10},{9,11},{16,18},{17,19},{24,26},{25,27},{32,34},... | collective-permute-start | bytes 786440 | tf_op jit(solution)/shard_map/ppermute | solution.py:63
  7.7 1.3 %collective-permute-start.3 = (f32[512,128]{1,0:T(8,128)S(1)}, f32[512,128]{1,0:T(8,128)S(1)}, u32[]{:S(2)}, u32[]{:S(2)}) collective-permute-start(f32[512,128]{1,0:T(8,128)S(1)} %get-tuple-element.36), channel_id=1, source_target_pairs={{0,2},{1,3},{8,10},{9,11},{16,18},{17,19},{24,26},{25,27},{32,34},... | collective-permute-start | bytes 786440 | tf_op jit(solution)/shard_map/ppermute | solution.py:65
  9.0 1.3 %collective-permute-start.2 = (f32[512,128]{1,0:T(8,128)S(1)}, f32[512,128]{1,0:T(8,128)S(1)}, u32[]{:S(2)}, u32[]{:S(2)}) collective-permute-start(f32[512,128]{1,0:T(8,128)S(1)} %get-tuple-element.37), channel_id=1, source_target_pairs={{0,6},{1,7},{8,14},{9,15},{16,22},{17,23},{24,30},{25,31},{32,38},... | collective-permute-start | bytes 786440 | tf_op jit(solution)/shard_map/ppermute | solution.py:66
  10.3 2.7 %collective-permute-done.4 = f32[512,128]{1,0:T(8,128)S(1)} collective-permute-done((f32[512,128]{1,0:T(8,128)S(1)}, f32[512,128]{1,0:T(8,128)S(1)}, u32[]{:S(2)}, u32[]{:S(2)}) %collective-permute-start.4) | collective-permute-done | bytes 262176 | tf_op jit(solution)/shard_map/ppermute | solution.py:64
  13.1 0.7 collective-permute-start.5
  13.7 0.6 collective-permute-done
  14.4 0.7 collective-permute-start.1
  15.1 3.8 %collective-permute-done.3 = f32[512,128]{1,0:T(8,128)S(1)} collective-permute-done((f32[512,128]{1,0:T(8,128)S(1)}, f32[512,128]{1,0:T(8,128)S(1)}, u32[]{:S(2)}, u32[]{:S(2)}) %collective-permute-start.3) | collective-permute-done | bytes 262176 | tf_op jit(solution)/shard_map/ppermute | solution.py:65
  18.8 0.0 collective-permute-done.2
  18.9 0.0 collective-permute-done.5
  18.9 0.0 collective-permute-done.1
  18.9 1.1 select_select_fusion
  20.0 0.1 collective-permute-start.7
  20.1 0.5 collective-permute-start.6
  20.6 1.0 collective-permute-done.7.oh_ref
  21.6 0.4 collective-permute-done.6.ol_ref
  22.0 5.0 %products.1 = (f32[64,1408]{1,0:T(8,128)S(1)}, f32[64,1408]{1,0:T(8,128)S(1)}, f32[64,1408]{1,0:T(8,128)S(1)}, f32[64,1408]{1,0:T(8,128)S(1)}, f32[1024,256]{1,0:T(8,128)S(1)}) custom-call(s32[1]{0:T(128)} %bitcast.1.x_ref, s32[1]{0:T(128)} %bitcast.y_ref, s32[1]{0:T(128)} %bitcast.2.core_ref, f32[512,128]{1,0:T(8,128)S(1)} %get-tuple-element.35.ml_ref, ...), custom_call_target="tpu_custom_call" | custom-call | tf_op jit(solution)/shard_map/products/pallas_call | solution.py:137
  27.0 0.0 copy-start
  27.0 1.7 %collective-permute-start.8 = (f32[64,1408]{1,0:T(8,128)S(1)}, f32[64,1408]{1,0:T(8,128)S(1)}, u32[]{:S(2)}, u32[]{:S(2)}) collective-permute-start(f32[64,1408]{1,0:T(8,128)S(1)} %get-tuple-element.19), channel_id=1, source_target_pairs={{0,8},{8,16},{16,24},{24,0},{1,9},{9,17},{17,25},{25,1},{2,10},{10... | collective-permute-start | bytes 1081352 | tf_op jit(solution)/shard_map/ppermute | solution.py:200
  28.6 0.9 collective-permute-start.9
  29.6 2.4 %collective-permute-start.10 = (f32[64,1408]{1,0:T(8,128)S(1)}, f32[64,1408]{1,0:T(8,128)S(1)}, u32[]{:S(2)}, u32[]{:S(2)}) collective-permute-start(f32[64,1408]{1,0:T(8,128)S(1)} %get-tuple-element.21), channel_id=1, source_target_pairs={{0,24},{8,0},{16,8},{24,16},{1,25},{9,1},{17,9},{25,17},{2,26},{10... | collective-permute-start | bytes 1081352 | tf_op jit(solution)/shard_map/ppermute | solution.py:200
  32.0 6.3 %collective-permute-done.8.a1_ref = f32[64,1408]{1,0:T(8,128)S(1)} collective-permute-done((f32[64,1408]{1,0:T(8,128)S(1)}, f32[64,1408]{1,0:T(8,128)S(1)}, u32[]{:S(2)}, u32[]{:S(2)}) %collective-permute-start.8) | collective-permute-done | bytes 360480 | tf_op jit(solution)/shard_map/ppermute | solution.py:200
  38.3 3.1 %collective-permute-done.9.a2_ref = f32[64,1408]{1,0:T(8,128)S(1)} collective-permute-done((f32[64,1408]{1,0:T(8,128)S(1)}, f32[64,1408]{1,0:T(8,128)S(1)}, u32[]{:S(2)}, u32[]{:S(2)}) %collective-permute-start.9) | collective-permute-done | bytes 360480 | tf_op jit(solution)/shard_map/ppermute | solution.py:200
  41.4 5.9 %collective-permute-done.10.a3_ref = f32[64,1408]{1,0:T(8,128)S(1)} collective-permute-done((f32[64,1408]{1,0:T(8,128)S(1)}, f32[64,1408]{1,0:T(8,128)S(1)}, u32[]{:S(2)}, u32[]{:S(2)}) %collective-permute-start.10) | collective-permute-done | bytes 360480 | tf_op jit(solution)/shard_map/ppermute | solution.py:200
  47.4 0.1 sum_y.1
  47.4 22.4 %all_to_all.10.a_ref = f32[8,8,1536]{2,1,0:T(8,128)S(1)} all-to-all(f32[8,8,1536]{2,1,0:T(8,128)S(1)} %sum_y.1), channel_id=1, replica_groups=mesh['z'=8,'y'=4,'x'=4,'c'=2] {'z'}, dimensions={0} | all-to-all | bytes 786432 | tf_op jit(solution)/shard_map/all_to_all | solution.py:415
  69.8 0.8 sum_z.1
  70.6 0.0 copy-done
  70.6 3.2 %collective-permute-start.13 = (f32[8,256]{1,0:T(8,128)S(1)}, f32[8,256]{1,0:T(8,128)S(1)}, u32[]{:S(2)}, u32[]{:S(2)}) collective-permute-start(f32[8,256]{1,0:T(8,128)S(1)} %get-tuple-element.23), channel_id=1, source_target_pairs={{0,2},{2,4},{4,6},{6,0},{1,3},{3,5},{5,7},{7,1},{8,10},{10,12},{12... | collective-permute-start | bytes 24584 | tf_op jit(solution)/shard_map/ppermute | solution.py:206
  73.7 2.5 %collective-permute-start.12 = (f32[8,256]{1,0:T(8,128)S(1)}, f32[8,256]{1,0:T(8,128)S(1)}, u32[]{:S(2)}, u32[]{:S(2)}) collective-permute-start(f32[8,256]{1,0:T(8,128)S(1)} %get-tuple-element.23), channel_id=1, source_target_pairs={{0,4},{2,6},{4,0},{6,2},{1,5},{3,7},{5,1},{7,3},{8,12},{10,14},{12... | collective-permute-start | bytes 24584 | tf_op jit(solution)/shard_map/ppermute | solution.py:206
  76.3 2.6 %collective-permute-start.11 = (f32[8,256]{1,0:T(8,128)S(1)}, f32[8,256]{1,0:T(8,128)S(1)}, u32[]{:S(2)}, u32[]{:S(2)}) collective-permute-start(f32[8,256]{1,0:T(8,128)S(1)} %get-tuple-element.23), channel_id=1, source_target_pairs={{0,6},{2,0},{4,2},{6,4},{1,7},{3,1},{5,3},{7,5},{8,14},{10,8},{12,... | collective-permute-start | bytes 24584 | tf_op jit(solution)/shard_map/ppermute | solution.py:206
  78.9 3.4 %all-to-all-start.1 = ((f32[8,8,1280]{2,1,0:T(8,128)}), f32[8,8,1280]{2,1,0:T(8,128)S(1)}, u32[]{:S(2)}, u32[]{:S(2)}) async-start(f32[8,8,1280]{2,1,0:T(8,128)} %get-tuple-element.22), calls=%async_computation.1 | async-start | bytes 655360 | tf_op jit(solution)/shard_map/all_to_all | solution.py:415
  82.3 0.0 collective-permute-done.11
  82.4 0.0 collective-permute-done.12
  82.4 0.0 collective-permute-done.13
  82.4 0.9 collective-permute-start.14
  83.3 1.2 %collective-permute-start.16 = (f32[32,256]{1,0:T(8,128)S(1)}, f32[32,256]{1,0:T(8,128)S(1)}, u32[]{:S(2)}, u32[]{:S(2)}) collective-permute-start(f32[32,256]{1,0:T(8,128)S(1)} %get-tuple-element.38), channel_id=1, source_target_pairs={{0,8},{8,16},{16,24},{24,0},{1,9},{9,17},{17,25},{25,1},{2,10},{10... | collective-permute-start | bytes 98312 | tf_op jit(solution)/shard_map/ppermute | solution.py:206
  84.5 3.7 %collective-permute-start.15 = (f32[32,256]{1,0:T(8,128)S(1)}, f32[32,256]{1,0:T(8,128)S(1)}, u32[]{:S(2)}, u32[]{:S(2)}) collective-permute-start(f32[32,256]{1,0:T(8,128)S(1)} %get-tuple-element.38), channel_id=1, source_target_pairs={{0,16},{8,24},{16,0},{24,8},{1,17},{9,25},{17,1},{25,9},{2,18},{10... | collective-permute-start | bytes 98312 | tf_op jit(solution)/shard_map/ppermute | solution.py:206
  88.2 0.0 collective-permute-done.14
  88.2 1.9 %collective-permute-done.15 = f32[32,256]{1,0:T(8,128)S(1)} collective-permute-done((f32[32,256]{1,0:T(8,128)S(1)}, f32[32,256]{1,0:T(8,128)S(1)}, u32[]{:S(2)}, u32[]{:S(2)}) %collective-permute-start.15) | collective-permute-done | bytes 32800 | tf_op jit(solution)/shard_map/ppermute | solution.py:206
  90.1 0.0 collective-permute-done.16
  90.1 3.3 %all-to-all-done.1 = f32[8,8,1280]{2,1,0:T(8,128)S(1)} async-done(((f32[8,8,1280]{2,1,0:T(8,128)}), f32[8,8,1280]{2,1,0:T(8,128)S(1)}, u32[]{:S(2)}, u32[]{:S(2)}) %all-to-all-start.1) | async-done | bytes 327712 | tf_op jit(solution)/shard_map/all_to_all | solution.py:415
  93.4 1.0 collective-permute-start.20
  94.5 1.8 %collective-permute-start.19 = (f32[64,1280]{1,0:T(8,128)S(1)}, f32[64,1280]{1,0:T(8,128)S(1)}, u32[]{:S(2)}, u32[]{:S(2)}) collective-permute-start(f32[64,1280]{1,0:T(8,128)S(1)} %bitcast.16), channel_id=1, source_target_pairs={{0,16},{8,24},{16,0},{24,8},{1,17},{9,25},{17,1},{25,9},{2,18},{10... | collective-permute-start | bytes 983048 | tf_op jit(solution)/shard_map/ppermute | solution.py:206
  96.3 2.3 %collective-permute-start.18 = (f32[64,1280]{1,0:T(8,128)S(1)}, f32[64,1280]{1,0:T(8,128)S(1)}, u32[]{:S(2)}, u32[]{:S(2)}) collective-permute-start(f32[64,1280]{1,0:T(8,128)S(1)} %bitcast.17), channel_id=1, source_target_pairs={{0,24},{8,0},{16,8},{24,16},{1,25},{9,1},{17,9},{25,17},{2,26},{10... | collective-permute-start | bytes 983048 | tf_op jit(solution)/shard_map/ppermute | solution.py:206
  98.7 0.0 collective-permute-start.17
  98.7 1.3 %collective-permute-done.17.other_ref = f32[128,256]{1,0:T(8,128)S(1)} collective-permute-done((f32[128,256]{1,0:T(8,128)S(1)}, f32[128,256]{1,0:T(8,128)S(1)}, u32[]{:S(2)}, u32[]{:S(2)}) %collective-permute-start.17) | collective-permute-done | bytes 131104 | tf_op jit(solution)/shard_map/ppermute | solution.py:56
  100.0 5.6 %factor_first.1 = (f32[128,128]{1,0:T(8,128)S(1)}, f32[128,128]{1,0:T(8,128)S(1)}, f32[128,128]{1,0:T(8,128)S(1)}) custom-call(s32[1]{0:T(128)} %bitcast.1.x_ref, s32[1]{0:T(128)} %bitcast.y_ref, s32[1]{0:T(128)} %bitcast.2.core_ref, f32[128,256]{1,0:T(8,128)S(1)} %constant_dynamic-update-slice_fusion.4.mine_ref, ...), custom_call_target="tpu_custom_call" | custom-call | tf_op jit(solution)/shard_map/factor_first/pallas_call | solution.py:335
  105.6 6.5 %factor_last.1 = (f32[256,256]{1,0:T(8,128)S(1)}, bf16[1024,768]{1,0:T(8,128)(2,1)S(1)}) custom-call(f32[128,128]{1,0:T(8,128)S(1)} %get-tuple-element.25.w11_ref, f32[128,128]{1,0:T(8,128)S(1)} %get-tuple-element.26.l_ref, f32[128,128]{1,0:T(8,128)S(1)} %get-tuple-element.27.s_ref, f32[1024,256]{1,0:T(8,128)} %copy-done), custom_call_target="tpu_custom_call" | custom-call | tf_op jit(solution)/shard_map/factor_last/pallas_call | solution.py:348
  112.1 0.0 collective-permute-done.20.x3_ref
  112.1 0.0 collective-permute-done.19.x2_ref
  112.1 0.0 collective-permute-done.18.x1_ref
  112.1 5.5 %update.1 = (f32[10,1024,128]{2,1,0:T(8,128)}, f32[10,256,128]{2,1,0:T(8,128)}) custom-call(s32[1]{0:T(128)} %bitcast.y_ref, f32[256,256]{1,0:T(8,128)S(1)} %get-tuple-element.29.w_ref, bf16[1024,768]{1,0:T(8,128)(2,1)S(1)} %get-tuple-element.30.q_ref, f32[64,1280]{1,0:T(8,128)S(1)} %bitcast.18, f32[64,1280]{1,0:T(8,128)S(1)} %collective-permute-done.18.x1_ref, ...), custom_call_target="tpu_custom_call" | custom-call | tf_op jit(solution)/shard_map/update/pallas_call | solution.py:396
  (7 shorter events, 0.0 us)
Async XLA Ops:
  1.7 11.4 %collective-permute-start.4 = (f32[512,128]{1,0:T(8,128)S(1)}, f32[512,128]{1,0:T(8,128)S(1)}, u32[]{:S(2)}, u32[]{:S(2)}) collective-permute-start(f32[512,128]{1,0:T(8,128)S(1)} %get-tuple-element.36), channel_id=1, source_target_pairs={{0,6},{1,7},{8,14},{9,15},{16,22},{17,23},{24,30},{25,31},{32,38},... | collective-permute-start | bytes 786440 | tf_op jit(solution)/shard_map/ppermute | solution.py:64
  6.4 8.0 %collective-permute-start = (f32[512,128]{1,0:T(8,128)S(1)}, f32[512,128]{1,0:T(8,128)S(1)}, u32[]{:S(2)}, u32[]{:S(2)}) collective-permute-start(f32[512,128]{1,0:T(8,128)S(1)} %get-tuple-element.37), channel_id=1, source_target_pairs={{0,2},{1,3},{8,10},{9,11},{16,18},{17,19},{24,26},{25,27},{32,34},... | collective-permute-start | bytes 786440 | tf_op jit(solution)/shard_map/ppermute | solution.py:63
  7.7 11.1 %collective-permute-start.3 = (f32[512,128]{1,0:T(8,128)S(1)}, f32[512,128]{1,0:T(8,128)S(1)}, u32[]{:S(2)}, u32[]{:S(2)}) collective-permute-start(f32[512,128]{1,0:T(8,128)S(1)} %get-tuple-element.36), channel_id=1, source_target_pairs={{0,2},{1,3},{8,10},{9,11},{16,18},{17,19},{24,26},{25,27},{32,34},... | collective-permute-start | bytes 786440 | tf_op jit(solution)/shard_map/ppermute | solution.py:65
  9.0 9.8 %collective-permute-start.2 = (f32[512,128]{1,0:T(8,128)S(1)}, f32[512,128]{1,0:T(8,128)S(1)}, u32[]{:S(2)}, u32[]{:S(2)}) collective-permute-start(f32[512,128]{1,0:T(8,128)S(1)} %get-tuple-element.37), channel_id=1, source_target_pairs={{0,6},{1,7},{8,14},{9,15},{16,22},{17,23},{24,30},{25,31},{32,38},... | collective-permute-start | bytes 786440 | tf_op jit(solution)/shard_map/ppermute | solution.py:66
  13.1 5.8 %collective-permute-start.5 = (f32[512,128]{1,0:T(8,128)S(1)}, f32[512,128]{1,0:T(8,128)S(1)}, u32[]{:S(2)}, u32[]{:S(2)}) collective-permute-start(f32[512,128]{1,0:T(8,128)S(1)} %collective-permute-done.4), channel_id=1, source_target_pairs={{6,4},{7,5},{14,12},{15,13},{22,20},{23,21},{30,28},{31,29},{38,36... | collective-permute-start | bytes 786440 | tf_op jit(solution)/shard_map/ppermute | solution.py:68
  14.4 4.5 %collective-permute-start.1 = (f32[512,128]{1,0:T(8,128)S(1)}, f32[512,128]{1,0:T(8,128)S(1)}, u32[]{:S(2)}, u32[]{:S(2)}) collective-permute-start(f32[512,128]{1,0:T(8,128)S(1)} %collective-permute-done), channel_id=1, source_target_pairs={{2,4},{3,5},{10,12},{11,13},{18,20},{19,21},{26,28},{27,29},{34,36... | collective-permute-start | bytes 786440 | tf_op jit(solution)/shard_map/ppermute | solution.py:67
  20.0 1.6 %collective-permute-start.7 = (f32[512,128]{1,0:T(8,128)S(1)}, f32[512,128]{1,0:T(8,128)S(1)}, u32[]{:S(2)}, u32[]{:S(2)}) collective-permute-start(f32[512,128]{1,0:T(8,128)S(1)} %get-tuple-element.34.mh_ref), channel_id=1, source_target_pairs={{0,1},{1,0},{2,3},{3,2},{4,5},{5,4},{6,7},{7,6},{8,9},{9,8},{10,11... | collective-permute-start | bytes 786440 | tf_op jit(solution)/shard_map/ppermute | solution.py:56
  20.1 1.9 %collective-permute-start.6 = (f32[512,128]{1,0:T(8,128)S(1)}, f32[512,128]{1,0:T(8,128)S(1)}, u32[]{:S(2)}, u32[]{:S(2)}) collective-permute-start(f32[512,128]{1,0:T(8,128)S(1)} %get-tuple-element.35.ml_ref), channel_id=1, source_target_pairs={{0,1},{1,0},{2,3},{3,2},{4,5},{5,4},{6,7},{7,6},{8,9},{9,8},{10,11... | collective-permute-start | bytes 786440 | tf_op jit(solution)/shard_map/ppermute | solution.py:56
  27.0 43.6 %copy-start = (f32[1024,256]{1,0:T(8,128)}, f32[1024,256]{1,0:T(8,128)S(1)}, u32[]{:S(2)}) copy-start(f32[1024,256]{1,0:T(8,128)S(1)} %get-tuple-element.28.p_hbm) | copy-start | bytes 3145732
  27.0 11.3 %collective-permute-start.8 = (f32[64,1408]{1,0:T(8,128)S(1)}, f32[64,1408]{1,0:T(8,128)S(1)}, u32[]{:S(2)}, u32[]{:S(2)}) collective-permute-start(f32[64,1408]{1,0:T(8,128)S(1)} %get-tuple-element.19), channel_id=1, source_target_pairs={{0,8},{8,16},{16,24},{24,0},{1,9},{9,17},{17,25},{25,1},{2,10},{10... | collective-permute-start | bytes 1081352 | tf_op jit(solution)/shard_map/ppermute | solution.py:200
  28.6 12.8 %collective-permute-start.9 = (f32[64,1408]{1,0:T(8,128)S(1)}, f32[64,1408]{1,0:T(8,128)S(1)}, u32[]{:S(2)}, u32[]{:S(2)}) collective-permute-start(f32[64,1408]{1,0:T(8,128)S(1)} %get-tuple-element.20), channel_id=1, source_target_pairs={{0,16},{8,24},{16,0},{24,8},{1,17},{9,25},{17,1},{25,9},{2,18},{10... | collective-permute-start | bytes 1081352 | tf_op jit(solution)/shard_map/ppermute | solution.py:200
  29.6 17.8 %collective-permute-start.10 = (f32[64,1408]{1,0:T(8,128)S(1)}, f32[64,1408]{1,0:T(8,128)S(1)}, u32[]{:S(2)}, u32[]{:S(2)}) collective-permute-start(f32[64,1408]{1,0:T(8,128)S(1)} %get-tuple-element.21), channel_id=1, source_target_pairs={{0,24},{8,0},{16,8},{24,16},{1,25},{9,1},{17,9},{25,17},{2,26},{10... | collective-permute-start | bytes 1081352 | tf_op jit(solution)/shard_map/ppermute | solution.py:200
  70.6 11.8 %collective-permute-start.13 = (f32[8,256]{1,0:T(8,128)S(1)}, f32[8,256]{1,0:T(8,128)S(1)}, u32[]{:S(2)}, u32[]{:S(2)}) collective-permute-start(f32[8,256]{1,0:T(8,128)S(1)} %get-tuple-element.23), channel_id=1, source_target_pairs={{0,2},{2,4},{4,6},{6,0},{1,3},{3,5},{5,7},{7,1},{8,10},{10,12},{12... | collective-permute-start | bytes 24584 | tf_op jit(solution)/shard_map/ppermute | solution.py:206
  73.7 8.6 %collective-permute-start.12 = (f32[8,256]{1,0:T(8,128)S(1)}, f32[8,256]{1,0:T(8,128)S(1)}, u32[]{:S(2)}, u32[]{:S(2)}) collective-permute-start(f32[8,256]{1,0:T(8,128)S(1)} %get-tuple-element.23), channel_id=1, source_target_pairs={{0,4},{2,6},{4,0},{6,2},{1,5},{3,7},{5,1},{7,3},{8,12},{10,14},{12... | collective-permute-start | bytes 24584 | tf_op jit(solution)/shard_map/ppermute | solution.py:206
  76.3 6.1 %collective-permute-start.11 = (f32[8,256]{1,0:T(8,128)S(1)}, f32[8,256]{1,0:T(8,128)S(1)}, u32[]{:S(2)}, u32[]{:S(2)}) collective-permute-start(f32[8,256]{1,0:T(8,128)S(1)} %get-tuple-element.23), channel_id=1, source_target_pairs={{0,6},{2,0},{4,2},{6,4},{1,7},{3,1},{5,3},{7,5},{8,14},{10,8},{12,... | collective-permute-start | bytes 24584 | tf_op jit(solution)/shard_map/ppermute | solution.py:206
  78.9 14.5 %all-to-all-start.1 = ((f32[8,8,1280]{2,1,0:T(8,128)}), f32[8,8,1280]{2,1,0:T(8,128)S(1)}, u32[]{:S(2)}, u32[]{:S(2)}) async-start(f32[8,8,1280]{2,1,0:T(8,128)} %get-tuple-element.22), calls=%async_computation.1 | async-start | bytes 655360 | tf_op jit(solution)/shard_map/all_to_all | solution.py:415
  82.4 5.8 %collective-permute-start.14 = (f32[32,256]{1,0:T(8,128)S(1)}, f32[32,256]{1,0:T(8,128)S(1)}, u32[]{:S(2)}, u32[]{:S(2)}) collective-permute-start(f32[32,256]{1,0:T(8,128)S(1)} %get-tuple-element.38), channel_id=1, source_target_pairs={{0,24},{8,0},{16,8},{24,16},{1,25},{9,1},{17,9},{25,17},{2,26},{10... | collective-permute-start | bytes 98312 | tf_op jit(solution)/shard_map/ppermute | solution.py:206
  83.3 6.8 %collective-permute-start.16 = (f32[32,256]{1,0:T(8,128)S(1)}, f32[32,256]{1,0:T(8,128)S(1)}, u32[]{:S(2)}, u32[]{:S(2)}) collective-permute-start(f32[32,256]{1,0:T(8,128)S(1)} %get-tuple-element.38), channel_id=1, source_target_pairs={{0,8},{8,16},{16,24},{24,0},{1,9},{9,17},{17,25},{25,1},{2,10},{10... | collective-permute-start | bytes 98312 | tf_op jit(solution)/shard_map/ppermute | solution.py:206
  84.5 5.6 %collective-permute-start.15 = (f32[32,256]{1,0:T(8,128)S(1)}, f32[32,256]{1,0:T(8,128)S(1)}, u32[]{:S(2)}, u32[]{:S(2)}) collective-permute-start(f32[32,256]{1,0:T(8,128)S(1)} %get-tuple-element.38), channel_id=1, source_target_pairs={{0,16},{8,24},{16,0},{24,8},{1,17},{9,25},{17,1},{25,9},{2,18},{10... | collective-permute-start | bytes 98312 | tf_op jit(solution)/shard_map/ppermute | solution.py:206
  93.4 18.7 %collective-permute-start.20 = (f32[64,1280]{1,0:T(8,128)S(1)}, f32[64,1280]{1,0:T(8,128)S(1)}, u32[]{:S(2)}, u32[]{:S(2)}) collective-permute-start(f32[64,1280]{1,0:T(8,128)S(1)} %bitcast.15), channel_id=1, source_target_pairs={{0,8},{8,16},{16,24},{24,0},{1,9},{9,17},{17,25},{25,1},{2,10},{10... | collective-permute-start | bytes 983048 | tf_op jit(solution)/shard_map/ppermute | solution.py:206
  94.5 17.6 %collective-permute-start.19 = (f32[64,1280]{1,0:T(8,128)S(1)}, f32[64,1280]{1,0:T(8,128)S(1)}, u32[]{:S(2)}, u32[]{:S(2)}) collective-permute-start(f32[64,1280]{1,0:T(8,128)S(1)} %bitcast.16), channel_id=1, source_target_pairs={{0,16},{8,24},{16,0},{24,8},{1,17},{9,25},{17,1},{25,9},{2,18},{10... | collective-permute-start | bytes 983048 | tf_op jit(solution)/shard_map/ppermute | solution.py:206
  96.3 15.8 %collective-permute-start.18 = (f32[64,1280]{1,0:T(8,128)S(1)}, f32[64,1280]{1,0:T(8,128)S(1)}, u32[]{:S(2)}, u32[]{:S(2)}) collective-permute-start(f32[64,1280]{1,0:T(8,128)S(1)} %bitcast.17), channel_id=1, source_target_pairs={{0,24},{8,0},{16,8},{24,16},{1,25},{9,1},{17,9},{25,17},{2,26},{10... | collective-permute-start | bytes 983048 | tf_op jit(solution)/shard_map/ppermute | solution.py:206
  98.7 1.3 %collective-permute-start.17 = (f32[128,256]{1,0:T(8,128)S(1)}, f32[128,256]{1,0:T(8,128)S(1)}, u32[]{:S(2)}, u32[]{:S(2)}) collective-permute-start(f32[128,256]{1,0:T(8,128)S(1)} %constant_dynamic-update-slice_fusion.4.mine_ref), channel_id=1, source_target_pairs={{0,1},{1,0},{2,3},{3,2},{4,5},{5,4},{6,7},{7,6},{8,9},{9,8},{10,11... | collective-permute-start | bytes 393224 | tf_op jit(solution)/shard_map/ppermute | solution.py:56

commit v3 on v2

--- a/solution.py
+++ b/solution.py
@@ -298,25 +298,26 @@
             w_ref[row0 + j + k : row0 + j + k + 1, col0 : col0 + LANES] = w[0:1]
 
 
-def factor_first_kernel(x_ref, y_ref, core_ref, mine_ref, other_ref, w_ref, l_ref, s_ref, g_ref):
+def factor_first_kernel(x_ref, y_ref, core_ref, p_ref, w_ref, l_ref, s_ref, g_ref):
     h = LANES
-    for half, half_ref in enumerate((mine_ref, other_ref)):
-        core = (core_ref[0] + half) % NC
-        for dy in range(NY):
-            for dx in range(NX):
-                x, y = (x_ref[0] + dx) % NX, (y_ref[0] + dy) % NY
+    for dy in range(NY):
+        for dx in range(NX):
+            for dc in range(NC):
+                x, y, core = (x_ref[0] + dx) % NX, (y_ref[0] + dy) % NY, (core_ref[0] + dc) % NC
                 at = pl.multiple_of(((x * NC + core) * NY + y) * SUB, SUB)
-                row = (dy * NX + dx) * SUB
-                g_ref[pl.ds(at, SUB), :] = half_ref[row : row + SUB, :]
+                row = ((dy * NX + dx) * NC + dc) * SUB
+                g_ref[pl.ds(at, SUB), :] = p_ref[row : row + SUB, :]
     invert_factor(g_ref[:h, :h], w_ref, 0, 0)
     l21 = dot(g_ref[h:, :h], w_ref[...], NT)
     l_ref[...] = l21
     s_ref[...] = g_ref[h:, h:] - dot(l21, l21, NT)
 
 
-def factor_last_kernel(w11_ref, l_ref, s_ref, p_hbm, w_ref, q_ref, p_ref, sem):
+def factor_last_kernel(w11_ref, l_ref, s_ref, p_hbm, c_hbm, w_ref, q_ref, c_ref, p_ref, sem, c_sem):
     arriving = pltpu.make_async_copy(p_hbm, p_ref, sem)
     arriving.start()
+    resident = pltpu.make_async_copy(c_hbm, c_ref, c_sem)
+    resident.start()
     h = LANES
     w11 = w11_ref[...]
     w_ref[:h, :h] = w11
@@ -328,47 +329,52 @@
     right = jnp.concatenate([high, low, high], axis=1)
     basis = lax.dot_general(wide_left(p_ref[...]), right, NT, preferred_element_type=jnp.float32)
     q_ref[...] = wide_left(basis)
-
-
-def factor_first(mine, other):
-    h, w = mine.shape
+    resident.wait()
+
+
+def factor_first(pieces):
+    w = pieces.shape[0]
+    h = w // 2
     return pl.pallas_call(
         factor_first_kernel,
-        in_specs=[SCALAR] * 3 + [VMEM] * 2,
+        in_specs=[SCALAR] * 3 + [VMEM],
         out_specs=[VMEM] * 3,
         out_shape=[jax.ShapeDtypeStruct((h, h), jnp.float32)] * 3,
         scratch_shapes=[pltpu.VMEM((w, w), jnp.float32)],
         compiler_params=params(8),
         name="factor_first",
-    )(index_of("x"), index_of("y"), index_of("c"), mine, other)
-
-
-def factor_last(w11, l21, schur, panels):
+    )(index_of("x"), index_of("y"), index_of("c"), pieces)
+
+
+def factor_last(w11, l21, schur, panels, columns):
     n, w = panels.shape
     return pl.pallas_call(
         factor_last_kernel,
-        in_specs=[VMEM] * 3 + [HBM],
-        out_specs=[VMEM] * 2,
-        out_shape=[jax.ShapeDtypeStruct((w, w), jnp.float32), jax.ShapeDtypeStruct((n, 3 * w), jnp.bfloat16)],
-        scratch_shapes=[pltpu.VMEM((n, w), jnp.float32), pltpu.SemaphoreType.DMA(())],
+        in_specs=[VMEM] * 3 + [HBM] * 2,
+        out_specs=[VMEM] * 3,
+        out_shape=[
+            jax.ShapeDtypeStruct((w, w), jnp.float32),
+            jax.ShapeDtypeStruct((n, 3 * w), jnp.bfloat16),
+            jax.ShapeDtypeStruct(columns.shape, jnp.float32),
+        ],
+        scratch_shapes=[
+            pltpu.VMEM((n, w), jnp.float32),
+            pltpu.SemaphoreType.DMA(()),
+            pltpu.SemaphoreType.DMA(()),
+        ],
         compiler_params=params(12),
         name="factor_last",
-    )(w11, l21, schur, panels)
+    )(w11, l21, schur, panels, columns)
 
 
 BAND = 256
 
 
 def update_kernel(
-    y_ref, w_ref, q_ref, x0_ref, x1_ref, x2_ref, x3_ref, c_hbm, red_hbm, top_hbm, x_ref, red_ref, top_ref, c_sem, red_sem, top_sem
+    y_ref, w_ref, q_ref, x0_ref, x1_ref, x2_ref, x3_ref, c_ref, red_hbm, top_hbm, x_ref, red_ref, top_ref, red_sem, top_sem
 ):
     rounds, n, k = red_ref.shape
     bands = [pl.ds(at, BAND) for at in range(0, n, BAND)]
-    arriving = [
-        pltpu.make_async_copy(c_hbm.at[:, band], red_ref.at[:, band], c_sem.at[at]) for at, band in enumerate(bands)
-    ]
-    for copy in arriving:
-        copy.start()
     for by, part_ref in enumerate((x0_ref, x1_ref, x2_ref, x3_ref)):
         x_ref[around(y_ref, by, NY, part_ref.shape[0]), :] = part_ref[...]
     top = narrow_dot(wide_left(w_ref[...]), wide_right(x_ref[...]))
@@ -379,9 +385,9 @@
     right = wide_right(top)
     for at, band in enumerate(bands):
         fit = narrow_dot(q_ref[at * BAND : (at + 1) * BAND], right)
-        arriving[at].wait()
+        rows = slice(at * BAND, (at + 1) * BAND)
         for r in range(rounds):
-            red_ref[r, at * BAND : (at + 1) * BAND] -= fit[:, r * k : (r + 1) * k]
+            red_ref[r, rows] = c_ref[r, rows] - fit[:, r * k : (r + 1) * k]
         copy = pltpu.make_async_copy(red_ref.at[:, band], red_hbm.at[:, band], red_sem.at[at])
         copy.start()
         leaving.append(copy)
@@ -395,7 +401,7 @@
     reduced, top = (rounds, n, k), (rounds, w, k)
     return pl.pallas_call(
         update_kernel,
-        in_specs=[SCALAR] + [VMEM] * (2 + NY) + [HBM],
+        in_specs=[SCALAR] + [VMEM] * (3 + NY),
         out_specs=[HBM] * 2,
         out_shape=[jax.ShapeDtypeStruct(reduced, jnp.float32), jax.ShapeDtypeStruct(top, jnp.float32)],
         scratch_shapes=[
@@ -403,7 +409,6 @@
             pltpu.VMEM(reduced, jnp.float32),
             pltpu.VMEM(top, jnp.float32),
             pltpu.SemaphoreType.DMA((n // BAND,)),
-            pltpu.SemaphoreType.DMA((n // BAND,)),
             pltpu.SemaphoreType.DMA(()),
         ],
         compiler_params=params(24),
@@ -421,10 +426,11 @@
     *pieces, panels = products(relay(own), columns)
     copies, gram = sum_z(exchange_z(sum_y(deal(pieces, "y"))))
     part = exchange_z(copies).reshape(NZ * SUB, RIDE)
+    gram = jnp.concatenate([gram, swap(gram)], axis=0)
     gram = collect(collect(gram, "x", NX), "y", NY)
     part, gram = lax.optimization_barrier((part, gram))
-    inverse, basis = factor_last(*factor_first(gram, swap(gram)), in_hbm(panels))
-    reduced, top = update(inverse, basis, every(part, "y", NY), columns)
+    inverse, basis, resident = factor_last(*factor_first(gram), in_hbm(panels), columns)
+    reduced, top = update(inverse, basis, every(part, "y", NY), resident)
     return jnp.transpose(reduced, (1, 0, 2)), jnp.transpose(top, (1, 0, 2))
 
 

time: 119 us -> 117 us (0.983)
  waiting for transfers between devices: 30.5 us -> 29.2 us
    all_to_all x1, waiting for transfers between devices: 3.3 us -> 0.01 us  [exchange_z(): return lax.all_to_all(pieces, 'z', 0, 0)]
    ppermute x9, waiting for transfers between devices: 1.9 us -> 4.13 us  [every(): lax.ppermute(values, axis, [(at, (at - by) % size) for at in range(size)])]
  transfers between devices with their start and end apart: 22 -> 22, of which waited for: 11 -> 11; matrix products, arithmetic and copies ran while one was open for 0% -> 0% of each run, Pallas kernels for 10% -> 11%
where the time goes in v3:
time: 117 us
  starting transfers between devices  38.8 us (33%)
  waiting for transfers between devices  29.2 us (25%)
  Pallas kernels  22.9 us (20%)
  blocking collectives  22.4 us (19%)
    all_to_all x1, blocking collectives, exchange_z(): return lax.all_to_all(pieces, 'z', 0, 0)  22.4 us
    ppermute x9, starting transfers between devices, every(): lax.ppermute(values, axis, [(at, (at - by) % size) for at in range(size)])  19.8 us
    ppermute x3, waiting for transfers between devices, deal(): lax.ppermute(pieces[by], axis, [(at, (at + by) % size) for at in range(si...  15.4 us
    pallas_call x1, Pallas kernels, factor_last(): pl.pallas_call(factor_last_kernel, in_specs=[VMEM] * 3 + [HBM] * 2, out_s...  7.52 us
    pallas_call x1, Pallas kernels, factor_first(): pl.pallas_call(factor_first_kernel, in_specs=[SCALAR] * 3 + [VMEM], out_s...  5.56 us
    ppermute x3, starting transfers between devices, deal(): lax.ppermute(pieces[by], axis, [(at, (at + by) % size) for at in range(si...  5 us
    pallas_call x1, Pallas kernels, products(): pl.pallas_call(products_kernel, in_specs=[SCALAR] * 3 + [VMEM] * 4 + [HBM...  4.97 us
    ppermute x1, starting transfers between devices, relay(): down_high = lax.ppermute(high, 'x', [(0, 3)])  4.68 us
  transfers between devices with their start and end apart: 22, of which 11 were waited for; matrix products, arithmetic and copies ran while one was open for 0% of the time, Pallas kernels for 11%

profile of v3, /device:TPU:8, one launch (start us, length us, event | category | flops | bytes accessed | tf_op | source)
XLA Modules:
  0.0 116.5 jit_solution(7722879171574146513)
XLA Ops:
  0.6 1.1 slice_bitcast_fusion
  1.7 4.7 %collective-permute-start.4 = (f32[512,128]{1,0:T(8,128)S(1)}, f32[512,128]{1,0:T(8,128)S(1)}, u32[]{:S(2)}, u32[]{:S(2)}) collective-permute-start(f32[512,128]{1,0:T(8,128)S(1)} %get-tuple-element.38), channel_id=1, source_target_pairs={{0,6},{1,7},{8,14},{9,15},{16,22},{17,23},{24,30},{25,31},{32,38},... | collective-permute-start | bytes 786440 | tf_op jit(solution)/shard_map/ppermute | solution.py:64
  6.4 1.3 %collective-permute-start = (f32[512,128]{1,0:T(8,128)S(1)}, f32[512,128]{1,0:T(8,128)S(1)}, u32[]{:S(2)}, u32[]{:S(2)}) collective-permute-start(f32[512,128]{1,0:T(8,128)S(1)} %get-tuple-element.39), channel_id=1, source_target_pairs={{0,2},{1,3},{8,10},{9,11},{16,18},{17,19},{24,26},{25,27},{32,34},... | collective-permute-start | bytes 786440 | tf_op jit(solution)/shard_map/ppermute | solution.py:63
  7.7 1.3 %collective-permute-start.3 = (f32[512,128]{1,0:T(8,128)S(1)}, f32[512,128]{1,0:T(8,128)S(1)}, u32[]{:S(2)}, u32[]{:S(2)}) collective-permute-start(f32[512,128]{1,0:T(8,128)S(1)} %get-tuple-element.38), channel_id=1, source_target_pairs={{0,2},{1,3},{8,10},{9,11},{16,18},{17,19},{24,26},{25,27},{32,34},... | collective-permute-start | bytes 786440 | tf_op jit(solution)/shard_map/ppermute | solution.py:65
  9.0 1.3 %collective-permute-start.2 = (f32[512,128]{1,0:T(8,128)S(1)}, f32[512,128]{1,0:T(8,128)S(1)}, u32[]{:S(2)}, u32[]{:S(2)}) collective-permute-start(f32[512,128]{1,0:T(8,128)S(1)} %get-tuple-element.39), channel_id=1, source_target_pairs={{0,6},{1,7},{8,14},{9,15},{16,22},{17,23},{24,30},{25,31},{32,38},... | collective-permute-start | bytes 786440 | tf_op jit(solution)/shard_map/ppermute | solution.py:66
  10.3 2.7 %collective-permute-done.4 = f32[512,128]{1,0:T(8,128)S(1)} collective-permute-done((f32[512,128]{1,0:T(8,128)S(1)}, f32[512,128]{1,0:T(8,128)S(1)}, u32[]{:S(2)}, u32[]{:S(2)}) %collective-permute-start.4) | collective-permute-done | bytes 262176 | tf_op jit(solution)/shard_map/ppermute | solution.py:64
  13.1 0.7 collective-permute-start.5
  13.7 0.6 collective-permute-done
  14.4 0.7 collective-permute-start.1
  15.1 3.8 %collective-permute-done.3 = f32[512,128]{1,0:T(8,128)S(1)} collective-permute-done((f32[512,128]{1,0:T(8,128)S(1)}, f32[512,128]{1,0:T(8,128)S(1)}, u32[]{:S(2)}, u32[]{:S(2)}) %collective-permute-start.3) | collective-permute-done | bytes 262176 | tf_op jit(solution)/shard_map/ppermute | solution.py:65
  18.8 0.0 collective-permute-done.2
  18.9 0.0 collective-permute-done.5
  18.9 0.0 collective-permute-done.1
  18.9 1.1 select_select_fusion
  20.0 0.1 collective-permute-start.7
  20.1 0.5 collective-permute-start.6
  20.6 1.0 collective-permute-done.7.oh_ref
  21.6 0.4 collective-permute-done.6.ol_ref
  22.0 5.0 %products.1 = (f32[64,1408]{1,0:T(8,128)S(1)}, f32[64,1408]{1,0:T(8,128)S(1)}, f32[64,1408]{1,0:T(8,128)S(1)}, f32[64,1408]{1,0:T(8,128)S(1)}, f32[1024,256]{1,0:T(8,128)S(1)}) custom-call(s32[1]{0:T(128)} %bitcast.1.x_ref, s32[1]{0:T(128)} %bitcast.y_ref, s32[1]{0:T(128)} %bitcast.2.core_ref, f32[512,128]{1,0:T(8,128)S(1)} %get-tuple-element.37.ml_ref, ...), custom_call_target="tpu_custom_call" | custom-call | tf_op jit(solution)/shard_map/products/pallas_call | solution.py:137
  27.0 0.0 copy-start
  27.0 1.7 %collective-permute-start.8 = (f32[64,1408]{1,0:T(8,128)S(1)}, f32[64,1408]{1,0:T(8,128)S(1)}, u32[]{:S(2)}, u32[]{:S(2)}) collective-permute-start(f32[64,1408]{1,0:T(8,128)S(1)} %get-tuple-element.20), channel_id=1, source_target_pairs={{0,8},{8,16},{16,24},{24,0},{1,9},{9,17},{17,25},{25,1},{2,10},{10... | collective-permute-start | bytes 1081352 | tf_op jit(solution)/shard_map/ppermute | solution.py:200
  28.6 0.9 collective-permute-start.9
  29.6 2.4 %collective-permute-start.10 = (f32[64,1408]{1,0:T(8,128)S(1)}, f32[64,1408]{1,0:T(8,128)S(1)}, u32[]{:S(2)}, u32[]{:S(2)}) collective-permute-start(f32[64,1408]{1,0:T(8,128)S(1)} %get-tuple-element.22), channel_id=1, source_target_pairs={{0,24},{8,0},{16,8},{24,16},{1,25},{9,1},{17,9},{25,17},{2,26},{10... | collective-permute-start | bytes 1081352 | tf_op jit(solution)/shard_map/ppermute | solution.py:200
  32.0 6.3 %collective-permute-done.8.a1_ref = f32[64,1408]{1,0:T(8,128)S(1)} collective-permute-done((f32[64,1408]{1,0:T(8,128)S(1)}, f32[64,1408]{1,0:T(8,128)S(1)}, u32[]{:S(2)}, u32[]{:S(2)}) %collective-permute-start.8) | collective-permute-done | bytes 360480 | tf_op jit(solution)/shard_map/ppermute | solution.py:200
  38.3 3.1 %collective-permute-done.9.a2_ref = f32[64,1408]{1,0:T(8,128)S(1)} collective-permute-done((f32[64,1408]{1,0:T(8,128)S(1)}, f32[64,1408]{1,0:T(8,128)S(1)}, u32[]{:S(2)}, u32[]{:S(2)}) %collective-permute-start.9) | collective-permute-done | bytes 360480 | tf_op jit(solution)/shard_map/ppermute | solution.py:200
  41.4 5.9 %collective-permute-done.10.a3_ref = f32[64,1408]{1,0:T(8,128)S(1)} collective-permute-done((f32[64,1408]{1,0:T(8,128)S(1)}, f32[64,1408]{1,0:T(8,128)S(1)}, u32[]{:S(2)}, u32[]{:S(2)}) %collective-permute-start.10) | collective-permute-done | bytes 360480 | tf_op jit(solution)/shard_map/ppermute | solution.py:200
  47.4 0.1 sum_y.1
  47.4 22.4 %all_to_all.10.a_ref = f32[8,8,1536]{2,1,0:T(8,128)S(1)} all-to-all(f32[8,8,1536]{2,1,0:T(8,128)S(1)} %sum_y.1), channel_id=1, replica_groups=mesh['z'=8,'y'=4,'x'=4,'c'=2] {'z'}, dimensions={0} | all-to-all | bytes 786432 | tf_op jit(solution)/shard_map/all_to_all | solution.py:420
  69.8 0.8 sum_z.1
  70.6 0.0 copy-done
  70.6 0.0 collective-permute-start.11
  70.6 1.2 collective-permute-done.11
  71.8 3.1 %collective-permute-start.12 = (f32[16,256]{1,0:T(8,128)S(1)}, f32[16,256]{1,0:T(8,128)S(1)}, u32[]{:S(2)}, u32[]{:S(2)}) collective-permute-start(f32[16,256]{1,0:T(8,128)S(1)} %get-tuple-element.48), channel_id=1, source_target_pairs={{0,6},{2,0},{4,2},{6,4},{1,7},{3,1},{5,3},{7,5},{8,14},{10,8},{12,... | collective-permute-start | bytes 49160 | tf_op jit(solution)/shard_map/ppermute | solution.py:206
  74.8 3.4 %all-to-all-start.1 = ((f32[8,8,1280]{2,1,0:T(8,128)}), f32[8,8,1280]{2,1,0:T(8,128)S(1)}, u32[]{:S(2)}, u32[]{:S(2)}) async-start(f32[8,8,1280]{2,1,0:T(8,128)} %get-tuple-element.23), calls=%async_computation.1 | async-start | bytes 655360 | tf_op jit(solution)/shard_map/all_to_all | solution.py:420
  78.3 0.2 collective-permute-start.14
  78.4 4.5 %collective-permute-start.13 = (f32[16,256]{1,0:T(8,128)S(1)}, f32[16,256]{1,0:T(8,128)S(1)}, u32[]{:S(2)}, u32[]{:S(2)}) collective-permute-start(f32[16,256]{1,0:T(8,128)S(1)} %get-tuple-element.48), channel_id=1, source_target_pairs={{0,4},{2,6},{4,0},{6,2},{1,5},{3,7},{5,1},{7,3},{8,12},{10,14},{12... | collective-permute-start | bytes 49160 | tf_op jit(solution)/shard_map/ppermute | solution.py:206
  83.0 0.0 collective-permute-done.12
  83.0 1.9 %collective-permute-done.13 = f32[16,256]{1,0:T(8,128)S(1)} collective-permute-done((f32[16,256]{1,0:T(8,128)S(1)}, f32[16,256]{1,0:T(8,128)S(1)}, u32[]{:S(2)}, u32[]{:S(2)}) %collective-permute-start.13) | collective-permute-done | bytes 16416 | tf_op jit(solution)/shard_map/ppermute | solution.py:206
  84.9 0.0 collective-permute-done.14
  84.9 0.9 collective-permute-start.15
  85.8 1.2 %collective-permute-start.17 = (f32[64,256]{1,0:T(8,128)S(1)}, f32[64,256]{1,0:T(8,128)S(1)}, u32[]{:S(2)}, u32[]{:S(2)}) collective-permute-start(f32[64,256]{1,0:T(8,128)S(1)} %get-tuple-element.40), channel_id=1, source_target_pairs={{0,8},{8,16},{16,24},{24,0},{1,9},{9,17},{17,25},{25,1},{2,10},{10... | collective-permute-start | bytes 196616 | tf_op jit(solution)/shard_map/ppermute | solution.py:206
  87.0 3.7 %collective-permute-start.16 = (f32[64,256]{1,0:T(8,128)S(1)}, f32[64,256]{1,0:T(8,128)S(1)}, u32[]{:S(2)}, u32[]{:S(2)}) collective-permute-start(f32[64,256]{1,0:T(8,128)S(1)} %get-tuple-element.40), channel_id=1, source_target_pairs={{0,16},{8,24},{16,0},{24,8},{1,17},{9,25},{17,1},{25,9},{2,18},{10... | collective-permute-start | bytes 196616 | tf_op jit(solution)/shard_map/ppermute | solution.py:206
  90.7 0.0 collective-permute-done.15
  90.7 2.2 %collective-permute-done.16 = f32[64,256]{1,0:T(8,128)S(1)} collective-permute-done((f32[64,256]{1,0:T(8,128)S(1)}, f32[64,256]{1,0:T(8,128)S(1)}, u32[]{:S(2)}, u32[]{:S(2)}) %collective-permute-start.16) | collective-permute-done | bytes 65568 | tf_op jit(solution)/shard_map/ppermute | solution.py:206
  93.0 0.0 collective-permute-done.17
  93.0 0.0 all-to-all-done.1
  93.0 1.2 %collective-permute-start.20 = (f32[64,1280]{1,0:T(8,128)S(1)}, f32[64,1280]{1,0:T(8,128)S(1)}, u32[]{:S(2)}, u32[]{:S(2)}) collective-permute-start(f32[64,1280]{1,0:T(8,128)S(1)} %bitcast.15), channel_id=1, source_target_pairs={{0,8},{8,16},{16,24},{24,0},{1,9},{9,17},{17,25},{25,1},{2,10},{10... | collective-permute-start | bytes 983048 | tf_op jit(solution)/shard_map/ppermute | solution.py:206
  94.2 2.8 %collective-permute-start.19 = (f32[64,1280]{1,0:T(8,128)S(1)}, f32[64,1280]{1,0:T(8,128)S(1)}, u32[]{:S(2)}, u32[]{:S(2)}) collective-permute-start(f32[64,1280]{1,0:T(8,128)S(1)} %bitcast.16), channel_id=1, source_target_pairs={{0,16},{8,24},{16,0},{24,8},{1,17},{9,25},{17,1},{25,9},{2,18},{10... | collective-permute-start | bytes 983048 | tf_op jit(solution)/shard_map/ppermute | solution.py:206
  97.0 2.2 %collective-permute-start.18 = (f32[64,1280]{1,0:T(8,128)S(1)}, f32[64,1280]{1,0:T(8,128)S(1)}, u32[]{:S(2)}, u32[]{:S(2)}) collective-permute-start(f32[64,1280]{1,0:T(8,128)S(1)} %bitcast.17), channel_id=1, source_target_pairs={{0,24},{8,0},{16,8},{24,16},{1,25},{9,1},{17,9},{25,17},{2,26},{10... | collective-permute-start | bytes 983048 | tf_op jit(solution)/shard_map/ppermute | solution.py:206
  99.2 5.6 %factor_first.1 = (f32[128,128]{1,0:T(8,128)S(1)}, f32[128,128]{1,0:T(8,128)S(1)}, f32[128,128]{1,0:T(8,128)S(1)}) custom-call(s32[1]{0:T(128)} %bitcast.1.x_ref, s32[1]{0:T(128)} %bitcast.y_ref, s32[1]{0:T(128)} %bitcast.2.core_ref, f32[256,256]{1,0:T(8,128)S(1)} %constant_dynamic-update-slice_fusion.7.p_ref), custom_call_target="tpu_custom_call" | custom-call | tf_op jit(solution)/shard_map/factor_first/pallas_call | solution.py:338
  104.8 7.5 %factor_last.1 = (f32[256,256]{1,0:T(8,128)S(1)}, bf16[1024,768]{1,0:T(8,128)(2,1)S(1)}, f32[10,1024,128]{2,1,0:T(8,128)S(1)}) custom-call(f32[128,128]{1,0:T(8,128)S(1)} %get-tuple-element.26.w11_ref, f32[128,128]{1,0:T(8,128)S(1)} %get-tuple-element.27.l_ref, f32[128,128]{1,0:T(8,128)S(1)} %get-tuple-element.28.s_ref, f32[1024,256]{1,0:T(8,128)} %copy-done, ...), custom_call_target="tpu_custom_call" | custom-call | tf_op jit(solution)/shard_map/factor_last/pallas_call | solution.py:351
  112.3 0.0 collective-permute-done.20.x3_ref
  112.3 0.0 collective-permute-done.19.x2_ref
  112.3 0.0 collective-permute-done.18.x1_ref
  112.4 4.0 %update.1 = (f32[10,1024,128]{2,1,0:T(8,128)}, f32[10,256,128]{2,1,0:T(8,128)}) custom-call(s32[1]{0:T(128)} %bitcast.y_ref, f32[256,256]{1,0:T(8,128)S(1)} %get-tuple-element.30.w_ref, bf16[1024,768]{1,0:T(8,128)(2,1)S(1)} %get-tuple-element.31.q_ref, f32[64,1280]{1,0:T(8,128)S(1)} %bitcast.18, f32[64,1280]{1,0:T(8,128)S(1)} %collective-permute-done.18.x1_ref, ...), custom_call_target="tpu_custom_call" | custom-call | tf_op jit(solution)/shard_map/update/pallas_call | solution.py:402
  (8 shorter events, 0.0 us)
Async XLA Ops:
  1.7 11.4 %collective-permute-start.4 = (f32[512,128]{1,0:T(8,128)S(1)}, f32[512,128]{1,0:T(8,128)S(1)}, u32[]{:S(2)}, u32[]{:S(2)}) collective-permute-start(f32[512,128]{1,0:T(8,128)S(1)} %get-tuple-element.38), channel_id=1, source_target_pairs={{0,6},{1,7},{8,14},{9,15},{16,22},{17,23},{24,30},{25,31},{32,38},... | collective-permute-start | bytes 786440 | tf_op jit(solution)/shard_map/ppermute | solution.py:64
  6.4 8.0 %collective-permute-start = (f32[512,128]{1,0:T(8,128)S(1)}, f32[512,128]{1,0:T(8,128)S(1)}, u32[]{:S(2)}, u32[]{:S(2)}) collective-permute-start(f32[512,128]{1,0:T(8,128)S(1)} %get-tuple-element.39), channel_id=1, source_target_pairs={{0,2},{1,3},{8,10},{9,11},{16,18},{17,19},{24,26},{25,27},{32,34},... | collective-permute-start | bytes 786440 | tf_op jit(solution)/shard_map/ppermute | solution.py:63
  7.7 11.1 %collective-permute-start.3 = (f32[512,128]{1,0:T(8,128)S(1)}, f32[512,128]{1,0:T(8,128)S(1)}, u32[]{:S(2)}, u32[]{:S(2)}) collective-permute-start(f32[512,128]{1,0:T(8,128)S(1)} %get-tuple-element.38), channel_id=1, source_target_pairs={{0,2},{1,3},{8,10},{9,11},{16,18},{17,19},{24,26},{25,27},{32,34},... | collective-permute-start | bytes 786440 | tf_op jit(solution)/shard_map/ppermute | solution.py:65
  9.0 9.8 %collective-permute-start.2 = (f32[512,128]{1,0:T(8,128)S(1)}, f32[512,128]{1,0:T(8,128)S(1)}, u32[]{:S(2)}, u32[]{:S(2)}) collective-permute-start(f32[512,128]{1,0:T(8,128)S(1)} %get-tuple-element.39), channel_id=1, source_target_pairs={{0,6},{1,7},{8,14},{9,15},{16,22},{17,23},{24,30},{25,31},{32,38},... | collective-permute-start | bytes 786440 | tf_op jit(solution)/shard_map/ppermute | solution.py:66
  13.1 5.8 %collective-permute-start.5 = (f32[512,128]{1,0:T(8,128)S(1)}, f32[512,128]{1,0:T(8,128)S(1)}, u32[]{:S(2)}, u32[]{:S(2)}) collective-permute-start(f32[512,128]{1,0:T(8,128)S(1)} %collective-permute-done.4), channel_id=1, source_target_pairs={{6,4},{7,5},{14,12},{15,13},{22,20},{23,21},{30,28},{31,29},{38,36... | collective-permute-start | bytes 786440 | tf_op jit(solution)/shard_map/ppermute | solution.py:68
  14.4 4.5 %collective-permute-start.1 = (f32[512,128]{1,0:T(8,128)S(1)}, f32[512,128]{1,0:T(8,128)S(1)}, u32[]{:S(2)}, u32[]{:S(2)}) collective-permute-start(f32[512,128]{1,0:T(8,128)S(1)} %collective-permute-done), channel_id=1, source_target_pairs={{2,4},{3,5},{10,12},{11,13},{18,20},{19,21},{26,28},{27,29},{34,36... | collective-permute-start | bytes 786440 | tf_op jit(solution)/shard_map/ppermute | solution.py:67
  20.0 1.6 %collective-permute-start.7 = (f32[512,128]{1,0:T(8,128)S(1)}, f32[512,128]{1,0:T(8,128)S(1)}, u32[]{:S(2)}, u32[]{:S(2)}) collective-permute-start(f32[512,128]{1,0:T(8,128)S(1)} %get-tuple-element.36.mh_ref), channel_id=1, source_target_pairs={{0,1},{1,0},{2,3},{3,2},{4,5},{5,4},{6,7},{7,6},{8,9},{9,8},{10,11... | collective-permute-start | bytes 786440 | tf_op jit(solution)/shard_map/ppermute | solution.py:56
  20.1 1.9 %collective-permute-start.6 = (f32[512,128]{1,0:T(8,128)S(1)}, f32[512,128]{1,0:T(8,128)S(1)}, u32[]{:S(2)}, u32[]{:S(2)}) collective-permute-start(f32[512,128]{1,0:T(8,128)S(1)} %get-tuple-element.37.ml_ref), channel_id=1, source_target_pairs={{0,1},{1,0},{2,3},{3,2},{4,5},{5,4},{6,7},{7,6},{8,9},{9,8},{10,11... | collective-permute-start | bytes 786440 | tf_op jit(solution)/shard_map/ppermute | solution.py:56
  27.0 43.6 %copy-start = (f32[1024,256]{1,0:T(8,128)}, f32[1024,256]{1,0:T(8,128)S(1)}, u32[]{:S(2)}) copy-start(f32[1024,256]{1,0:T(8,128)S(1)} %get-tuple-element.29.p_hbm) | copy-start | bytes 3145732
  27.0 11.3 %collective-permute-start.8 = (f32[64,1408]{1,0:T(8,128)S(1)}, f32[64,1408]{1,0:T(8,128)S(1)}, u32[]{:S(2)}, u32[]{:S(2)}) collective-permute-start(f32[64,1408]{1,0:T(8,128)S(1)} %get-tuple-element.20), channel_id=1, source_target_pairs={{0,8},{8,16},{16,24},{24,0},{1,9},{9,17},{17,25},{25,1},{2,10},{10... | collective-permute-start | bytes 1081352 | tf_op jit(solution)/shard_map/ppermute | solution.py:200
  28.6 12.8 %collective-permute-start.9 = (f32[64,1408]{1,0:T(8,128)S(1)}, f32[64,1408]{1,0:T(8,128)S(1)}, u32[]{:S(2)}, u32[]{:S(2)}) collective-permute-start(f32[64,1408]{1,0:T(8,128)S(1)} %get-tuple-element.21), channel_id=1, source_target_pairs={{0,16},{8,24},{16,0},{24,8},{1,17},{9,25},{17,1},{25,9},{2,18},{10... | collective-permute-start | bytes 1081352 | tf_op jit(solution)/shard_map/ppermute | solution.py:200
  29.6 17.8 %collective-permute-start.10 = (f32[64,1408]{1,0:T(8,128)S(1)}, f32[64,1408]{1,0:T(8,128)S(1)}, u32[]{:S(2)}, u32[]{:S(2)}) collective-permute-start(f32[64,1408]{1,0:T(8,128)S(1)} %get-tuple-element.22), channel_id=1, source_target_pairs={{0,24},{8,0},{16,8},{24,16},{1,25},{9,1},{17,9},{25,17},{2,26},{10... | collective-permute-start | bytes 1081352 | tf_op jit(solution)/shard_map/ppermute | solution.py:200
  70.6 1.2 %collective-permute-start.11 = (f32[8,256]{1,0:T(8,128)S(1)}, f32[8,256]{1,0:T(8,128)S(1)}, u32[]{:S(2)}, u32[]{:S(2)}) collective-permute-start(f32[8,256]{1,0:T(8,128)S(1)} %get-tuple-element.24), channel_id=1, source_target_pairs={{0,1},{1,0},{2,3},{3,2},{4,5},{5,4},{6,7},{7,6},{8,9},{9,8},{10,11... | collective-permute-start | bytes 24584 | tf_op jit(solution)/shard_map/ppermute | solution.py:56
  71.8 11.2 %collective-permute-start.12 = (f32[16,256]{1,0:T(8,128)S(1)}, f32[16,256]{1,0:T(8,128)S(1)}, u32[]{:S(2)}, u32[]{:S(2)}) collective-permute-start(f32[16,256]{1,0:T(8,128)S(1)} %get-tuple-element.48), channel_id=1, source_target_pairs={{0,6},{2,0},{4,2},{6,4},{1,7},{3,1},{5,3},{7,5},{8,14},{10,8},{12,... | collective-permute-start | bytes 49160 | tf_op jit(solution)/shard_map/ppermute | solution.py:206
  74.8 18.2 %all-to-all-start.1 = ((f32[8,8,1280]{2,1,0:T(8,128)}), f32[8,8,1280]{2,1,0:T(8,128)S(1)}, u32[]{:S(2)}, u32[]{:S(2)}) async-start(f32[8,8,1280]{2,1,0:T(8,128)} %get-tuple-element.23), calls=%async_computation.1 | async-start | bytes 655360 | tf_op jit(solution)/shard_map/all_to_all | solution.py:420
  78.3 6.6 %collective-permute-start.14 = (f32[16,256]{1,0:T(8,128)S(1)}, f32[16,256]{1,0:T(8,128)S(1)}, u32[]{:S(2)}, u32[]{:S(2)}) collective-permute-start(f32[16,256]{1,0:T(8,128)S(1)} %get-tuple-element.48), channel_id=1, source_target_pairs={{0,2},{2,4},{4,6},{6,0},{1,3},{3,5},{5,7},{7,1},{8,10},{10,12},{12... | collective-permute-start | bytes 49160 | tf_op jit(solution)/shard_map/ppermute | solution.py:206
  78.4 6.4 %collective-permute-start.13 = (f32[16,256]{1,0:T(8,128)S(1)}, f32[16,256]{1,0:T(8,128)S(1)}, u32[]{:S(2)}, u32[]{:S(2)}) collective-permute-start(f32[16,256]{1,0:T(8,128)S(1)} %get-tuple-element.48), channel_id=1, source_target_pairs={{0,4},{2,6},{4,0},{6,2},{1,5},{3,7},{5,1},{7,3},{8,12},{10,14},{12... | collective-permute-start | bytes 49160 | tf_op jit(solution)/shard_map/ppermute | solution.py:206
  84.9 5.8 %collective-permute-start.15 = (f32[64,256]{1,0:T(8,128)S(1)}, f32[64,256]{1,0:T(8,128)S(1)}, u32[]{:S(2)}, u32[]{:S(2)}) collective-permute-start(f32[64,256]{1,0:T(8,128)S(1)} %get-tuple-element.40), channel_id=1, source_target_pairs={{0,24},{8,0},{16,8},{24,16},{1,25},{9,1},{17,9},{25,17},{2,26},{10... | collective-permute-start | bytes 196616 | tf_op jit(solution)/shard_map/ppermute | solution.py:206
  85.8 7.2 %collective-permute-start.17 = (f32[64,256]{1,0:T(8,128)S(1)}, f32[64,256]{1,0:T(8,128)S(1)}, u32[]{:S(2)}, u32[]{:S(2)}) collective-permute-start(f32[64,256]{1,0:T(8,128)S(1)} %get-tuple-element.40), channel_id=1, source_target_pairs={{0,8},{8,16},{16,24},{24,0},{1,9},{9,17},{17,25},{25,1},{2,10},{10... | collective-permute-start | bytes 196616 | tf_op jit(solution)/shard_map/ppermute | solution.py:206
  87.0 6.0 %collective-permute-start.16 = (f32[64,256]{1,0:T(8,128)S(1)}, f32[64,256]{1,0:T(8,128)S(1)}, u32[]{:S(2)}, u32[]{:S(2)}) collective-permute-start(f32[64,256]{1,0:T(8,128)S(1)} %get-tuple-element.40), channel_id=1, source_target_pairs={{0,16},{8,24},{16,0},{24,8},{1,17},{9,25},{17,1},{25,9},{2,18},{10... | collective-permute-start | bytes 196616 | tf_op jit(solution)/shard_map/ppermute | solution.py:206
  93.0 19.3 %collective-permute-start.20 = (f32[64,1280]{1,0:T(8,128)S(1)}, f32[64,1280]{1,0:T(8,128)S(1)}, u32[]{:S(2)}, u32[]{:S(2)}) collective-permute-start(f32[64,1280]{1,0:T(8,128)S(1)} %bitcast.15), channel_id=1, source_target_pairs={{0,8},{8,16},{16,24},{24,0},{1,9},{9,17},{17,25},{25,1},{2,10},{10... | collective-permute-start | bytes 983048 | tf_op jit(solution)/shard_map/ppermute | solution.py:206
  94.2 18.1 %collective-permute-start.19 = (f32[64,1280]{1,0:T(8,128)S(1)}, f32[64,1280]{1,0:T(8,128)S(1)}, u32[]{:S(2)}, u32[]{:S(2)}) collective-permute-start(f32[64,1280]{1,0:T(8,128)S(1)} %bitcast.16), channel_id=1, source_target_pairs={{0,16},{8,24},{16,0},{24,8},{1,17},{9,25},{17,1},{25,9},{2,18},{10... | collective-permute-start | bytes 983048 | tf_op jit(solution)/shard_map/ppermute | solution.py:206
  97.0 15.4 %collective-permute-start.18 = (f32[64,1280]{1,0:T(8,128)S(1)}, f32[64,1280]{1,0:T(8,128)S(1)}, u32[]{:S(2)}, u32[]{:S(2)}) collective-permute-start(f32[64,1280]{1,0:T(8,128)S(1)} %bitcast.17), channel_id=1, source_target_pairs={{0,24},{8,0},{16,8},{24,16},{1,25},{9,1},{17,9},{25,17},{2,26},{10... | collective-permute-start | bytes 983048 | tf_op jit(solution)/shard_map/ppermute | solution.py:206

commit v4 on v3

--- a/solution.py
+++ b/solution.py
@@ -301,11 +301,11 @@
 def factor_first_kernel(x_ref, y_ref, core_ref, p_ref, w_ref, l_ref, s_ref, g_ref):
     h = LANES
     for dy in range(NY):
-        for dx in range(NX):
-            for dc in range(NC):
+        for dc in range(NC):
+            for dx in range(NX):
                 x, y, core = (x_ref[0] + dx) % NX, (y_ref[0] + dy) % NY, (core_ref[0] + dc) % NC
                 at = pl.multiple_of(((x * NC + core) * NY + y) * SUB, SUB)
-                row = ((dy * NX + dx) * NC + dc) * SUB
+                row = ((dy * NC + dc) * NX + dx) * SUB
                 g_ref[pl.ds(at, SUB), :] = p_ref[row : row + SUB, :]
     invert_factor(g_ref[:h, :h], w_ref, 0, 0)
     l21 = dot(g_ref[h:, :h], w_ref[...], NT)
@@ -426,8 +426,8 @@
     *pieces, panels = products(relay(own), columns)
     copies, gram = sum_z(exchange_z(sum_y(deal(pieces, "y"))))
     part = exchange_z(copies).reshape(NZ * SUB, RIDE)
-    gram = jnp.concatenate([gram, swap(gram)], axis=0)
-    gram = collect(collect(gram, "x", NX), "y", NY)
+    gram = collect(gram, "x", NX)
+    gram = collect(jnp.concatenate([gram, swap(gram)], axis=0), "y", NY)
     part, gram = lax.optimization_barrier((part, gram))
     inverse, basis, resident = factor_last(*factor_first(gram), in_hbm(panels), columns)
     reduced, top = update(inverse, basis, every(part, "y", NY), resident)

time: 117 us -> 116 us (level)
    ppermute x9, waiting for transfers between devices: 4.13 us -> 2.25 us  [every(): lax.ppermute(values, axis, [(at, (at - by) % size) for at in range(size)])]
    all_to_all x1, waiting for transfers between devices: 0.01 us -> 1.74 us  [exchange_z(): return lax.all_to_all(pieces, 'z', 0, 0)]
where the time goes in v4:
time: 116 us
  starting transfers between devices  38.3 us (33%)
  waiting for transfers between devices  29.1 us (25%)
  Pallas kernels  22.9 us (20%)
  blocking collectives  22.4 us (19%)
    all_to_all x1, blocking collectives, exchange_z(): return lax.all_to_all(pieces, 'z', 0, 0)  22.4 us
    ppermute x9, starting transfers between devices, every(): lax.ppermute(values, axis, [(at, (at - by) % size) for at in range(size)])  19.3 us
    ppermute x3, waiting for transfers between devices, deal(): lax.ppermute(pieces[by], axis, [(at, (at + by) % size) for at in range(si...  15.4 us
    pallas_call x1, Pallas kernels, factor_last(): pl.pallas_call(factor_last_kernel, in_specs=[VMEM] * 3 + [HBM] * 2, out_s...  7.52 us
    pallas_call x1, Pallas kernels, factor_first(): pl.pallas_call(factor_first_kernel, in_specs=[SCALAR] * 3 + [VMEM], out_s...  5.56 us
    ppermute x3, starting transfers between devices, deal(): lax.ppermute(pieces[by], axis, [(at, (at + by) % size) for at in range(si...  5 us
    pallas_call x1, Pallas kernels, products(): pl.pallas_call(products_kernel, in_specs=[SCALAR] * 3 + [VMEM] * 4 + [HBM...  4.97 us
    ppermute x1, starting transfers between devices, relay(): down_high = lax.ppermute(high, 'x', [(0, 3)])  4.68 us
  transfers between devices with their start and end apart: 22, of which 11 were waited for; matrix products, arithmetic and copies ran while one was open for 0% of the time, Pallas kernels for 11%

profile of v4, /device:TPU:8, one launch (start us, length us, event | category | flops | bytes accessed | tf_op | source)
XLA Modules:
  0.0 115.9 jit_solution(2893812505268969011)
XLA Ops:
  0.6 1.1 slice_bitcast_fusion
  1.7 4.7 %collective-permute-start.4 = (f32[512,128]{1,0:T(8,128)S(1)}, f32[512,128]{1,0:T(8,128)S(1)}, u32[]{:S(2)}, u32[]{:S(2)}) collective-permute-start(f32[512,128]{1,0:T(8,128)S(1)} %get-tuple-element.38), channel_id=1, source_target_pairs={{0,6},{1,7},{8,14},{9,15},{16,22},{17,23},{24,30},{25,31},{32,38},... | collective-permute-start | bytes 786440 | tf_op jit(solution)/shard_map/ppermute | solution.py:64
  6.4 1.3 %collective-permute-start = (f32[512,128]{1,0:T(8,128)S(1)}, f32[512,128]{1,0:T(8,128)S(1)}, u32[]{:S(2)}, u32[]{:S(2)}) collective-permute-start(f32[512,128]{1,0:T(8,128)S(1)} %get-tuple-element.39), channel_id=1, source_target_pairs={{0,2},{1,3},{8,10},{9,11},{16,18},{17,19},{24,26},{25,27},{32,34},... | collective-permute-start | bytes 786440 | tf_op jit(solution)/shard_map/ppermute | solution.py:63
  7.7 1.3 %collective-permute-start.3 = (f32[512,128]{1,0:T(8,128)S(1)}, f32[512,128]{1,0:T(8,128)S(1)}, u32[]{:S(2)}, u32[]{:S(2)}) collective-permute-start(f32[512,128]{1,0:T(8,128)S(1)} %get-tuple-element.38), channel_id=1, source_target_pairs={{0,2},{1,3},{8,10},{9,11},{16,18},{17,19},{24,26},{25,27},{32,34},... | collective-permute-start | bytes 786440 | tf_op jit(solution)/shard_map/ppermute | solution.py:65
  9.0 1.3 %collective-permute-start.2 = (f32[512,128]{1,0:T(8,128)S(1)}, f32[512,128]{1,0:T(8,128)S(1)}, u32[]{:S(2)}, u32[]{:S(2)}) collective-permute-start(f32[512,128]{1,0:T(8,128)S(1)} %get-tuple-element.39), channel_id=1, source_target_pairs={{0,6},{1,7},{8,14},{9,15},{16,22},{17,23},{24,30},{25,31},{32,38},... | collective-permute-start | bytes 786440 | tf_op jit(solution)/shard_map/ppermute | solution.py:66
  10.3 2.7 %collective-permute-done.4 = f32[512,128]{1,0:T(8,128)S(1)} collective-permute-done((f32[512,128]{1,0:T(8,128)S(1)}, f32[512,128]{1,0:T(8,128)S(1)}, u32[]{:S(2)}, u32[]{:S(2)}) %collective-permute-start.4) | collective-permute-done | bytes 262176 | tf_op jit(solution)/shard_map/ppermute | solution.py:64
  13.1 0.7 collective-permute-start.5
  13.7 0.6 collective-permute-done
  14.4 0.7 collective-permute-start.1
  15.1 3.8 %collective-permute-done.3 = f32[512,128]{1,0:T(8,128)S(1)} collective-permute-done((f32[512,128]{1,0:T(8,128)S(1)}, f32[512,128]{1,0:T(8,128)S(1)}, u32[]{:S(2)}, u32[]{:S(2)}) %collective-permute-start.3) | collective-permute-done | bytes 262176 | tf_op jit(solution)/shard_map/ppermute | solution.py:65
  18.8 0.0 collective-permute-done.2
  18.9 0.0 collective-permute-done.5
  18.9 0.0 collective-permute-done.1
  18.9 1.1 select_select_fusion
  20.0 0.1 collective-permute-start.7
  20.1 0.5 collective-permute-start.6
  20.6 1.0 collective-permute-done.7.oh_ref
  21.6 0.4 collective-permute-done.6.ol_ref
  22.0 5.0 %products.1 = (f32[64,1408]{1,0:T(8,128)S(1)}, f32[64,1408]{1,0:T(8,128)S(1)}, f32[64,1408]{1,0:T(8,128)S(1)}, f32[64,1408]{1,0:T(8,128)S(1)}, f32[1024,256]{1,0:T(8,128)S(1)}) custom-call(s32[1]{0:T(128)} %bitcast.1.x_ref, s32[1]{0:T(128)} %bitcast.y_ref, s32[1]{0:T(128)} %bitcast.2.core_ref, f32[512,128]{1,0:T(8,128)S(1)} %get-tuple-element.37.ml_ref, ...), custom_call_target="tpu_custom_call" | custom-call | tf_op jit(solution)/shard_map/products/pallas_call | solution.py:137
  27.0 0.0 copy-start
  27.0 1.7 %collective-permute-start.8 = (f32[64,1408]{1,0:T(8,128)S(1)}, f32[64,1408]{1,0:T(8,128)S(1)}, u32[]{:S(2)}, u32[]{:S(2)}) collective-permute-start(f32[64,1408]{1,0:T(8,128)S(1)} %get-tuple-element.20), channel_id=1, source_target_pairs={{0,8},{8,16},{16,24},{24,0},{1,9},{9,17},{17,25},{25,1},{2,10},{10... | collective-permute-start | bytes 1081352 | tf_op jit(solution)/shard_map/ppermute | solution.py:200
  28.6 0.9 collective-permute-start.9
  29.6 2.4 %collective-permute-start.10 = (f32[64,1408]{1,0:T(8,128)S(1)}, f32[64,1408]{1,0:T(8,128)S(1)}, u32[]{:S(2)}, u32[]{:S(2)}) collective-permute-start(f32[64,1408]{1,0:T(8,128)S(1)} %get-tuple-element.22), channel_id=1, source_target_pairs={{0,24},{8,0},{16,8},{24,16},{1,25},{9,1},{17,9},{25,17},{2,26},{10... | collective-permute-start | bytes 1081352 | tf_op jit(solution)/shard_map/ppermute | solution.py:200
  32.0 6.3 %collective-permute-done.8.a1_ref = f32[64,1408]{1,0:T(8,128)S(1)} collective-permute-done((f32[64,1408]{1,0:T(8,128)S(1)}, f32[64,1408]{1,0:T(8,128)S(1)}, u32[]{:S(2)}, u32[]{:S(2)}) %collective-permute-start.8) | collective-permute-done | bytes 360480 | tf_op jit(solution)/shard_map/ppermute | solution.py:200
  38.3 3.1 %collective-permute-done.9.a2_ref = f32[64,1408]{1,0:T(8,128)S(1)} collective-permute-done((f32[64,1408]{1,0:T(8,128)S(1)}, f32[64,1408]{1,0:T(8,128)S(1)}, u32[]{:S(2)}, u32[]{:S(2)}) %collective-permute-start.9) | collective-permute-done | bytes 360480 | tf_op jit(solution)/shard_map/ppermute | solution.py:200
  41.4 5.9 %collective-permute-done.10.a3_ref = f32[64,1408]{1,0:T(8,128)S(1)} collective-permute-done((f32[64,1408]{1,0:T(8,128)S(1)}, f32[64,1408]{1,0:T(8,128)S(1)}, u32[]{:S(2)}, u32[]{:S(2)}) %collective-permute-start.10) | collective-permute-done | bytes 360480 | tf_op jit(solution)/shard_map/ppermute | solution.py:200
  47.4 0.1 sum_y.1
  47.4 22.4 %all_to_all.10.a_ref = f32[8,8,1536]{2,1,0:T(8,128)S(1)} all-to-all(f32[8,8,1536]{2,1,0:T(8,128)S(1)} %sum_y.1), channel_id=1, replica_groups=mesh['z'=8,'y'=4,'x'=4,'c'=2] {'z'}, dimensions={0} | all-to-all | bytes 786432 | tf_op jit(solution)/shard_map/all_to_all | solution.py:420
  69.8 0.8 sum_z.1
  70.6 0.0 copy-done
  70.6 3.2 %collective-permute-start.13 = (f32[8,256]{1,0:T(8,128)S(1)}, f32[8,256]{1,0:T(8,128)S(1)}, u32[]{:S(2)}, u32[]{:S(2)}) collective-permute-start(f32[8,256]{1,0:T(8,128)S(1)} %get-tuple-element.24), channel_id=1, source_target_pairs={{0,2},{2,4},{4,6},{6,0},{1,3},{3,5},{5,7},{7,1},{8,10},{10,12},{12... | collective-permute-start | bytes 24584 | tf_op jit(solution)/shard_map/ppermute | solution.py:206
  73.7 2.5 %collective-permute-start.12 = (f32[8,256]{1,0:T(8,128)S(1)}, f32[8,256]{1,0:T(8,128)S(1)}, u32[]{:S(2)}, u32[]{:S(2)}) collective-permute-start(f32[8,256]{1,0:T(8,128)S(1)} %get-tuple-element.24), channel_id=1, source_target_pairs={{0,4},{2,6},{4,0},{6,2},{1,5},{3,7},{5,1},{7,3},{8,12},{10,14},{12... | collective-permute-start | bytes 24584 | tf_op jit(solution)/shard_map/ppermute | solution.py:206
  76.3 2.6 %collective-permute-start.11 = (f32[8,256]{1,0:T(8,128)S(1)}, f32[8,256]{1,0:T(8,128)S(1)}, u32[]{:S(2)}, u32[]{:S(2)}) collective-permute-start(f32[8,256]{1,0:T(8,128)S(1)} %get-tuple-element.24), channel_id=1, source_target_pairs={{0,6},{2,0},{4,2},{6,4},{1,7},{3,1},{5,3},{7,5},{8,14},{10,8},{12,... | collective-permute-start | bytes 24584 | tf_op jit(solution)/shard_map/ppermute | solution.py:206
  78.9 3.4 %all-to-all-start.1 = ((f32[8,8,1280]{2,1,0:T(8,128)}), f32[8,8,1280]{2,1,0:T(8,128)S(1)}, u32[]{:S(2)}, u32[]{:S(2)}) async-start(f32[8,8,1280]{2,1,0:T(8,128)} %get-tuple-element.23), calls=%async_computation.1 | async-start | bytes 655360 | tf_op jit(solution)/shard_map/all_to_all | solution.py:420
  82.3 0.0 collective-permute-done.13
  82.4 0.0 collective-permute-done.12
  82.4 0.0 collective-permute-done.11
  82.4 0.1 collective-permute-start.14
  82.5 1.2 collective-permute-done.14
  83.7 0.8 collective-permute-start.15
  84.5 1.2 %collective-permute-start.17 = (f32[64,256]{1,0:T(8,128)S(1)}, f32[64,256]{1,0:T(8,128)S(1)}, u32[]{:S(2)}, u32[]{:S(2)}) collective-permute-start(f32[64,256]{1,0:T(8,128)S(1)} %get-tuple-element.40), channel_id=1, source_target_pairs={{0,8},{8,16},{16,24},{24,0},{1,9},{9,17},{17,25},{25,1},{2,10},{10... | collective-permute-start | bytes 196616 | tf_op jit(solution)/shard_map/ppermute | solution.py:206
  85.7 3.7 %collective-permute-start.16 = (f32[64,256]{1,0:T(8,128)S(1)}, f32[64,256]{1,0:T(8,128)S(1)}, u32[]{:S(2)}, u32[]{:S(2)}) collective-permute-start(f32[64,256]{1,0:T(8,128)S(1)} %get-tuple-element.40), channel_id=1, source_target_pairs={{0,16},{8,24},{16,0},{24,8},{1,17},{9,25},{17,1},{25,9},{2,18},{10... | collective-permute-start | bytes 196616 | tf_op jit(solution)/shard_map/ppermute | solution.py:206
  89.4 0.0 collective-permute-done.15
  89.4 2.2 %collective-permute-done.16 = f32[64,256]{1,0:T(8,128)S(1)} collective-permute-done((f32[64,256]{1,0:T(8,128)S(1)}, f32[64,256]{1,0:T(8,128)S(1)}, u32[]{:S(2)}, u32[]{:S(2)}) %collective-permute-start.16) | collective-permute-done | bytes 65568 | tf_op jit(solution)/shard_map/ppermute | solution.py:206
  91.7 0.0 collective-permute-done.17
  91.7 1.7 %all-to-all-done.1 = f32[8,8,1280]{2,1,0:T(8,128)S(1)} async-done(((f32[8,8,1280]{2,1,0:T(8,128)}), f32[8,8,1280]{2,1,0:T(8,128)S(1)}, u32[]{:S(2)}, u32[]{:S(2)}) %all-to-all-start.1) | async-done | bytes 327712 | tf_op jit(solution)/shard_map/all_to_all | solution.py:420
  93.4 1.0 collective-permute-start.20
  94.5 1.8 %collective-permute-start.19 = (f32[64,1280]{1,0:T(8,128)S(1)}, f32[64,1280]{1,0:T(8,128)S(1)}, u32[]{:S(2)}, u32[]{:S(2)}) collective-permute-start(f32[64,1280]{1,0:T(8,128)S(1)} %bitcast.16), channel_id=1, source_target_pairs={{0,16},{8,24},{16,0},{24,8},{1,17},{9,25},{17,1},{25,9},{2,18},{10... | collective-permute-start | bytes 983048 | tf_op jit(solution)/shard_map/ppermute | solution.py:206
  96.3 2.3 %collective-permute-start.18 = (f32[64,1280]{1,0:T(8,128)S(1)}, f32[64,1280]{1,0:T(8,128)S(1)}, u32[]{:S(2)}, u32[]{:S(2)}) collective-permute-start(f32[64,1280]{1,0:T(8,128)S(1)} %bitcast.17), channel_id=1, source_target_pairs={{0,24},{8,0},{16,8},{24,16},{1,25},{9,1},{17,9},{25,17},{2,26},{10... | collective-permute-start | bytes 983048 | tf_op jit(solution)/shard_map/ppermute | solution.py:206
  98.7 5.6 %factor_first.1 = (f32[128,128]{1,0:T(8,128)S(1)}, f32[128,128]{1,0:T(8,128)S(1)}, f32[128,128]{1,0:T(8,128)S(1)}) custom-call(s32[1]{0:T(128)} %bitcast.1.x_ref, s32[1]{0:T(128)} %bitcast.y_ref, s32[1]{0:T(128)} %bitcast.2.core_ref, f32[256,256]{1,0:T(8,128)S(1)} %constant_dynamic-update-slice_fusion.5.p_ref), custom_call_target="tpu_custom_call" | custom-call | tf_op jit(solution)/shard_map/factor_first/pallas_call | solution.py:338
  104.2 7.5 %factor_last.1 = (f32[256,256]{1,0:T(8,128)S(1)}, bf16[1024,768]{1,0:T(8,128)(2,1)S(1)}, f32[10,1024,128]{2,1,0:T(8,128)S(1)}) custom-call(f32[128,128]{1,0:T(8,128)S(1)} %get-tuple-element.26.w11_ref, f32[128,128]{1,0:T(8,128)S(1)} %get-tuple-element.27.l_ref, f32[128,128]{1,0:T(8,128)S(1)} %get-tuple-element.28.s_ref, f32[1024,256]{1,0:T(8,128)} %copy-done, ...), custom_call_target="tpu_custom_call" | custom-call | tf_op jit(solution)/shard_map/factor_last/pallas_call | solution.py:351
  111.7 0.0 collective-permute-done.20.x3_ref
  111.8 0.0 collective-permute-done.19.x2_ref
  111.8 0.0 collective-permute-done.18.x1_ref
  111.8 4.0 %update.1 = (f32[10,1024,128]{2,1,0:T(8,128)}, f32[10,256,128]{2,1,0:T(8,128)}) custom-call(s32[1]{0:T(128)} %bitcast.y_ref, f32[256,256]{1,0:T(8,128)S(1)} %get-tuple-element.30.w_ref, bf16[1024,768]{1,0:T(8,128)(2,1)S(1)} %get-tuple-element.31.q_ref, f32[64,1280]{1,0:T(8,128)S(1)} %bitcast.18, f32[64,1280]{1,0:T(8,128)S(1)} %collective-permute-done.18.x1_ref, ...), custom_call_target="tpu_custom_call" | custom-call | tf_op jit(solution)/shard_map/update/pallas_call | solution.py:402
  (9 shorter events, 0.0 us)
Async XLA Ops:
  1.7 11.4 %collective-permute-start.4 = (f32[512,128]{1,0:T(8,128)S(1)}, f32[512,128]{1,0:T(8,128)S(1)}, u32[]{:S(2)}, u32[]{:S(2)}) collective-permute-start(f32[512,128]{1,0:T(8,128)S(1)} %get-tuple-element.38), channel_id=1, source_target_pairs={{0,6},{1,7},{8,14},{9,15},{16,22},{17,23},{24,30},{25,31},{32,38},... | collective-permute-start | bytes 786440 | tf_op jit(solution)/shard_map/ppermute | solution.py:64
  6.4 8.0 %collective-permute-start = (f32[512,128]{1,0:T(8,128)S(1)}, f32[512,128]{1,0:T(8,128)S(1)}, u32[]{:S(2)}, u32[]{:S(2)}) collective-permute-start(f32[512,128]{1,0:T(8,128)S(1)} %get-tuple-element.39), channel_id=1, source_target_pairs={{0,2},{1,3},{8,10},{9,11},{16,18},{17,19},{24,26},{25,27},{32,34},... | collective-permute-start | bytes 786440 | tf_op jit(solution)/shard_map/ppermute | solution.py:63
  7.7 11.1 %collective-permute-start.3 = (f32[512,128]{1,0:T(8,128)S(1)}, f32[512,128]{1,0:T(8,128)S(1)}, u32[]{:S(2)}, u32[]{:S(2)}) collective-permute-start(f32[512,128]{1,0:T(8,128)S(1)} %get-tuple-element.38), channel_id=1, source_target_pairs={{0,2},{1,3},{8,10},{9,11},{16,18},{17,19},{24,26},{25,27},{32,34},... | collective-permute-start | bytes 786440 | tf_op jit(solution)/shard_map/ppermute | solution.py:65
  9.0 9.8 %collective-permute-start.2 = (f32[512,128]{1,0:T(8,128)S(1)}, f32[512,128]{1,0:T(8,128)S(1)}, u32[]{:S(2)}, u32[]{:S(2)}) collective-permute-start(f32[512,128]{1,0:T(8,128)S(1)} %get-tuple-element.39), channel_id=1, source_target_pairs={{0,6},{1,7},{8,14},{9,15},{16,22},{17,23},{24,30},{25,31},{32,38},... | collective-permute-start | bytes 786440 | tf_op jit(solution)/shard_map/ppermute | solution.py:66
  13.1 5.8 %collective-permute-start.5 = (f32[512,128]{1,0:T(8,128)S(1)}, f32[512,128]{1,0:T(8,128)S(1)}, u32[]{:S(2)}, u32[]{:S(2)}) collective-permute-start(f32[512,128]{1,0:T(8,128)S(1)} %collective-permute-done.4), channel_id=1, source_target_pairs={{6,4},{7,5},{14,12},{15,13},{22,20},{23,21},{30,28},{31,29},{38,36... | collective-permute-start | bytes 786440 | tf_op jit(solution)/shard_map/ppermute | solution.py:68
  14.4 4.5 %collective-permute-start.1 = (f32[512,128]{1,0:T(8,128)S(1)}, f32[512,128]{1,0:T(8,128)S(1)}, u32[]{:S(2)}, u32[]{:S(2)}) collective-permute-start(f32[512,128]{1,0:T(8,128)S(1)} %collective-permute-done), channel_id=1, source_target_pairs={{2,4},{3,5},{10,12},{11,13},{18,20},{19,21},{26,28},{27,29},{34,36... | collective-permute-start | bytes 786440 | tf_op jit(solution)/shard_map/ppermute | solution.py:67
  20.0 1.6 %collective-permute-start.7 = (f32[512,128]{1,0:T(8,128)S(1)}, f32[512,128]{1,0:T(8,128)S(1)}, u32[]{:S(2)}, u32[]{:S(2)}) collective-permute-start(f32[512,128]{1,0:T(8,128)S(1)} %get-tuple-element.36.mh_ref), channel_id=1, source_target_pairs={{0,1},{1,0},{2,3},{3,2},{4,5},{5,4},{6,7},{7,6},{8,9},{9,8},{10,11... | collective-permute-start | bytes 786440 | tf_op jit(solution)/shard_map/ppermute | solution.py:56
  20.1 1.9 %collective-permute-start.6 = (f32[512,128]{1,0:T(8,128)S(1)}, f32[512,128]{1,0:T(8,128)S(1)}, u32[]{:S(2)}, u32[]{:S(2)}) collective-permute-start(f32[512,128]{1,0:T(8,128)S(1)} %get-tuple-element.37.ml_ref), channel_id=1, source_target_pairs={{0,1},{1,0},{2,3},{3,2},{4,5},{5,4},{6,7},{7,6},{8,9},{9,8},{10,11... | collective-permute-start | bytes 786440 | tf_op jit(solution)/shard_map/ppermute | solution.py:56
  27.0 43.6 %copy-start = (f32[1024,256]{1,0:T(8,128)}, f32[1024,256]{1,0:T(8,128)S(1)}, u32[]{:S(2)}) copy-start(f32[1024,256]{1,0:T(8,128)S(1)} %get-tuple-element.29.p_hbm) | copy-start | bytes 3145732
  27.0 11.3 %collective-permute-start.8 = (f32[64,1408]{1,0:T(8,128)S(1)}, f32[64,1408]{1,0:T(8,128)S(1)}, u32[]{:S(2)}, u32[]{:S(2)}) collective-permute-start(f32[64,1408]{1,0:T(8,128)S(1)} %get-tuple-element.20), channel_id=1, source_target_pairs={{0,8},{8,16},{16,24},{24,0},{1,9},{9,17},{17,25},{25,1},{2,10},{10... | collective-permute-start | bytes 1081352 | tf_op jit(solution)/shard_map/ppermute | solution.py:200
  28.6 12.8 %collective-permute-start.9 = (f32[64,1408]{1,0:T(8,128)S(1)}, f32[64,1408]{1,0:T(8,128)S(1)}, u32[]{:S(2)}, u32[]{:S(2)}) collective-permute-start(f32[64,1408]{1,0:T(8,128)S(1)} %get-tuple-element.21), channel_id=1, source_target_pairs={{0,16},{8,24},{16,0},{24,8},{1,17},{9,25},{17,1},{25,9},{2,18},{10... | collective-permute-start | bytes 1081352 | tf_op jit(solution)/shard_map/ppermute | solution.py:200
  29.6 17.8 %collective-permute-start.10 = (f32[64,1408]{1,0:T(8,128)S(1)}, f32[64,1408]{1,0:T(8,128)S(1)}, u32[]{:S(2)}, u32[]{:S(2)}) collective-permute-start(f32[64,1408]{1,0:T(8,128)S(1)} %get-tuple-element.22), channel_id=1, source_target_pairs={{0,24},{8,0},{16,8},{24,16},{1,25},{9,1},{17,9},{25,17},{2,26},{10... | collective-permute-start | bytes 1081352 | tf_op jit(solution)/shard_map/ppermute | solution.py:200
  70.6 11.8 %collective-permute-start.13 = (f32[8,256]{1,0:T(8,128)S(1)}, f32[8,256]{1,0:T(8,128)S(1)}, u32[]{:S(2)}, u32[]{:S(2)}) collective-permute-start(f32[8,256]{1,0:T(8,128)S(1)} %get-tuple-element.24), channel_id=1, source_target_pairs={{0,2},{2,4},{4,6},{6,0},{1,3},{3,5},{5,7},{7,1},{8,10},{10,12},{12... | collective-permute-start | bytes 24584 | tf_op jit(solution)/shard_map/ppermute | solution.py:206
  73.7 8.6 %collective-permute-start.12 = (f32[8,256]{1,0:T(8,128)S(1)}, f32[8,256]{1,0:T(8,128)S(1)}, u32[]{:S(2)}, u32[]{:S(2)}) collective-permute-start(f32[8,256]{1,0:T(8,128)S(1)} %get-tuple-element.24), channel_id=1, source_target_pairs={{0,4},{2,6},{4,0},{6,2},{1,5},{3,7},{5,1},{7,3},{8,12},{10,14},{12... | collective-permute-start | bytes 24584 | tf_op jit(solution)/shard_map/ppermute | solution.py:206
  76.3 6.1 %collective-permute-start.11 = (f32[8,256]{1,0:T(8,128)S(1)}, f32[8,256]{1,0:T(8,128)S(1)}, u32[]{:S(2)}, u32[]{:S(2)}) collective-permute-start(f32[8,256]{1,0:T(8,128)S(1)} %get-tuple-element.24), channel_id=1, source_target_pairs={{0,6},{2,0},{4,2},{6,4},{1,7},{3,1},{5,3},{7,5},{8,14},{10,8},{12,... | collective-permute-start | bytes 24584 | tf_op jit(solution)/shard_map/ppermute | solution.py:206
  78.9 14.5 %all-to-all-start.1 = ((f32[8,8,1280]{2,1,0:T(8,128)}), f32[8,8,1280]{2,1,0:T(8,128)S(1)}, u32[]{:S(2)}, u32[]{:S(2)}) async-start(f32[8,8,1280]{2,1,0:T(8,128)} %get-tuple-element.23), calls=%async_computation.1 | async-start | bytes 655360 | tf_op jit(solution)/shard_map/all_to_all | solution.py:420
  82.4 1.3 %collective-permute-start.14 = (f32[32,256]{1,0:T(8,128)S(1)}, f32[32,256]{1,0:T(8,128)S(1)}, u32[]{:S(2)}, u32[]{:S(2)}) collective-permute-start(f32[32,256]{1,0:T(8,128)S(1)} %pad_maximum_fusion), channel_id=1, source_target_pairs={{0,1},{1,0},{2,3},{3,2},{4,5},{5,4},{6,7},{7,6},{8,9},{9,8},{10,11... | collective-permute-start | bytes 98312 | tf_op jit(solution)/shard_map/ppermute | solution.py:56
  83.7 5.7 %collective-permute-start.15 = (f32[64,256]{1,0:T(8,128)S(1)}, f32[64,256]{1,0:T(8,128)S(1)}, u32[]{:S(2)}, u32[]{:S(2)}) collective-permute-start(f32[64,256]{1,0:T(8,128)S(1)} %get-tuple-element.40), channel_id=1, source_target_pairs={{0,24},{8,0},{16,8},{24,16},{1,25},{9,1},{17,9},{25,17},{2,26},{10... | collective-permute-start | bytes 196616 | tf_op jit(solution)/shard_map/ppermute | solution.py:206
  84.5 7.2 %collective-permute-start.17 = (f32[64,256]{1,0:T(8,128)S(1)}, f32[64,256]{1,0:T(8,128)S(1)}, u32[]{:S(2)}, u32[]{:S(2)}) collective-permute-start(f32[64,256]{1,0:T(8,128)S(1)} %get-tuple-element.40), channel_id=1, source_target_pairs={{0,8},{8,16},{16,24},{24,0},{1,9},{9,17},{17,25},{25,1},{2,10},{10... | collective-permute-start | bytes 196616 | tf_op jit(solution)/shard_map/ppermute | solution.py:206
  85.7 6.0 %collective-permute-start.16 = (f32[64,256]{1,0:T(8,128)S(1)}, f32[64,256]{1,0:T(8,128)S(1)}, u32[]{:S(2)}, u32[]{:S(2)}) collective-permute-start(f32[64,256]{1,0:T(8,128)S(1)} %get-tuple-element.40), channel_id=1, source_target_pairs={{0,16},{8,24},{16,0},{24,8},{1,17},{9,25},{17,1},{25,9},{2,18},{10... | collective-permute-start | bytes 196616 | tf_op jit(solution)/shard_map/ppermute | solution.py:206
  93.4 18.3 %collective-permute-start.20 = (f32[64,1280]{1,0:T(8,128)S(1)}, f32[64,1280]{1,0:T(8,128)S(1)}, u32[]{:S(2)}, u32[]{:S(2)}) collective-permute-start(f32[64,1280]{1,0:T(8,128)S(1)} %bitcast.15), channel_id=1, source_target_pairs={{0,8},{8,16},{16,24},{24,0},{1,9},{9,17},{17,25},{25,1},{2,10},{10... | collective-permute-start | bytes 983048 | tf_op jit(solution)/shard_map/ppermute | solution.py:206
  94.5 17.3 %collective-permute-start.19 = (f32[64,1280]{1,0:T(8,128)S(1)}, f32[64,1280]{1,0:T(8,128)S(1)}, u32[]{:S(2)}, u32[]{:S(2)}) collective-permute-start(f32[64,1280]{1,0:T(8,128)S(1)} %bitcast.16), channel_id=1, source_target_pairs={{0,16},{8,24},{16,0},{24,8},{1,17},{9,25},{17,1},{25,9},{2,18},{10... | collective-permute-start | bytes 983048 | tf_op jit(solution)/shard_map/ppermute | solution.py:206
  96.3 15.5 %collective-permute-start.18 = (f32[64,1280]{1,0:T(8,128)S(1)}, f32[64,1280]{1,0:T(8,128)S(1)}, u32[]{:S(2)}, u32[]{:S(2)}) collective-permute-start(f32[64,1280]{1,0:T(8,128)S(1)} %bitcast.17), channel_id=1, source_target_pairs={{0,24},{8,0},{16,8},{24,16},{1,25},{9,1},{17,9},{25,17},{2,26},{10... | collective-permute-start | bytes 983048 | tf_op jit(solution)/shard_map/ppermute | solution.py:206

commit v5 on v4

--- a/solution.py
+++ b/solution.py
@@ -298,7 +298,11 @@
             w_ref[row0 + j + k : row0 + j + k + 1, col0 : col0 + LANES] = w[0:1]
 
 
-def factor_first_kernel(x_ref, y_ref, core_ref, p_ref, w_ref, l_ref, s_ref, g_ref):
+def factor_kernel(x_ref, y_ref, core_ref, pieces_ref, p_hbm, c_hbm, w_ref, q_ref, c_ref, g_ref, p_ref, sem, c_sem):
+    arriving = pltpu.make_async_copy(p_hbm, p_ref, sem)
+    arriving.start()
+    resident = pltpu.make_async_copy(c_hbm, c_ref, c_sem)
+    resident.start()
     h = LANES
     for dy in range(NY):
         for dc in range(NC):
@@ -306,51 +310,26 @@
                 x, y, core = (x_ref[0] + dx) % NX, (y_ref[0] + dy) % NY, (core_ref[0] + dc) % NC
                 at = pl.multiple_of(((x * NC + core) * NY + y) * SUB, SUB)
                 row = ((dy * NC + dc) * NX + dx) * SUB
-                g_ref[pl.ds(at, SUB), :] = p_ref[row : row + SUB, :]
+                g_ref[pl.ds(at, SUB), :] = pieces_ref[row : row + SUB, :]
     invert_factor(g_ref[:h, :h], w_ref, 0, 0)
-    l21 = dot(g_ref[h:, :h], w_ref[...], NT)
-    l_ref[...] = l21
-    s_ref[...] = g_ref[h:, h:] - dot(l21, l21, NT)
-
-
-def factor_last_kernel(w11_ref, l_ref, s_ref, p_hbm, c_hbm, w_ref, q_ref, c_ref, p_ref, sem, c_sem):
-    arriving = pltpu.make_async_copy(p_hbm, p_ref, sem)
-    arriving.start()
-    resident = pltpu.make_async_copy(c_hbm, c_ref, c_sem)
-    resident.start()
-    h = LANES
-    w11 = w11_ref[...]
-    w_ref[:h, :h] = w11
     w_ref[:h, h:] = jnp.zeros((h, h), jnp.float32)
-    invert_factor(s_ref[...], w_ref, h, h)
-    w_ref[h:, :h] = -dot(w_ref[h:, h:], dot(l_ref[...], w11))
-    arriving.wait()
+    w11 = w_ref[:h, :h]
+    l21 = dot(g_ref[h:, :h], w11, NT)
+    invert_factor(g_ref[h:, h:] - dot(l21, l21, NT), w_ref, h, h)
+    w_ref[h:, :h] = -dot(w_ref[h:, h:], dot(l21, w11))
     high, low = split(w_ref[...])
     right = jnp.concatenate([high, low, high], axis=1)
+    arriving.wait()
     basis = lax.dot_general(wide_left(p_ref[...]), right, NT, preferred_element_type=jnp.float32)
     q_ref[...] = wide_left(basis)
     resident.wait()
 
 
-def factor_first(pieces):
-    w = pieces.shape[0]
-    h = w // 2
-    return pl.pallas_call(
-        factor_first_kernel,
-        in_specs=[SCALAR] * 3 + [VMEM],
-        out_specs=[VMEM] * 3,
-        out_shape=[jax.ShapeDtypeStruct((h, h), jnp.float32)] * 3,
-        scratch_shapes=[pltpu.VMEM((w, w), jnp.float32)],
-        compiler_params=params(8),
-        name="factor_first",
-    )(index_of("x"), index_of("y"), index_of("c"), pieces)
-
-
-def factor_last(w11, l21, schur, panels, columns):
+def factor(pieces, panels, columns):
     n, w = panels.shape
     return pl.pallas_call(
-        factor_last_kernel,
-        in_specs=[VMEM] * 3 + [HBM] * 2,
+        factor_kernel,
+        in_specs=[SCALAR] * 3 + [VMEM] + [HBM] * 2,
         out_specs=[VMEM] * 3,
         out_shape=[
             jax.ShapeDtypeStruct((w, w), jnp.float32),
@@ -358,13 +337,14 @@
             jax.ShapeDtypeStruct(columns.shape, jnp.float32),
         ],
         scratch_shapes=[
+            pltpu.VMEM((w, w), jnp.float32),
             pltpu.VMEM((n, w), jnp.float32),
             pltpu.SemaphoreType.DMA(()),
             pltpu.SemaphoreType.DMA(()),
         ],
         compiler_params=params(12),
-        name="factor_last",
-    )(w11, l21, schur, panels, columns)
+        name="factor",
+    )(index_of("x"), index_of("y"), index_of("c"), pieces, panels, columns)
 
 
 BAND = 256
@@ -429,7 +409,7 @@
     gram = collect(gram, "x", NX)
     gram = collect(jnp.concatenate([gram, swap(gram)], axis=0), "y", NY)
     part, gram = lax.optimization_barrier((part, gram))
-    inverse, basis, resident = factor_last(*factor_first(gram), in_hbm(panels), columns)
+    inverse, basis, resident = factor(gram, in_hbm(panels), columns)
     reduced, top = update(inverse, basis, every(part, "y", NY), resident)
     return jnp.transpose(reduced, (1, 0, 2)), jnp.transpose(top, (1, 0, 2))
 

time: 116 us -> 116 us (level)
    pallas_call x2 -> x1, Pallas kernels: 13.1 us -> 13.1 us  [factor(): pl.pallas_call(factor_kernel, in_specs=[SCALAR] * 3 + [VMEM] + [HBM] * 2,...]
where the time goes in v5:
time: 116 us
  starting transfers between devices  38.3 us (33%)
  waiting for transfers between devices  29.1 us (25%)
  Pallas kernels  22.9 us (20%)
  blocking collectives  22.4 us (19%)
    all_to_all x1, blocking collectives, exchange_z(): return lax.all_to_all(pieces, 'z', 0, 0)  22.4 us
    ppermute x9, starting transfers between devices, every(): lax.ppermute(values, axis, [(at, (at - by) % size) for at in range(size)])  19.3 us
    ppermute x3, waiting for transfers between devices, deal(): lax.ppermute(pieces[by], axis, [(at, (at + by) % size) for at in range(si...  15.4 us
    pallas_call x1, Pallas kernels, factor(): pl.pallas_call(factor_kernel, in_specs=[SCALAR] * 3 + [VMEM] + [HBM] * 2,...  13.1 us
    ppermute x3, starting transfers between devices, deal(): lax.ppermute(pieces[by], axis, [(at, (at + by) % size) for at in range(si...  5 us
    pallas_call x1, Pallas kernels, products(): pl.pallas_call(products_kernel, in_specs=[SCALAR] * 3 + [VMEM] * 4 + [HBM...  4.97 us
    ppermute x1, starting transfers between devices, relay(): down_high = lax.ppermute(high, 'x', [(0, 3)])  4.68 us
    pallas_call x1, Pallas kernels, update(): pl.pallas_call(update_kernel, in_specs=[SCALAR] + [VMEM] * (3 + NY), out_...  3.98 us
  transfers between devices with their start and end apart: 22, of which 11 were waited for; matrix products, arithmetic and copies ran while one was open for 0% of the time, Pallas kernels for 11%

profile of v5, /device:TPU:8, one launch (start us, length us, event | category | flops | bytes accessed | tf_op | source)
XLA Modules:
  0.0 116.0 jit_solution(17934206472858175775)
XLA Ops:
  0.6 1.1 slice_bitcast_fusion
  1.7 4.7 %collective-permute-start.4 = (f32[512,128]{1,0:T(8,128)S(1)}, f32[512,128]{1,0:T(8,128)S(1)}, u32[]{:S(2)}, u32[]{:S(2)}) collective-permute-start(f32[512,128]{1,0:T(8,128)S(1)} %get-tuple-element.32), channel_id=1, source_target_pairs={{0,6},{1,7},{8,14},{9,15},{16,22},{17,23},{24,30},{25,31},{32,38},... | collective-permute-start | bytes 786440 | tf_op jit(solution)/shard_map/ppermute | solution.py:64
  6.4 1.3 %collective-permute-start = (f32[512,128]{1,0:T(8,128)S(1)}, f32[512,128]{1,0:T(8,128)S(1)}, u32[]{:S(2)}, u32[]{:S(2)}) collective-permute-start(f32[512,128]{1,0:T(8,128)S(1)} %get-tuple-element.33), channel_id=1, source_target_pairs={{0,2},{1,3},{8,10},{9,11},{16,18},{17,19},{24,26},{25,27},{32,34},... | collective-permute-start | bytes 786440 | tf_op jit(solution)/shard_map/ppermute | solution.py:63
  7.7 1.3 %collective-permute-start.3 = (f32[512,128]{1,0:T(8,128)S(1)}, f32[512,128]{1,0:T(8,128)S(1)}, u32[]{:S(2)}, u32[]{:S(2)}) collective-permute-start(f32[512,128]{1,0:T(8,128)S(1)} %get-tuple-element.32), channel_id=1, source_target_pairs={{0,2},{1,3},{8,10},{9,11},{16,18},{17,19},{24,26},{25,27},{32,34},... | collective-permute-start | bytes 786440 | tf_op jit(solution)/shard_map/ppermute | solution.py:65
  9.0 1.3 %collective-permute-start.2 = (f32[512,128]{1,0:T(8,128)S(1)}, f32[512,128]{1,0:T(8,128)S(1)}, u32[]{:S(2)}, u32[]{:S(2)}) collective-permute-start(f32[512,128]{1,0:T(8,128)S(1)} %get-tuple-element.33), channel_id=1, source_target_pairs={{0,6},{1,7},{8,14},{9,15},{16,22},{17,23},{24,30},{25,31},{32,38},... | collective-permute-start | bytes 786440 | tf_op jit(solution)/shard_map/ppermute | solution.py:66
  10.3 2.7 %collective-permute-done.4 = f32[512,128]{1,0:T(8,128)S(1)} collective-permute-done((f32[512,128]{1,0:T(8,128)S(1)}, f32[512,128]{1,0:T(8,128)S(1)}, u32[]{:S(2)}, u32[]{:S(2)}) %collective-permute-start.4) | collective-permute-done | bytes 262176 | tf_op jit(solution)/shard_map/ppermute | solution.py:64
  13.1 0.7 collective-permute-start.5
  13.7 0.6 collective-permute-done
  14.4 0.7 collective-permute-start.1
  15.1 3.8 %collective-permute-done.3 = f32[512,128]{1,0:T(8,128)S(1)} collective-permute-done((f32[512,128]{1,0:T(8,128)S(1)}, f32[512,128]{1,0:T(8,128)S(1)}, u32[]{:S(2)}, u32[]{:S(2)}) %collective-permute-start.3) | collective-permute-done | bytes 262176 | tf_op jit(solution)/shard_map/ppermute | solution.py:65
  18.8 0.0 collective-permute-done.2
  18.9 0.0 collective-permute-done.5
  18.9 0.0 collective-permute-done.1
  18.9 1.1 select_select_fusion
  20.0 0.1 collective-permute-start.7
  20.1 0.5 collective-permute-start.6
  20.6 1.0 collective-permute-done.7.oh_ref
  21.6 0.4 collective-permute-done.6.ol_ref
  22.0 5.0 %products.1 = (f32[64,1408]{1,0:T(8,128)S(1)}, f32[64,1408]{1,0:T(8,128)S(1)}, f32[64,1408]{1,0:T(8,128)S(1)}, f32[64,1408]{1,0:T(8,128)S(1)}, f32[1024,256]{1,0:T(8,128)S(1)}) custom-call(s32[1]{0:T(128)} %bitcast.1.x_ref, s32[1]{0:T(128)} %bitcast.y_ref, s32[1]{0:T(128)} %bitcast.2.core_ref, f32[512,128]{1,0:T(8,128)S(1)} %get-tuple-element.31.ml_ref, ...), custom_call_target="tpu_custom_call" | custom-call | tf_op jit(solution)/shard_map/products/pallas_call | solution.py:137
  27.0 0.0 copy-start
  27.0 1.7 %collective-permute-start.8 = (f32[64,1408]{1,0:T(8,128)S(1)}, f32[64,1408]{1,0:T(8,128)S(1)}, u32[]{:S(2)}, u32[]{:S(2)}) collective-permute-start(f32[64,1408]{1,0:T(8,128)S(1)} %get-tuple-element.17), channel_id=1, source_target_pairs={{0,8},{8,16},{16,24},{24,0},{1,9},{9,17},{17,25},{25,1},{2,10},{10... | collective-permute-start | bytes 1081352 | tf_op jit(solution)/shard_map/ppermute | solution.py:200
  28.6 0.9 collective-permute-start.9
  29.6 2.4 %collective-permute-start.10 = (f32[64,1408]{1,0:T(8,128)S(1)}, f32[64,1408]{1,0:T(8,128)S(1)}, u32[]{:S(2)}, u32[]{:S(2)}) collective-permute-start(f32[64,1408]{1,0:T(8,128)S(1)} %get-tuple-element.19), channel_id=1, source_target_pairs={{0,24},{8,0},{16,8},{24,16},{1,25},{9,1},{17,9},{25,17},{2,26},{10... | collective-permute-start | bytes 1081352 | tf_op jit(solution)/shard_map/ppermute | solution.py:200
  32.0 6.3 %collective-permute-done.8.a1_ref = f32[64,1408]{1,0:T(8,128)S(1)} collective-permute-done((f32[64,1408]{1,0:T(8,128)S(1)}, f32[64,1408]{1,0:T(8,128)S(1)}, u32[]{:S(2)}, u32[]{:S(2)}) %collective-permute-start.8) | collective-permute-done | bytes 360480 | tf_op jit(solution)/shard_map/ppermute | solution.py:200
  38.3 3.1 %collective-permute-done.9.a2_ref = f32[64,1408]{1,0:T(8,128)S(1)} collective-permute-done((f32[64,1408]{1,0:T(8,128)S(1)}, f32[64,1408]{1,0:T(8,128)S(1)}, u32[]{:S(2)}, u32[]{:S(2)}) %collective-permute-start.9) | collective-permute-done | bytes 360480 | tf_op jit(solution)/shard_map/ppermute | solution.py:200
  41.4 5.9 %collective-permute-done.10.a3_ref = f32[64,1408]{1,0:T(8,128)S(1)} collective-permute-done((f32[64,1408]{1,0:T(8,128)S(1)}, f32[64,1408]{1,0:T(8,128)S(1)}, u32[]{:S(2)}, u32[]{:S(2)}) %collective-permute-start.10) | collective-permute-done | bytes 360480 | tf_op jit(solution)/shard_map/ppermute | solution.py:200
  47.4 0.1 sum_y.1
  47.4 22.4 %all_to_all.10.a_ref = f32[8,8,1536]{2,1,0:T(8,128)S(1)} all-to-all(f32[8,8,1536]{2,1,0:T(8,128)S(1)} %sum_y.1), channel_id=1, replica_groups=mesh['z'=8,'y'=4,'x'=4,'c'=2] {'z'}, dimensions={0} | all-to-all | bytes 786432 | tf_op jit(solution)/shard_map/all_to_all | solution.py:400
  69.8 0.8 sum_z.1
  70.6 0.0 copy-done
  70.6 3.2 %collective-permute-start.13 = (f32[8,256]{1,0:T(8,128)S(1)}, f32[8,256]{1,0:T(8,128)S(1)}, u32[]{:S(2)}, u32[]{:S(2)}) collective-permute-start(f32[8,256]{1,0:T(8,128)S(1)} %get-tuple-element.21), channel_id=1, source_target_pairs={{0,2},{2,4},{4,6},{6,0},{1,3},{3,5},{5,7},{7,1},{8,10},{10,12},{12... | collective-permute-start | bytes 24584 | tf_op jit(solution)/shard_map/ppermute | solution.py:206
  73.7 2.5 %collective-permute-start.12 = (f32[8,256]{1,0:T(8,128)S(1)}, f32[8,256]{1,0:T(8,128)S(1)}, u32[]{:S(2)}, u32[]{:S(2)}) collective-permute-start(f32[8,256]{1,0:T(8,128)S(1)} %get-tuple-element.21), channel_id=1, source_target_pairs={{0,4},{2,6},{4,0},{6,2},{1,5},{3,7},{5,1},{7,3},{8,12},{10,14},{12... | collective-permute-start | bytes 24584 | tf_op jit(solution)/shard_map/ppermute | solution.py:206
  76.3 2.6 %collective-permute-start.11 = (f32[8,256]{1,0:T(8,128)S(1)}, f32[8,256]{1,0:T(8,128)S(1)}, u32[]{:S(2)}, u32[]{:S(2)}) collective-permute-start(f32[8,256]{1,0:T(8,128)S(1)} %get-tuple-element.21), channel_id=1, source_target_pairs={{0,6},{2,0},{4,2},{6,4},{1,7},{3,1},{5,3},{7,5},{8,14},{10,8},{12,... | collective-permute-start | bytes 24584 | tf_op jit(solution)/shard_map/ppermute | solution.py:206
  78.9 3.4 %all-to-all-start.1 = ((f32[8,8,1280]{2,1,0:T(8,128)}), f32[8,8,1280]{2,1,0:T(8,128)S(1)}, u32[]{:S(2)}, u32[]{:S(2)}) async-start(f32[8,8,1280]{2,1,0:T(8,128)} %get-tuple-element.20), calls=%async_computation.1 | async-start | bytes 655360 | tf_op jit(solution)/shard_map/all_to_all | solution.py:400
  82.3 0.0 collective-permute-done.13
  82.4 0.0 collective-permute-done.12
  82.4 0.0 collective-permute-done.11
  82.4 0.1 collective-permute-start.14
  82.5 1.2 collective-permute-done.14
  83.7 0.8 collective-permute-start.15
  84.5 1.2 %collective-permute-start.17 = (f32[64,256]{1,0:T(8,128)S(1)}, f32[64,256]{1,0:T(8,128)S(1)}, u32[]{:S(2)}, u32[]{:S(2)}) collective-permute-start(f32[64,256]{1,0:T(8,128)S(1)} %get-tuple-element.34), channel_id=1, source_target_pairs={{0,8},{8,16},{16,24},{24,0},{1,9},{9,17},{17,25},{25,1},{2,10},{10... | collective-permute-start | bytes 196616 | tf_op jit(solution)/shard_map/ppermute | solution.py:206
  85.7 3.7 %collective-permute-start.16 = (f32[64,256]{1,0:T(8,128)S(1)}, f32[64,256]{1,0:T(8,128)S(1)}, u32[]{:S(2)}, u32[]{:S(2)}) collective-permute-start(f32[64,256]{1,0:T(8,128)S(1)} %get-tuple-element.34), channel_id=1, source_target_pairs={{0,16},{8,24},{16,0},{24,8},{1,17},{9,25},{17,1},{25,9},{2,18},{10... | collective-permute-start | bytes 196616 | tf_op jit(solution)/shard_map/ppermute | solution.py:206
  89.4 0.0 collective-permute-done.15
  89.4 2.2 %collective-permute-done.16 = f32[64,256]{1,0:T(8,128)S(1)} collective-permute-done((f32[64,256]{1,0:T(8,128)S(1)}, f32[64,256]{1,0:T(8,128)S(1)}, u32[]{:S(2)}, u32[]{:S(2)}) %collective-permute-start.16) | collective-permute-done | bytes 65568 | tf_op jit(solution)/shard_map/ppermute | solution.py:206
  91.7 0.0 collective-permute-done.17
  91.7 1.7 %all-to-all-done.1 = f32[8,8,1280]{2,1,0:T(8,128)S(1)} async-done(((f32[8,8,1280]{2,1,0:T(8,128)}), f32[8,8,1280]{2,1,0:T(8,128)S(1)}, u32[]{:S(2)}, u32[]{:S(2)}) %all-to-all-start.1) | async-done | bytes 327712 | tf_op jit(solution)/shard_map/all_to_all | solution.py:400
  93.4 1.0 collective-permute-start.20
  94.5 1.8 %collective-permute-start.19 = (f32[64,1280]{1,0:T(8,128)S(1)}, f32[64,1280]{1,0:T(8,128)S(1)}, u32[]{:S(2)}, u32[]{:S(2)}) collective-permute-start(f32[64,1280]{1,0:T(8,128)S(1)} %bitcast.16), channel_id=1, source_target_pairs={{0,16},{8,24},{16,0},{24,8},{1,17},{9,25},{17,1},{25,9},{2,18},{10... | collective-permute-start | bytes 983048 | tf_op jit(solution)/shard_map/ppermute | solution.py:206
  96.3 2.3 %collective-permute-start.18 = (f32[64,1280]{1,0:T(8,128)S(1)}, f32[64,1280]{1,0:T(8,128)S(1)}, u32[]{:S(2)}, u32[]{:S(2)}) collective-permute-start(f32[64,1280]{1,0:T(8,128)S(1)} %bitcast.17), channel_id=1, source_target_pairs={{0,24},{8,0},{16,8},{24,16},{1,25},{9,1},{17,9},{25,17},{2,26},{10... | collective-permute-start | bytes 983048 | tf_op jit(solution)/shard_map/ppermute | solution.py:206
  98.7 13.1 %factor.1 = (f32[256,256]{1,0:T(8,128)S(1)}, bf16[1024,768]{1,0:T(8,128)(2,1)S(1)}, f32[10,1024,128]{2,1,0:T(8,128)S(1)}) custom-call(s32[1]{0:T(128)} %bitcast.1.x_ref, s32[1]{0:T(128)} %bitcast.y_ref, s32[1]{0:T(128)} %bitcast.2.core_ref, f32[256,256]{1,0:T(8,128)S(1)} %constant_dynamic-update-slice_fusion.5.pieces_ref, f32[1024,256]{1,0:T(8,128)} %copy-done, ...), custom_call_target="tpu_custom_call" | custom-call | tf_op jit(solution)/shard_map/factor/pallas_call | solution.py:330
  111.8 0.0 collective-permute-done.20.x3_ref
  111.8 0.0 collective-permute-done.19.x2_ref
  111.8 0.0 collective-permute-done.18.x1_ref
  111.8 4.0 %update.1 = (f32[10,1024,128]{2,1,0:T(8,128)}, f32[10,256,128]{2,1,0:T(8,128)}) custom-call(s32[1]{0:T(128)} %bitcast.y_ref, f32[256,256]{1,0:T(8,128)S(1)} %get-tuple-element.24.w_ref, bf16[1024,768]{1,0:T(8,128)(2,1)S(1)} %get-tuple-element.25.q_ref, f32[64,1280]{1,0:T(8,128)S(1)} %bitcast.18, f32[64,1280]{1,0:T(8,128)S(1)} %collective-permute-done.18.x1_ref, ...), custom_call_target="tpu_custom_call" | custom-call | tf_op jit(solution)/shard_map/update/pallas_call | solution.py:382
  (9 shorter events, 0.0 us)
Async XLA Ops:
  1.7 11.4 %collective-permute-start.4 = (f32[512,128]{1,0:T(8,128)S(1)}, f32[512,128]{1,0:T(8,128)S(1)}, u32[]{:S(2)}, u32[]{:S(2)}) collective-permute-start(f32[512,128]{1,0:T(8,128)S(1)} %get-tuple-element.32), channel_id=1, source_target_pairs={{0,6},{1,7},{8,14},{9,15},{16,22},{17,23},{24,30},{25,31},{32,38},... | collective-permute-start | bytes 786440 | tf_op jit(solution)/shard_map/ppermute | solution.py:64
  6.4 8.0 %collective-permute-start = (f32[512,128]{1,0:T(8,128)S(1)}, f32[512,128]{1,0:T(8,128)S(1)}, u32[]{:S(2)}, u32[]{:S(2)}) collective-permute-start(f32[512,128]{1,0:T(8,128)S(1)} %get-tuple-element.33), channel_id=1, source_target_pairs={{0,2},{1,3},{8,10},{9,11},{16,18},{17,19},{24,26},{25,27},{32,34},... | collective-permute-start | bytes 786440 | tf_op jit(solution)/shard_map/ppermute | solution.py:63
  7.7 11.1 %collective-permute-start.3 = (f32[512,128]{1,0:T(8,128)S(1)}, f32[512,128]{1,0:T(8,128)S(1)}, u32[]{:S(2)}, u32[]{:S(2)}) collective-permute-start(f32[512,128]{1,0:T(8,128)S(1)} %get-tuple-element.32), channel_id=1, source_target_pairs={{0,2},{1,3},{8,10},{9,11},{16,18},{17,19},{24,26},{25,27},{32,34},... | collective-permute-start | bytes 786440 | tf_op jit(solution)/shard_map/ppermute | solution.py:65
  9.0 9.8 %collective-permute-start.2 = (f32[512,128]{1,0:T(8,128)S(1)}, f32[512,128]{1,0:T(8,128)S(1)}, u32[]{:S(2)}, u32[]{:S(2)}) collective-permute-start(f32[512,128]{1,0:T(8,128)S(1)} %get-tuple-element.33), channel_id=1, source_target_pairs={{0,6},{1,7},{8,14},{9,15},{16,22},{17,23},{24,30},{25,31},{32,38},... | collective-permute-start | bytes 786440 | tf_op jit(solution)/shard_map/ppermute | solution.py:66
  13.1 5.8 %collective-permute-start.5 = (f32[512,128]{1,0:T(8,128)S(1)}, f32[512,128]{1,0:T(8,128)S(1)}, u32[]{:S(2)}, u32[]{:S(2)}) collective-permute-start(f32[512,128]{1,0:T(8,128)S(1)} %collective-permute-done.4), channel_id=1, source_target_pairs={{6,4},{7,5},{14,12},{15,13},{22,20},{23,21},{30,28},{31,29},{38,36... | collective-permute-start | bytes 786440 | tf_op jit(solution)/shard_map/ppermute | solution.py:68
  14.4 4.5 %collective-permute-start.1 = (f32[512,128]{1,0:T(8,128)S(1)}, f32[512,128]{1,0:T(8,128)S(1)}, u32[]{:S(2)}, u32[]{:S(2)}) collective-permute-start(f32[512,128]{1,0:T(8,128)S(1)} %collective-permute-done), channel_id=1, source_target_pairs={{2,4},{3,5},{10,12},{11,13},{18,20},{19,21},{26,28},{27,29},{34,36... | collective-permute-start | bytes 786440 | tf_op jit(solution)/shard_map/ppermute | solution.py:67
  20.0 1.6 %collective-permute-start.7 = (f32[512,128]{1,0:T(8,128)S(1)}, f32[512,128]{1,0:T(8,128)S(1)}, u32[]{:S(2)}, u32[]{:S(2)}) collective-permute-start(f32[512,128]{1,0:T(8,128)S(1)} %get-tuple-element.30.mh_ref), channel_id=1, source_target_pairs={{0,1},{1,0},{2,3},{3,2},{4,5},{5,4},{6,7},{7,6},{8,9},{9,8},{10,11... | collective-permute-start | bytes 786440 | tf_op jit(solution)/shard_map/ppermute | solution.py:56
  20.1 1.9 %collective-permute-start.6 = (f32[512,128]{1,0:T(8,128)S(1)}, f32[512,128]{1,0:T(8,128)S(1)}, u32[]{:S(2)}, u32[]{:S(2)}) collective-permute-start(f32[512,128]{1,0:T(8,128)S(1)} %get-tuple-element.31.ml_ref), channel_id=1, source_target_pairs={{0,1},{1,0},{2,3},{3,2},{4,5},{5,4},{6,7},{7,6},{8,9},{9,8},{10,11... | collective-permute-start | bytes 786440 | tf_op jit(solution)/shard_map/ppermute | solution.py:56
  27.0 43.6 %copy-start = (f32[1024,256]{1,0:T(8,128)}, f32[1024,256]{1,0:T(8,128)S(1)}, u32[]{:S(2)}) copy-start(f32[1024,256]{1,0:T(8,128)S(1)} %get-tuple-element.23.p_hbm) | copy-start | bytes 3145732
  27.0 11.3 %collective-permute-start.8 = (f32[64,1408]{1,0:T(8,128)S(1)}, f32[64,1408]{1,0:T(8,128)S(1)}, u32[]{:S(2)}, u32[]{:S(2)}) collective-permute-start(f32[64,1408]{1,0:T(8,128)S(1)} %get-tuple-element.17), channel_id=1, source_target_pairs={{0,8},{8,16},{16,24},{24,0},{1,9},{9,17},{17,25},{25,1},{2,10},{10... | collective-permute-start | bytes 1081352 | tf_op jit(solution)/shard_map/ppermute | solution.py:200
  28.6 12.8 %collective-permute-start.9 = (f32[64,1408]{1,0:T(8,128)S(1)}, f32[64,1408]{1,0:T(8,128)S(1)}, u32[]{:S(2)}, u32[]{:S(2)}) collective-permute-start(f32[64,1408]{1,0:T(8,128)S(1)} %get-tuple-element.18), channel_id=1, source_target_pairs={{0,16},{8,24},{16,0},{24,8},{1,17},{9,25},{17,1},{25,9},{2,18},{10... | collective-permute-start | bytes 1081352 | tf_op jit(solution)/shard_map/ppermute | solution.py:200
  29.6 17.8 %collective-permute-start.10 = (f32[64,1408]{1,0:T(8,128)S(1)}, f32[64,1408]{1,0:T(8,128)S(1)}, u32[]{:S(2)}, u32[]{:S(2)}) collective-permute-start(f32[64,1408]{1,0:T(8,128)S(1)} %get-tuple-element.19), channel_id=1, source_target_pairs={{0,24},{8,0},{16,8},{24,16},{1,25},{9,1},{17,9},{25,17},{2,26},{10... | collective-permute-start | bytes 1081352 | tf_op jit(solution)/shard_map/ppermute | solution.py:200
  70.6 11.8 %collective-permute-start.13 = (f32[8,256]{1,0:T(8,128)S(1)}, f32[8,256]{1,0:T(8,128)S(1)}, u32[]{:S(2)}, u32[]{:S(2)}) collective-permute-start(f32[8,256]{1,0:T(8,128)S(1)} %get-tuple-element.21), channel_id=1, source_target_pairs={{0,2},{2,4},{4,6},{6,0},{1,3},{3,5},{5,7},{7,1},{8,10},{10,12},{12... | collective-permute-start | bytes 24584 | tf_op jit(solution)/shard_map/ppermute | solution.py:206
  73.7 8.6 %collective-permute-start.12 = (f32[8,256]{1,0:T(8,128)S(1)}, f32[8,256]{1,0:T(8,128)S(1)}, u32[]{:S(2)}, u32[]{:S(2)}) collective-permute-start(f32[8,256]{1,0:T(8,128)S(1)} %get-tuple-element.21), channel_id=1, source_target_pairs={{0,4},{2,6},{4,0},{6,2},{1,5},{3,7},{5,1},{7,3},{8,12},{10,14},{12... | collective-permute-start | bytes 24584 | tf_op jit(solution)/shard_map/ppermute | solution.py:206
  76.3 6.1 %collective-permute-start.11 = (f32[8,256]{1,0:T(8,128)S(1)}, f32[8,256]{1,0:T(8,128)S(1)}, u32[]{:S(2)}, u32[]{:S(2)}) collective-permute-start(f32[8,256]{1,0:T(8,128)S(1)} %get-tuple-element.21), channel_id=1, source_target_pairs={{0,6},{2,0},{4,2},{6,4},{1,7},{3,1},{5,3},{7,5},{8,14},{10,8},{12,... | collective-permute-start | bytes 24584 | tf_op jit(solution)/shard_map/ppermute | solution.py:206
  78.9 14.5 %all-to-all-start.1 = ((f32[8,8,1280]{2,1,0:T(8,128)}), f32[8,8,1280]{2,1,0:T(8,128)S(1)}, u32[]{:S(2)}, u32[]{:S(2)}) async-start(f32[8,8,1280]{2,1,0:T(8,128)} %get-tuple-element.20), calls=%async_computation.1 | async-start | bytes 655360 | tf_op jit(solution)/shard_map/all_to_all | solution.py:400
  82.4 1.3 %collective-permute-start.14 = (f32[32,256]{1,0:T(8,128)S(1)}, f32[32,256]{1,0:T(8,128)S(1)}, u32[]{:S(2)}, u32[]{:S(2)}) collective-permute-start(f32[32,256]{1,0:T(8,128)S(1)} %pad_maximum_fusion), channel_id=1, source_target_pairs={{0,1},{1,0},{2,3},{3,2},{4,5},{5,4},{6,7},{7,6},{8,9},{9,8},{10,11... | collective-permute-start | bytes 98312 | tf_op jit(solution)/shard_map/ppermute | solution.py:56
  83.7 5.7 %collective-permute-start.15 = (f32[64,256]{1,0:T(8,128)S(1)}, f32[64,256]{1,0:T(8,128)S(1)}, u32[]{:S(2)}, u32[]{:S(2)}) collective-permute-start(f32[64,256]{1,0:T(8,128)S(1)} %get-tuple-element.34), channel_id=1, source_target_pairs={{0,24},{8,0},{16,8},{24,16},{1,25},{9,1},{17,9},{25,17},{2,26},{10... | collective-permute-start | bytes 196616 | tf_op jit(solution)/shard_map/ppermute | solution.py:206
  84.5 7.2 %collective-permute-start.17 = (f32[64,256]{1,0:T(8,128)S(1)}, f32[64,256]{1,0:T(8,128)S(1)}, u32[]{:S(2)}, u32[]{:S(2)}) collective-permute-start(f32[64,256]{1,0:T(8,128)S(1)} %get-tuple-element.34), channel_id=1, source_target_pairs={{0,8},{8,16},{16,24},{24,0},{1,9},{9,17},{17,25},{25,1},{2,10},{10... | collective-permute-start | bytes 196616 | tf_op jit(solution)/shard_map/ppermute | solution.py:206
  85.7 6.0 %collective-permute-start.16 = (f32[64,256]{1,0:T(8,128)S(1)}, f32[64,256]{1,0:T(8,128)S(1)}, u32[]{:S(2)}, u32[]{:S(2)}) collective-permute-start(f32[64,256]{1,0:T(8,128)S(1)} %get-tuple-element.34), channel_id=1, source_target_pairs={{0,16},{8,24},{16,0},{24,8},{1,17},{9,25},{17,1},{25,9},{2,18},{10... | collective-permute-start | bytes 196616 | tf_op jit(solution)/shard_map/ppermute | solution.py:206
  93.4 18.3 %collective-permute-start.20 = (f32[64,1280]{1,0:T(8,128)S(1)}, f32[64,1280]{1,0:T(8,128)S(1)}, u32[]{:S(2)}, u32[]{:S(2)}) collective-permute-start(f32[64,1280]{1,0:T(8,128)S(1)} %bitcast.15), channel_id=1, source_target_pairs={{0,8},{8,16},{16,24},{24,0},{1,9},{9,17},{17,25},{25,1},{2,10},{10... | collective-permute-start | bytes 983048 | tf_op jit(solution)/shard_map/ppermute | solution.py:206
  94.5 17.3 %collective-permute-start.19 = (f32[64,1280]{1,0:T(8,128)S(1)}, f32[64,1280]{1,0:T(8,128)S(1)}, u32[]{:S(2)}, u32[]{:S(2)}) collective-permute-start(f32[64,1280]{1,0:T(8,128)S(1)} %bitcast.16), channel_id=1, source_target_pairs={{0,16},{8,24},{16,0},{24,8},{1,17},{9,25},{17,1},{25,9},{2,18},{10... | collective-permute-start | bytes 983048 | tf_op jit(solution)/shard_map/ppermute | solution.py:206
  96.3 15.5 %collective-permute-start.18 = (f32[64,1280]{1,0:T(8,128)S(1)}, f32[64,1280]{1,0:T(8,128)S(1)}, u32[]{:S(2)}, u32[]{:S(2)}) collective-permute-start(f32[64,1280]{1,0:T(8,128)S(1)} %bitcast.17), channel_id=1, source_target_pairs={{0,24},{8,0},{16,8},{24,16},{1,25},{9,1},{17,9},{25,17},{2,26},{10... | collective-permute-start | bytes 983048 | tf_op jit(solution)/shard_map/ppermute | solution.py:206
